TPU v7x, 128 devices: a whole 4x4x4 slice. The times are simulated.
128 devices in a mesh: expert: 8 (over z, core), hidden: 16 (over x, y).
Axes of the slice: x: 4, y: 4, z: 4, core: 2. Of those that a mesh axis runs over, the one named last changes fastest.
Arguments:
- queries: bfloat16 [512, 4096], P('expert', 'hidden'), may hold values from -1000 to 1000
- new_key: bfloat16 [512, 4096], P('expert', 'hidden'), may hold values from -12 to 12
- new_value: bfloat16 [512, 4096], P('expert', 'hidden'), may hold values from -6 to 6
- key_cache: bfloat16 [512, 32, 64, 128], P('expert', 'hidden'), may hold values from -12 to 12
- value_cache: bfloat16 [512, 32, 64, 128], P('expert', 'hidden'), may hold values from -6 to 6
- cache_lengths: int32 [512], P('expert'), may hold values from 1 to 64, as said below
- residual: bfloat16 [512, 4096], P('expert'), may hold values from -1.5 to 1.5
- out_weight: bfloat16 [4096, 4096], P('hidden'), may hold values from -0.125 to 0.125
- norm_gain: bfloat16 [4096], replicated, may hold values from 0.25 to 1.75
- expert_ids: int32 [512, 2], P('expert'), may hold values from 0 to 7, all different within a row; in each aligned block of 64 rows (0 to 63, 64 to 127, ...) at most 32 rows name the same one
- gate_weight: bfloat16 [8, 4096, 11008], P('expert', None, 'hidden'), may hold values from -0.09375 to 0.09375
- up_weight: bfloat16 [8, 4096, 11008], P('expert', None, 'hidden'), may hold values from -0.09375 to 0.09375
- down_weight: bfloat16 [8, 11008, 4096], P('expert', 'hidden'), may hold values from -0.078125 to 0.078125
Outputs:
- layer_out: bfloat16 [512, 4096], P('expert', 'hidden')
Inputs may be any that keep to these rules, and one draw needn't show every extreme that they name: `expert_ids`: each row names two different experts; within each aligned block of 64 rows no expert is named by more than 32 rows, and in every draw some expert is named by exactly 32 rows of some block. Request r attends its cached positions 0 to cache_lengths[r] - 1 and its own new key; some request has exactly 64.
All inputs are finite; a program needn't handle non-finite values.
Results may differ from a plain program's by a relative error of at most 0.012.
Values may be sent and summed in bfloat16 or wider, within the bound.
No kernel may reach another device: no remote copies, remote signals or barrier semaphores. Data moves between devices by JAX's collectives and lax.ppermute only.
A program may use at most 128 MiB of HBM per device.

v0:
```python
import math

import jax
import jax.numpy as jnp
from jax import lax
from jax.sharding import PartitionSpec as P

epsilon = 1e-05


def in_blocks(array, dim, count):
    before, after = (array.shape[:dim], array.shape[dim + 1 :])
    return jnp.moveaxis(array.reshape(*before, count, -1, *after), dim, 0)


def sent_and_summed(array, axis, dim):
    count = lax.axis_size(axis)
    parts = lax.all_to_all(in_blocks(array, dim, count), axis, 0, 0, tiled=True)
    return jnp.sum(parts, axis=0)


def sent_to_all(array, axis):
    copies = jnp.broadcast_to(array, (lax.axis_size(axis), *array.shape))
    return lax.all_to_all(copies, axis, split_axis=0, concat_axis=0, tiled=True)


def taken_together(array, axis):
    everything = sent_to_all(array, axis)
    return jnp.sum(everything, axis=0)


def in_order(parts, dim):
    parts = jnp.moveaxis(parts, 0, dim)
    shape = parts.shape
    return parts.reshape(*shape[:dim], shape[dim] * shape[dim + 1], *shape[dim + 2 :])


def collect(array, axis, dim):
    parts = sent_to_all(array, axis)
    return in_order(parts, dim)


def attend(queries, new_key, new_value, key_cache, value_cache, cache_lengths):
    requests, head_count, positions, head_size = key_cache.shape
    scale = 1.0 / math.sqrt(head_size)
    query_heads = queries.reshape(requests, head_count, head_size)
    key_heads = new_key.reshape(requests, head_count, head_size)
    value_heads = new_value.reshape(requests, head_count, head_size)
    scores = (
        jnp.einsum("rhd,rhld->rhl", query_heads, key_cache, preferred_element_type=jnp.float32)
        * scale
    )
    own_score = (
        jnp.sum(query_heads.astype(jnp.float32) * key_heads.astype(jnp.float32), axis=-1) * scale
    )
    valid = jnp.arange(positions, dtype=jnp.int32)[None, None, :] < cache_lengths[:, None, None]
    masked = jnp.where(valid, scores, jnp.float32(-1e30))
    highest = jnp.maximum(jnp.max(masked, axis=-1), own_score)
    weights = jnp.where(valid, jnp.exp(masked - highest[..., None]), jnp.float32(0.0))
    own_weight = jnp.exp(own_score - highest)
    total = jnp.sum(weights, axis=-1) + own_weight
    mixed = jnp.einsum(
        "rhl,rhld->rhd",
        weights.astype(jnp.bfloat16),
        value_cache,
        preferred_element_type=jnp.float32,
    )
    own_rounded = own_weight.astype(jnp.bfloat16).astype(jnp.float32)
    mixed = mixed + own_rounded[..., None] * value_heads.astype(jnp.float32)
    return (mixed / total[..., None]).reshape(requests, head_count * head_size).astype(jnp.bfloat16)


def per_device(
    queries,
    new_key,
    new_value,
    key_cache,
    value_cache,
    cache_lengths,
    residual,
    out_weight,
    norm_gain,
    expert_ids,
    gate_weight,
    up_weight,
    down_weight,
):
    requests = queries.shape[0]
    model_width = out_weight.shape[1]
    hidden_count = lax.axis_size("hidden")
    expert_count = lax.axis_size("expert")
    columns = model_width // hidden_count
    experts_all = expert_count * gate_weight.shape[0]
    capacity = 4 * requests // experts_all
    received_rows = expert_count * capacity
    column_start = lax.axis_index("hidden") * columns
    gain = norm_gain.astype(jnp.float32)
    own_gain = lax.dynamic_slice_in_dim(gain, column_start, columns, 0)
    attended = attend(queries, new_key, new_value, key_cache, value_cache, cache_lengths)
    partial_value = jnp.dot(attended, out_weight, preferred_element_type=jnp.float32)
    attn_part = sent_and_summed(partial_value, "hidden", 1)
    own_residual = lax.dynamic_slice_in_dim(residual, column_start, columns, 1)
    stream_own = (own_residual.astype(jnp.float32) + attn_part).astype(jnp.bfloat16)
    stream_wide = stream_own.astype(jnp.float32)
    squares = taken_together(jnp.sum(stream_wide * stream_wide, axis=1), "hidden")
    factor = lax.rsqrt(squares / model_width + epsilon)
    normed_own = (stream_wide * factor[:, None] * own_gain[None, :]).astype(jnp.bfloat16)
    onehot = (
        expert_ids[:, :, None] == jnp.arange(experts_all, dtype=jnp.int32)[None, None, :]
    ).astype(jnp.int32)
    flat_hot = onehot.reshape(requests * 2, experts_all)
    before = jnp.cumsum(flat_hot, axis=0) - flat_hot
    slots = jnp.sum(before * flat_hot, axis=1).reshape(requests, 2)
    slot_hot = (slots[:, :, None] == jnp.arange(capacity, dtype=jnp.int32)[None, None, :]).astype(
        jnp.int32
    )
    placement_table = jnp.sum(onehot[:, :, :, None] * slot_hot[:, :, None, :], axis=1).astype(
        jnp.bfloat16
    )
    expert_gate = gate_weight[0]
    expert_up = up_weight[0]
    outgoing = jnp.einsum(
        "rec,rd->ecd", placement_table, normed_own, preferred_element_type=jnp.float32
    ).astype(jnp.bfloat16)
    incoming = lax.all_to_all(outgoing, "expert", split_axis=0, concat_axis=0, tiled=True)
    piece = collect(incoming, "hidden", 2)
    width_piece = piece.shape[2]
    flat_piece = piece.reshape(received_rows, width_piece)
    gate = jnp.dot(flat_piece, expert_gate, preferred_element_type=jnp.float32)
    up_part = jnp.dot(flat_piece, expert_up, preferred_element_type=jnp.float32)
    inner = (jax.nn.silu(gate) * up_part).astype(jnp.bfloat16)
    expert_down = down_weight[0]
    expert_part = sent_and_summed(
        lax.dot_general(
            expert_down, inner, (((0,), (1,)), ((), ())), preferred_element_type=jnp.float32
        ),
        "hidden",
        0,
    )
    expert_out = expert_part.astype(jnp.bfloat16).reshape(columns, expert_count, capacity)
    returned = lax.all_to_all(expert_out, "expert", split_axis=1, concat_axis=1, tiled=True)
    combined = jnp.einsum(
        "rec,dec->rd", placement_table, returned, preferred_element_type=jnp.float32
    )
    return (stream_own.astype(jnp.float32) + 0.5 * combined).astype(jnp.bfloat16)


def solution(mesh):
    return jax.shard_map(
        per_device,
        mesh=mesh,
        in_specs=(
            P("expert", "hidden"),
            P("expert", "hidden"),
            P("expert", "hidden"),
            P("expert", "hidden", None, None),
            P("expert", "hidden", None, None),
            P("expert"),
            P("expert", None),
            P("hidden", None),
            P(),
            P("expert", None),
            P("expert", None, "hidden"),
            P("expert", None, "hidden"),
            P("expert", "hidden", None),
        ),
        out_specs=P("expert", "hidden"),
        check_vma=False,
    )
```

profile of v0, /device:TPU:1, one launch (start us, length us, event | category | flops | bytes accessed | tf_op | source)
XLA Modules:
  0.0 183.1 jit_solution(13364771591217714077)
XLA Ops:
  0.0 0.9 reshape.83
  0.9 0.8 reshape.95
  1.7 0.7 iota_compare_fusion.2
  2.4 0.8 reshape.85
  3.5 0.8 reshape.86
  4.3 2.8 %fusion.43 = f32[64,2,1,64]{3,2,1,0:T(1,128)S(1)} fusion(bf16[64,2,128,1]{2,3,1,0:T(2,128)(2,1)S(1)} %reshape.95, bf16[64,2,64,128]{3,2,1,0:T(8,128)(2,1)} %param.16), kind=kOutput, calls=%fused_computation.58 | convolution fusion | flops 2097152 | bytes 2162688 | tf_op jit(solution)/shard_map/rhd,rhld->rhl/dot_general | solution.py:50
  7.2 0.2 fusion.29
  7.6 0.7 fusion.25
  8.2 0.2 fusion.28
  8.5 4.1 %copy.45 = bf16[4096,256]{1,0:T(8,128)(2,1)} copy(bf16[4096,256]{0,1:T(8,128)(2,1)} %bitcast.70) | data formatting | bytes 4194304 | tf_op jit(solution)/shard_map/dot_general | solution.py:100
  12.6 3.3 %convolution_bitcast_fusion = f32[16,64,256]{2,1,0:T(8,128)} fusion(bf16[64,256,1]{1,0,2:T(8,128)(2,1)S(1)} %reshape.91, bf16[16,256,256]{2,1,0:T(8,128)(2,1)} %bitcast.66), kind=kOutput, calls=%fused_computation.7 | convolution fusion | flops 134217728 | bytes 3178496 | tf_op jit(solution)/shard_map/dot_general | solution.py:100
  15.9 7.6 %all-to-all-start = ((f32[16,64,256]{2,1,0:T(8,128)}), f32[16,64,256]{2,1,0:T(8,128)S(1)}, u32[]{:S(2)}, u32[]{:S(2)}) async-start(f32[16,64,256]{2,1,0:T(8,128)} %convolution_bitcast_fusion), calls=%async_computation | async-start | bytes 2097152 | tf_op jit(solution)/shard_map/all_to_all | solution.py:18
  24.5 14.7 %all-to-all-done = f32[16,64,256]{2,1,0:T(8,128)S(1)} async-done(((f32[16,64,256]{2,1,0:T(8,128)}), f32[16,64,256]{2,1,0:T(8,128)S(1)}, u32[]{:S(2)}, u32[]{:S(2)}) %all-to-all-start) | async-done | bytes 1048608 | tf_op jit(solution)/shard_map/all_to_all | solution.py:18
  39.2 0.9 fusion.21
  40.1 0.6 broadcast_in_dim.39
  40.7 3.9 %all-to-all-start.1 = ((f32[16,1,64]{2,1,0:T(1,128)}), f32[16,1,64]{2,1,0:T(1,128)S(1)}, u32[]{:S(2)}, u32[]{:S(2)}) async-start(f32[16,1,64]{2,1,0:T(1,128)} %broadcast_in_dim.39), calls=%async_computation.1 | async-start | bytes 16384 | tf_op jit(solution)/shard_map/all_to_all | solution.py:24
  44.6 0.8 dynamic-slice_convert_fusion
  45.4 5.6 %all-to-all-done.1 = f32[16,1,64]{2,1,0:T(1,128)S(1)} async-done(((f32[16,1,64]{2,1,0:T(1,128)}), f32[16,1,64]{2,1,0:T(1,128)S(1)}, u32[]{:S(2)}, u32[]{:S(2)}) %all-to-all-start.1) | async-done | bytes 4128 | tf_op jit(solution)/shard_map/all_to_all | solution.py:24
  51.0 0.2 convolution_convert_fusion
  51.3 14.1 %all_to_all.31 = bf16[8,32,256]{2,1,0:T(8,128)(2,1)S(1)} all-to-all(bf16[8,32,256]{2,1,0:T(8,128)(2,1)S(1)} %convolution_convert_fusion), channel_id=1, replica_groups=mesh['expert'=8,'hidden'=16] {'expert'}, dimensions={0} | all-to-all | bytes 262144 | tf_op jit(solution)/shard_map/all_to_all | solution.py:125
  65.3 0.2 broadcast_in_dim.40
  65.6 30.1 %all_to_all.32 = bf16[16,8,32,256]{3,2,1,0:T(8,128)(2,1)S(1)} all-to-all(bf16[16,8,32,256]{3,2,1,0:T(8,128)(2,1)S(1)} %broadcast_in_dim.40), channel_id=1, replica_groups=mesh['expert'=8,'hidden'=16] {'hidden'}, dimensions={0} | all-to-all | bytes 4194304 | tf_op jit(solution)/shard_map/all_to_all | solution.py:24
  95.7 1.3 copy.39
  97.0 0.9 copy.47
  98.0 1.3 copy-done.1
  99.3 1.6 fusion.4
  101.0 13.1 %fusion = f32[256,4096]{1,0:T(8,128)} fusion(bf16[1,688,4096]{2,1,0:T(8,128)(2,1)} %param.25, bf16[256,4096]{1,0:T(8,128)(2,1)} %bitcast.72, bf16[1,4096,688]{1,2,0:T(8,128)(2,1)} %param.24, f32[256,688]{0,1:T(8,128)S(1)} %fusion.4), kind=kOutput, calls=%fused_computation | convolution fusion | flops 2886737920 | bytes 18268160 | tf_op jit(solution)/shard_map/dot_general | solution.py:134
  114.0 2.6 %copy.60 = f32[32,16,8,256]{3,2,0,1:T(8,128)S(1)} copy(f32[32,16,8,256]{3,2,1,0:T(8,128)} %bitcast.69) | data formatting | bytes 8388608 | tf_op jit(solution)/shard_map/reshape | solution.py:13
  116.7 52.5 %all_to_all.33 = f32[16,256,256]{1,2,0:T(8,128)} all-to-all(f32[16,256,256]{1,2,0:T(8,128)S(1)} %bitcast.65), channel_id=1, replica_groups=mesh['expert'=8,'hidden'=16] {'hidden'}, dimensions={0} | all-to-all | bytes 8388608 | tf_op jit(solution)/shard_map/all_to_all | solution.py:18
  169.2 2.5 %reduce_sum.79 = bf16[256,256]{0,1:T(8,128)(2,1)S(1)} reduce(f32[16,256,256]{1,2,0:T(8,128)} %all_to_all.33, f32[]{:T(128)} %constant.10.clone.1), dimensions={0}, to_apply=%region_9.10 | reduce | flops 983040 | bytes 4325380 | tf_op jit(solution)/shard_map/reduce_sum | solution.py:19
  171.6 10.7 %all_to_all.34 = bf16[256,8,32]{0,2,1:T(8,128)(2,1)S(1)} all-to-all(bf16[256,8,32]{0,2,1:T(8,128)(2,1)S(1)} %bitcast.73), channel_id=1, replica_groups=mesh['expert'=8,'hidden'=16] {'expert'}, dimensions={1} | all-to-all | bytes 262144 | tf_op jit(solution)/shard_map/all_to_all | solution.py:141
  182.3 0.8 fusion.14
  (31 shorter events, 1.6 us)
Async XLA Ops:
  0.0 7.6 %copy-start = (bf16[64,2,64,128]{3,2,1,0:T(8,128)(2,1)S(1)}, bf16[64,2,64,128]{3,2,1,0:T(8,128)(2,1)}, u32[]{:S(2)}) copy-start(bf16[64,2,64,128]{3,2,1,0:T(8,128)(2,1)} %param.17) | copy-start | bytes 6291460
  12.6 10.9 %copy-start.2 = (s32[64,2]{0,1:T(2,128)S(1)}, s32[64,2]{0,1:T(2,128)}, u32[]{:S(2)}) copy-start(s32[64,2]{0,1:T(2,128)} %param.22) | copy-start | bytes 1540
  15.9 23.2 %all-to-all-start = ((f32[16,64,256]{2,1,0:T(8,128)}), f32[16,64,256]{2,1,0:T(8,128)S(1)}, u32[]{:S(2)}, u32[]{:S(2)}) async-start(f32[16,64,256]{2,1,0:T(8,128)} %convolution_bitcast_fusion), calls=%async_computation | async-start | bytes 2097152 | tf_op jit(solution)/shard_map/all_to_all | solution.py:18
  40.7 10.3 %all-to-all-start.1 = ((f32[16,1,64]{2,1,0:T(1,128)}), f32[16,1,64]{2,1,0:T(1,128)S(1)}, u32[]{:S(2)}, u32[]{:S(2)}) async-start(f32[16,1,64]{2,1,0:T(1,128)} %broadcast_in_dim.39), calls=%async_computation.1 | async-start | bytes 16384 | tf_op jit(solution)/shard_map/all_to_all | solution.py:24
  65.6 33.7 %slice-start = ((s8[5636096]{0:T(1024)(128)(4,1)}), s8[4194304]{0:T(1024)(128)(4,1)S(1)}, s32[]{:S(2)}) async-start(s8[5636096]{0:T(1024)(128)(4,1)} %bitcast.76), calls=%async_computation.6 | async-start | bytes 8388608
  95.7 3.6 %slice-start.1 = ((s8[5636096]{0:T(1024)(128)(4,1)}), s8[1441792]{0:T(1024)(128)(4,1)S(1)}, s32[]{:S(2)}) async-start(s8[5636096]{0:T(1024)(128)(4,1)} %bitcast.76), calls=%async_computation.7 | async-start | bytes 2883584
  98.0 1.3 copy-start.1
where the time goes:
time: 184 us; the launch traced here: 183 us
  blocking collectives  107 us (58%)
  matrix products  22.5 us (12%)
  waiting for transfers between devices  20.3 us (11%)
  local copies, waits for them, and re-layouts  15.2 us (8%)
  starting transfers between devices  11.5 us (6%)
  other arithmetic  6.06 us (3%)
    all_to_all x1, blocking collectives, sent_and_summed(): parts = lax.all_to_all(in_blocks(array, dim, count), axis, 0, 0, tiled=True)  52.5 us
    all_to_all x1, blocking collectives, sent_to_all(): return lax.all_to_all(copies, axis, split_axis=0, concat_axis=0, tiled=True)  30.1 us
    all_to_all x1, waiting for transfers between devices, sent_and_summed(): parts = lax.all_to_all(in_blocks(array, dim, count), axis, 0, 0, tiled=True)  14.7 us
    all_to_all x1, blocking collectives, per_device(): lax.all_to_all(outgoing, 'expert', split_axis=0, concat_axis=0, tiled=True)  14.1 us
    dot_general x1, matrix products, per_device(): lax.dot_general(expert_down, inner, (((0,), (1,)), ((), ())), preferred_e...  13.1 us
    all_to_all x1, blocking collectives, per_device(): lax.all_to_all(expert_out, 'expert', split_axis=1, concat_axis=1, tiled=T...  10.7 us
    all_to_all x1, starting transfers between devices, sent_and_summed(): parts = lax.all_to_all(in_blocks(array, dim, count), axis, 0, 0, tiled=True)  7.58 us
    all_to_all x1, waiting for transfers between devices, sent_to_all(): return lax.all_to_all(copies, axis, split_axis=0, concat_axis=0, tiled=True)  5.6 us
  transfers between devices with their start and end apart: 2, of which 2 were waited for; matrix products, arithmetic and copies ran while one was open for 1% of the time, Pallas kernels for 0%

commit v1 on v0

v1 whole, which is shorter than its diff:
```python
import math

import jax
import jax.numpy as jnp
from jax import lax
from jax.experimental import pallas as pl
from jax.experimental.pallas import tpu as pltpu
from jax.sharding import PartitionSpec as P

epsilon = 1e-05
bf16 = jnp.bfloat16
f32 = jnp.float32
ANY = pl.BlockSpec(memory_space=pltpu.MemorySpace.HBM)
VMEM = pl.BlockSpec(memory_space=pltpu.VMEM)

EXPERTS = 8
CAP = 32
GROUP = 16


def dot(a, b, dims):
    return lax.dot_general(a, b, (dims, ((), ())), preferred_element_type=f32)


def attend_kernel(
    lens_hbm, q_hbm, nk_hbm, nv_hbm, k_hbm, v_hbm, w_hbm, ids_hbm, out_ref, table_ref,
    lens, q, nk, nv, k, v, w, ids, attended, small_sem, k_sem, v_sem, w_sem,
):
    requests, head_count, positions, size = k.shape
    groups = requests // GROUP
    parts = out_ref.shape[0]
    width = out_ref.shape[2]
    small = [
        pltpu.make_async_copy(src, dst, small_sem.at[i])
        for i, (src, dst) in enumerate(
            ((lens_hbm, lens), (q_hbm, q), (nk_hbm, nk), (nv_hbm, nv), (ids_hbm, ids))
        )
    ]
    for copy in small:
        copy.start()
    keys, values = [], []
    for g in range(groups):
        rows = pl.ds(g * GROUP, GROUP)
        keys.append(pltpu.make_async_copy(k_hbm.at[rows], k.at[rows], k_sem.at[g]))
        values.append(pltpu.make_async_copy(v_hbm.at[rows], v.at[rows], v_sem.at[g]))
        keys[g].start()
        values[g].start()
    weight = pltpu.make_async_copy(w_hbm, w, w_sem)
    weight.start()
    for copy in small:
        copy.wait()

    slots = EXPERTS * CAP
    slot = lax.broadcasted_iota(jnp.int32, (slots, requests), 0)
    expert = slot // CAP
    named = (ids[0:1, :] == expert) | (ids[1:2, :] == expert)
    earlier = (
        lax.broadcasted_iota(jnp.int32, (requests, requests), 0)
        < lax.broadcasted_iota(jnp.int32, (requests, requests), 1)
    )
    count = dot(
        jnp.where(named, 1.0, 0.0).astype(bf16),
        jnp.where(earlier, 1.0, 0.0).astype(bf16),
        ((1,), (0,)),
    )
    taken = named & (count.astype(jnp.int32) == slot - expert * CAP)
    table_ref[...] = jnp.where(taken, 1.0, 0.0).astype(bf16)

    scale = 1.0 / math.sqrt(size)
    row = lax.broadcasted_iota(jnp.int32, (requests, requests), 0)
    col = lax.broadcasted_iota(jnp.int32, (requests, requests), 1)
    length = jnp.sum(jnp.where(row == col, lens[...], 0), axis=1, keepdims=True)
    place = lax.broadcasted_iota(jnp.int32, (GROUP, GROUP * positions), 1)
    first = lax.broadcasted_iota(jnp.int32, (GROUP, GROUP * positions), 0) * positions
    for g in range(groups):
        rows = slice(g * GROUP, (g + 1) * GROUP)
        keys[g].wait()
        values[g].wait()
        valid = (place >= first) & (place < first + length[rows])
        for h in range(head_count):
            lanes = slice(h * size, (h + 1) * size)
            query = q[rows, lanes]
            own_score = (
                jnp.sum(query.astype(f32) * nk[rows, lanes].astype(f32), axis=1, keepdims=True)
                * scale
            )
            key_rows = k[rows, h].reshape(GROUP * positions, size)
            scores = dot(query, key_rows, ((1,), (1,))) * scale
            masked = jnp.where(valid, scores, f32(-1e30))
            highest = jnp.maximum(jnp.max(masked, axis=1, keepdims=True), own_score)
            weights = jnp.where(valid, jnp.exp(masked - highest), f32(0.0))
            own_weight = jnp.exp(own_score - highest)
            total = jnp.sum(weights, axis=1, keepdims=True) + own_weight
            value_rows = v[rows, h].reshape(GROUP * positions, size)
            mixed = dot(weights.astype(bf16), value_rows, ((1,), (0,)))
            own_rounded = own_weight.astype(bf16).astype(f32)
            mixed = mixed + own_rounded * nv[rows, lanes].astype(f32)
            attended[rows, lanes] = (mixed / total).astype(bf16)
    weight.wait()
    everything = attended[...]
    for n in range(parts):
        out_ref[n] = dot(everything, w[:, n * width : (n + 1) * width], ((1,), (0,))).astype(bf16)


def attend_project(queries, new_key, new_value, key_cache, value_cache, lengths, out_weight, ids, parts):
    requests, head_count, positions, size = key_cache.shape
    width = out_weight.shape[1] // parts
    groups = requests // GROUP
    return pl.pallas_call(
        attend_kernel,
        name="attend_project",
        in_specs=[ANY] * 8,
        out_specs=[VMEM, VMEM],
        out_shape=[
            jax.ShapeDtypeStruct((parts, requests, width), bf16),
            jax.ShapeDtypeStruct((EXPERTS * CAP, requests), bf16),
        ],
        scratch_shapes=[
            pltpu.VMEM((1, requests), jnp.int32),
            pltpu.VMEM(queries.shape, bf16),
            pltpu.VMEM(queries.shape, bf16),
            pltpu.VMEM(queries.shape, bf16),
            pltpu.VMEM(key_cache.shape, bf16),
            pltpu.VMEM(value_cache.shape, bf16),
            pltpu.VMEM(out_weight.shape, bf16),
            pltpu.VMEM((2, requests), jnp.int32),
            pltpu.VMEM(queries.shape, bf16),
            pltpu.SemaphoreType.DMA((5,)),
            pltpu.SemaphoreType.DMA((groups,)),
            pltpu.SemaphoreType.DMA((groups,)),
            pltpu.SemaphoreType.DMA,
        ],
        compiler_params=pltpu.CompilerParams(vmem_limit_bytes=16 << 20),
    )(lengths[None, :], queries, new_key, new_value, key_cache, value_cache, out_weight, ids.T)


def stream_kernel(parts_ref, residual_ref, table_ref, stream_ref, outgoing_ref):
    total = residual_ref[...].astype(f32)
    projected = parts_ref[0].astype(f32)
    for n in range(1, parts_ref.shape[0]):
        projected = projected + parts_ref[n].astype(f32)
    stream = (total + projected).astype(bf16)
    stream_ref[...] = stream
    outgoing_ref[...] = dot(table_ref[...], stream, ((1,), (0,))).astype(bf16)


def make_stream(parts, own_residual, table):
    requests, columns = own_residual.shape
    return pl.pallas_call(
        stream_kernel,
        name="make_stream",
        in_specs=[VMEM] * 3,
        out_specs=[VMEM, VMEM],
        out_shape=[
            jax.ShapeDtypeStruct((requests, columns), bf16),
            jax.ShapeDtypeStruct((table.shape[0], columns), bf16),
        ],
        compiler_params=pltpu.CompilerParams(vmem_limit_bytes=8 << 20),
    )(parts, own_residual, table)


def expert_kernel(
    x_ref, gain_ref, gate_hbm, up_hbm, down_hbm, out_ref,
    gate_w, up_w, down_w, normed, gate_sem, up_sem, down_sem,
):
    parts, rows, piece = x_ref.shape
    width = parts * piece
    chunks = gate_sem.shape[0]
    span = width // chunks
    gates, ups, downs = [], [], []
    for c in range(chunks):
        at = (slice(None), pl.ds(c * span, span))
        gates.append(pltpu.make_async_copy(gate_hbm.at[at], gate_w.at[at], gate_sem.at[c]))
        ups.append(pltpu.make_async_copy(up_hbm.at[at], up_w.at[at], up_sem.at[c]))
        gates[c].start()
        ups[c].start()
    for c in range(chunks):
        at = (slice(None), pl.ds(c * span, span))
        downs.append(pltpu.make_async_copy(down_hbm.at[at], down_w.at[at], down_sem.at[c]))
        downs[c].start()
    squares = jnp.zeros((rows, piece), f32)
    for n in range(parts):
        wide = x_ref[n].astype(f32)
        squares = squares + wide * wide
    mean = jnp.sum(squares, axis=1, keepdims=True) * (1.0 / width)
    factor = lax.rsqrt(mean + epsilon)
    for n in range(parts):
        lanes = slice(n * piece, (n + 1) * piece)
        gain = gain_ref[:, lanes].astype(f32)
        normed[:, lanes] = (x_ref[n].astype(f32) * factor * gain).astype(bf16)
    gate = up = None
    for c in range(chunks):
        lanes = slice(c * span, (c + 1) * span)
        gates[c].wait()
        part = dot(gate_w[:, lanes], normed[:, lanes], ((1,), (1,)))
        gate = part if gate is None else gate + part
        ups[c].wait()
        part = dot(up_w[:, lanes], normed[:, lanes], ((1,), (1,)))
        up = part if up is None else up + part
    inner = (gate / (1.0 + jnp.exp(-gate)) * up).astype(bf16)
    per = parts // chunks
    for c in range(chunks):
        downs[c].wait()
        for n in range(c * per, (c + 1) * per):
            part = dot(inner, down_w[:, n * piece : (n + 1) * piece], ((0,), (0,)))
            out_ref[n] = part.astype(bf16)


def run_expert(x, gain, gate_weight, up_weight, down_weight):
    parts, rows, piece = x.shape
    hidden, width = down_weight.shape
    chunks = 4
    return pl.pallas_call(
        expert_kernel,
        name="run_expert",
        in_specs=[VMEM, VMEM, ANY, ANY, ANY],
        out_specs=VMEM,
        out_shape=jax.ShapeDtypeStruct(x.shape, bf16),
        scratch_shapes=[
            pltpu.VMEM((hidden, width), bf16),
            pltpu.VMEM((hidden, width), bf16),
            pltpu.VMEM((hidden, width), bf16),
            pltpu.VMEM((rows, width), bf16),
            pltpu.SemaphoreType.DMA((chunks,)),
            pltpu.SemaphoreType.DMA((chunks,)),
            pltpu.SemaphoreType.DMA((chunks,)),
        ],
        compiler_params=pltpu.CompilerParams(vmem_limit_bytes=40 << 20),
    )(x, gain[None, :], gate_weight.T, up_weight.T, down_weight)


def sum_kernel(parts_ref, out_ref):
    total = parts_ref[0].astype(f32)
    for n in range(1, parts_ref.shape[0]):
        total = total + parts_ref[n].astype(f32)
    out_ref[...] = total.astype(bf16)


def sum_parts(parts):
    return pl.pallas_call(
        sum_kernel,
        name="sum_parts",
        in_specs=[VMEM],
        out_specs=VMEM,
        out_shape=jax.ShapeDtypeStruct(parts.shape[1:], bf16),
        compiler_params=pltpu.CompilerParams(vmem_limit_bytes=8 << 20),
    )(parts)


def combine_kernel(stream_ref, returned_ref, table_ref, out_ref):
    mixed = dot(table_ref[...], returned_ref[...], ((0,), (0,)))
    out_ref[...] = (stream_ref[...].astype(f32) + 0.5 * mixed).astype(bf16)


def combine(stream, returned, table):
    return pl.pallas_call(
        combine_kernel,
        name="combine",
        in_specs=[VMEM] * 3,
        out_specs=VMEM,
        out_shape=jax.ShapeDtypeStruct(stream.shape, bf16),
        compiler_params=pltpu.CompilerParams(vmem_limit_bytes=8 << 20),
    )(stream, returned, table)


def swapped(parts, axis):
    return lax.all_to_all(parts, axis, 0, 0, tiled=True)


def per_device(
    queries, new_key, new_value, key_cache, value_cache, cache_lengths, residual,
    out_weight, norm_gain, expert_ids, gate_weight, up_weight, down_weight,
):
    requests = queries.shape[0]
    hidden_count = lax.axis_size("hidden")
    columns = out_weight.shape[1] // hidden_count
    partial_value, table = attend_project(
        queries, new_key, new_value, key_cache, value_cache, cache_lengths,
        out_weight, expert_ids, hidden_count,
    )
    own_residual = lax.dynamic_slice_in_dim(
        residual, lax.axis_index("hidden") * columns, columns, 1
    )
    stream, outgoing = make_stream(swapped(partial_value, "hidden"), own_residual, table)
    incoming = swapped(outgoing.reshape(EXPERTS, CAP, columns), "expert")
    incoming = incoming.reshape(EXPERTS * CAP, columns)
    copies = jnp.broadcast_to(incoming, (hidden_count, *incoming.shape))
    gathered = swapped(copies, "hidden")
    expert_part = run_expert(gathered, norm_gain, gate_weight[0], up_weight[0], down_weight[0])
    expert_out = sum_parts(swapped(expert_part, "hidden"))
    returned = swapped(expert_out.reshape(EXPERTS, CAP, columns), "expert")
    return combine(stream, returned.reshape(EXPERTS * CAP, columns), table)


def solution(mesh):
    return jax.shard_map(
        per_device,
        mesh=mesh,
        in_specs=(
            P("expert", "hidden"),
            P("expert", "hidden"),
            P("expert", "hidden"),
            P("expert", "hidden", None, None),
            P("expert", "hidden", None, None),
            P("expert"),
            P("expert", None),
            P("hidden", None),
            P(),
            P("expert", None),
            P("expert", None, "hidden"),
            P("expert", None, "hidden"),
            P("expert", "hidden", None),
        ),
        out_specs=P("expert", "hidden"),
        check_vma=False,
    )
```

time: 184 us -> 135 us (0.73)
  blocking collectives: 107 us -> 54 us
  matrix products: 22.5 us -> 0 us
  waiting for transfers between devices: 20.3 us -> 38.9 us
  Pallas kernels: 0 us -> 17.6 us
  other arithmetic: 6.06 us -> 0 us
  local copies, waits for them, and re-layouts: 15.2 us -> 12.6 us
    all_to_all x4 -> x3, blocking collectives: 107 us -> 54 us  [swapped(): return lax.all_to_all(parts, axis, 0, 0, tiled=True)]
    dot_general x7 -> x0, matrix products: 22.5 us -> none  [the longest x1 13.1 us: per_device(): lax.dot_general(expert_down, inner, (((0,), (1,)), ((), ())), preferred_e...]
    all_to_all x2, waiting for transfers between devices: 20.3 us -> 38.9 us  [swapped(): return lax.all_to_all(parts, axis, 0, 0, tiled=True)]
    pallas_call x0 -> x5, Pallas kernels: none -> 17.6 us  [the longest x1 11.3 us: run_expert(): pl.pallas_call(expert_kernel, name='run_expert', in_specs=[VMEM, VMEM, AN...]
    unnamed x12 -> x22, local copies, waits for them, and re-layouts: 2.37 us -> 11 us
    reshape x3 -> x0, local copies, waits for them, and re-layouts: 4.33 us -> none  [the longest x1 2.63 us: in_blocks(): return jnp.moveaxis(array.reshape(*before, count, -1, *after), dim, 0)]
    dot_general x1 -> x0, local copies, waits for them, and re-layouts: 4.11 us -> none  [per_device(): jnp.dot(attended, out_weight, preferred_element_type=jnp.float32)]
    reduce_sum x8 -> x0, other arithmetic: 3.94 us -> none  [the longest x2 2.52 us: sent_and_summed(): return jnp.sum(parts, axis=0)]
  transfers between devices with their start and end apart: 2 -> 2, of which waited for: 2 -> 2; matrix products, arithmetic and copies ran while one was open for 1% -> 0% of each run, Pallas kernels for 0% -> 0%
where the time goes in v1:
time: 135 us
  blocking collectives  54 us (40%)
  waiting for transfers between devices  38.9 us (29%)
  Pallas kernels  17.6 us (13%)
  local copies, waits for them, and re-layouts  12.6 us (9%)
  starting transfers between devices  11.4 us (8%)
    all_to_all x3, blocking collectives, swapped(): return lax.all_to_all(parts, axis, 0, 0, tiled=True)  54 us
    all_to_all x2, waiting for transfers between devices, swapped(): return lax.all_to_all(parts, axis, 0, 0, tiled=True)  38.9 us
    all_to_all x2, starting transfers between devices, swapped(): return lax.all_to_all(parts, axis, 0, 0, tiled=True)  11.4 us
    pallas_call x1, Pallas kernels, run_expert(): pl.pallas_call(expert_kernel, name='run_expert', in_specs=[VMEM, VMEM, AN...  11.3 us
    unnamed x22, local copies, waits for them, and re-layouts  11 us
    pallas_call x1, Pallas kernels, attend_project(): pl.pallas_call(attend_kernel, name='attend_project', in_specs=[ANY] * 8,...  4.95 us
  transfers between devices with their start and end apart: 2, of which 2 were waited for; matrix products, arithmetic and copies ran while one was open for 0% of the time, Pallas kernels for 0%

profile of v1, /device:TPU:1, one launch (start us, length us, event | category | flops | bytes accessed | tf_op | source)
XLA Modules:
  0.0 134.6 jit_solution(12724638765734072704)
XLA Ops:
  0.0 0.0 copy-start
  0.0 0.0 copy-start.2
  0.0 1.6 %copy-done.2 = bf16[64,2,64,128]{3,2,1,0:T(8,128)(2,1)S(1)} copy-done((bf16[64,2,64,128]{3,2,1,0:T(8,128)(2,1)S(1)}, bf16[64,2,64,128]{3,2,1,0:T(8,128)(2,1)}, u32[]{:S(2)}) %copy-start.2) | copy-done | bytes 2097176
  1.7 0.0 copy-start.3
  1.7 1.6 %copy-done.3 = bf16[64,2,64,128]{3,2,1,0:T(8,128)(2,1)S(1)} copy-done((bf16[64,2,64,128]{3,2,1,0:T(8,128)(2,1)S(1)}, bf16[64,2,64,128]{3,2,1,0:T(8,128)(2,1)}, u32[]{:S(2)}) %copy-start.3) | copy-done | bytes 2097176
  3.2 0.0 copy-start.4
  3.2 1.6 %copy-done.4 = bf16[256,4096]{1,0:T(8,128)(2,1)S(1)} copy-done((bf16[256,4096]{1,0:T(8,128)(2,1)S(1)}, bf16[256,4096]{1,0:T(8,128)(2,1)}, u32[]{:S(2)}) %copy-start.4) | copy-done | bytes 2097176
  4.8 0.0 copy-start.5
  4.8 0.8 copy-done.5
  5.6 0.0 copy-start.6
  5.6 0.8 copy-done.6
  6.4 0.0 copy-start.7
  6.4 0.8 copy-done.7
  7.1 0.0 copy-start.8
  7.1 0.7 copy-done.8
  7.8 0.7 copy-done.9
  8.4 5.0 %attend_project.1 = (bf16[16,64,256]{2,1,0:T(8,128)(2,1)}, bf16[256,64]{1,0:T(8,128)(2,1)S(1)}) custom-call(s32[1,64]{1,0:T(1,128)S(1)} %bitcast.18, bf16[64,256]{1,0:T(8,128)(2,1)S(1)} %copy-done.5, bf16[64,256]{1,0:T(8,128)(2,1)S(1)} %copy-done.6, bf16[64,256]{1,0:T(8,128)(2,1)S(1)} %copy-done.7, bf16[64,2,64,128]{3,2,1,0:T(8,128)(2,1)S(1)} %copy-done.2, ...), custom_call_target="tpu_custom_call" | custom-call | tf_op jit(solution)/shard_map/attend_project/pallas_call | solution.py:109
  13.4 7.6 %all-to-all-start = ((bf16[16,64,256]{2,1,0:T(8,128)(2,1)}), bf16[16,64,256]{2,1,0:T(8,128)(2,1)S(1)}, u32[]{:S(2)}, u32[]{:S(2)}) async-start(bf16[16,64,256]{2,1,0:T(8,128)(2,1)} %get-tuple-element.9), calls=%async_computation | async-start | bytes 1048576 | tf_op jit(solution)/shard_map/all_to_all | solution.py:267
  21.0 0.0 copy-done
  21.0 10.3 %all-to-all-done.parts_ref = bf16[16,64,256]{2,1,0:T(8,128)(2,1)S(1)} async-done(((bf16[16,64,256]{2,1,0:T(8,128)(2,1)}), bf16[16,64,256]{2,1,0:T(8,128)(2,1)S(1)}, u32[]{:S(2)}, u32[]{:S(2)}) %all-to-all-start) | async-done | bytes 524320 | tf_op jit(solution)/shard_map/all_to_all | solution.py:267
  31.4 0.2 make_stream.1
  31.6 12.4 %all_to_all.25 = bf16[8,32,256]{2,1,0:T(8,128)(2,1)S(1)} all-to-all(bf16[8,32,256]{2,1,0:T(8,128)(2,1)S(1)} %bitcast.16), channel_id=1, replica_groups=mesh['expert'=8,'hidden'=16] {'expert'}, dimensions={0} | all-to-all | bytes 262144 | tf_op jit(solution)/shard_map/all_to_all | solution.py:267
  44.0 1.5 %broadcast_in_dim.10 = bf16[16,256,256]{2,1,0:T(8,128)(2,1)} broadcast(bf16[256,256]{1,0:T(8,128)(2,1)S(1)} %bitcast.21), dimensions={1,2} | broadcast | bytes 2228224 | tf_op jit(solution)/shard_map/broadcast_in_dim | solution.py:287
  45.6 3.8 %all-to-all-start.2 = ((bf16[16,256,256]{2,1,0:T(8,128)(2,1)}), bf16[16,256,256]{2,1,0:T(8,128)(2,1)S(1)}, u32[]{:S(2)}, u32[]{:S(2)}) async-start(bf16[16,256,256]{2,1,0:T(8,128)(2,1)} %broadcast_in_dim.10), calls=%async_computation.2 | async-start | bytes 4194304 | tf_op jit(solution)/shard_map/all_to_all | solution.py:267
  49.4 0.0 copy-done.10
  49.5 28.6 %all-to-all-done.2.x_ref = bf16[16,256,256]{2,1,0:T(8,128)(2,1)S(1)} async-done(((bf16[16,256,256]{2,1,0:T(8,128)(2,1)}), bf16[16,256,256]{2,1,0:T(8,128)(2,1)S(1)}, u32[]{:S(2)}, u32[]{:S(2)}) %all-to-all-start.2) | async-done | bytes 2097184 | tf_op jit(solution)/shard_map/all_to_all | solution.py:267
  78.0 2.6 %copy-done.1 = bf16[1,4096,688]{1,2,0:T(8,128)(2,1)S(1)} copy-done((bf16[1,4096,688]{1,2,0:T(8,128)(2,1)S(1)}, bf16[1,4096,688]{1,2,0:T(8,128)(2,1)}, u32[]{:S(2)}) %copy-start.1) | copy-done | bytes 5636120
  80.6 11.3 %run_expert.1 = bf16[16,256,256]{2,1,0:T(8,128)(2,1)S(1)} custom-call(bf16[16,256,256]{2,1,0:T(8,128)(2,1)S(1)} %all-to-all-done.2.x_ref, bf16[1,4096]{1,0:T(2,128)(2,1)S(1)} %broadcast_in_dim.11.gain_ref, bf16[688,4096]{1,0:T(8,128)(2,1)S(1)} %bitcast.13, bf16[688,4096]{1,0:T(8,128)(2,1)} %bitcast.19, bf16[688,4096]{1,0:T(8,128)(2,1)} %bitcast.20), custom_call_target="tpu_custom_call" | custom-call | tf_op jit(solution)/shard_map/run_expert/pallas_call | solution.py:213
  91.9 27.4 %all_to_all.26.parts_ref = bf16[16,256,256]{2,1,0:T(8,128)(2,1)S(1)} all-to-all(bf16[16,256,256]{2,1,0:T(8,128)(2,1)S(1)} %run_expert.1), channel_id=1, replica_groups=mesh['expert'=8,'hidden'=16] {'hidden'}, dimensions={0} | all-to-all | bytes 4194304 | tf_op jit(solution)/shard_map/all_to_all | solution.py:267
  119.4 0.3 sum_parts.1
  119.6 14.2 %all_to_all.27 = bf16[8,32,256]{2,1,0:T(8,128)(2,1)S(1)} all-to-all(bf16[8,32,256]{2,1,0:T(8,128)(2,1)S(1)} %bitcast.14), channel_id=1, replica_groups=mesh['expert'=8,'hidden'=16] {'expert'}, dimensions={0} | all-to-all | bytes 262144 | tf_op jit(solution)/shard_map/all_to_all | solution.py:267
  133.8 0.8 combine.1
  (5 shorter events, 0.0 us)
Async XLA Ops:
  0.0 21.0 %copy-start = (bf16[64,4096]{1,0:T(8,128)(2,1)S(1)}, bf16[64,4096]{1,0:T(8,128)(2,1)}, u32[]{:S(2)}) copy-start(bf16[64,4096]{1,0:T(8,128)(2,1)} %param.19) | copy-start | bytes 1572868
  0.0 1.6 %copy-start.2 = (bf16[64,2,64,128]{3,2,1,0:T(8,128)(2,1)S(1)}, bf16[64,2,64,128]{3,2,1,0:T(8,128)(2,1)}, u32[]{:S(2)}) copy-start(bf16[64,2,64,128]{3,2,1,0:T(8,128)(2,1)} %k_hbm.1) | copy-start | bytes 6291460
  1.7 1.6 %copy-start.3 = (bf16[64,2,64,128]{3,2,1,0:T(8,128)(2,1)S(1)}, bf16[64,2,64,128]{3,2,1,0:T(8,128)(2,1)}, u32[]{:S(2)}) copy-start(bf16[64,2,64,128]{3,2,1,0:T(8,128)(2,1)} %v_hbm.1) | copy-start | bytes 6291460
  3.2 1.6 %copy-start.4 = (bf16[256,4096]{1,0:T(8,128)(2,1)S(1)}, bf16[256,4096]{1,0:T(8,128)(2,1)}, u32[]{:S(2)}) copy-start(bf16[256,4096]{1,0:T(8,128)(2,1)} %w_hbm.1) | copy-start | bytes 6291460
  4.8 0.8 copy-start.5
  5.6 0.8 copy-start.6
  6.4 0.8 copy-start.7
  7.1 0.7 copy-start.8
  7.8 0.7 copy-start.9
  13.4 18.0 %all-to-all-start = ((bf16[16,64,256]{2,1,0:T(8,128)(2,1)}), bf16[16,64,256]{2,1,0:T(8,128)(2,1)S(1)}, u32[]{:S(2)}, u32[]{:S(2)}) async-start(bf16[16,64,256]{2,1,0:T(8,128)(2,1)} %get-tuple-element.9), calls=%async_computation | async-start | bytes 1048576 | tf_op jit(solution)/shard_map/all_to_all | solution.py:267
  45.6 3.9 %copy-start.10 = (bf16[4096]{0:T(1024)(128)(2,1)S(1)}, bf16[4096]{0:T(1024)(128)(2,1)}, u32[]{:S(2)}) copy-start(bf16[4096]{0:T(1024)(128)(2,1)} %param.21) | copy-start | bytes 24580
  45.6 32.4 %all-to-all-start.2 = ((bf16[16,256,256]{2,1,0:T(8,128)(2,1)}), bf16[16,256,256]{2,1,0:T(8,128)(2,1)S(1)}, u32[]{:S(2)}, u32[]{:S(2)}) async-start(bf16[16,256,256]{2,1,0:T(8,128)(2,1)} %broadcast_in_dim.10), calls=%async_computation.2 | async-start | bytes 4194304 | tf_op jit(solution)/shard_map/all_to_all | solution.py:267
  78.0 2.6 %copy-start.1 = (bf16[1,4096,688]{1,2,0:T(8,128)(2,1)S(1)}, bf16[1,4096,688]{1,2,0:T(8,128)(2,1)}, u32[]{:S(2)}) copy-start(bf16[1,4096,688]{1,2,0:T(8,128)(2,1)} %param.23) | copy-start | bytes 16908292

commit v2 on v1

--- a/solution.py
+++ b/solution.py
@@ -1,3 +1,4 @@
+import functools
 import math
 
 import jax
@@ -10,12 +11,14 @@
 epsilon = 1e-05
 bf16 = jnp.bfloat16
 f32 = jnp.float32
-ANY = pl.BlockSpec(memory_space=pltpu.MemorySpace.HBM)
+ANY = pl.BlockSpec(memory_space=pl.ANY)
 VMEM = pl.BlockSpec(memory_space=pltpu.VMEM)
 
 EXPERTS = 8
 CAP = 32
 GROUP = 16
+STATS = 16
+STEPS = (0, 1, 3, 2)
 
 
 def dot(a, b, dims):
@@ -103,7 +106,7 @@
 
 
 def attend_project(queries, new_key, new_value, key_cache, value_cache, lengths, out_weight, ids, parts):
-    requests, head_count, positions, size = key_cache.shape
+    requests, _, _, _ = key_cache.shape
     width = out_weight.shape[1] // parts
     groups = requests // GROUP
     return pl.pallas_call(
@@ -130,18 +133,26 @@
             pltpu.SemaphoreType.DMA((groups,)),
             pltpu.SemaphoreType.DMA,
         ],
-        compiler_params=pltpu.CompilerParams(vmem_limit_bytes=16 << 20),
+        compiler_params=pltpu.CompilerParams(vmem_limit_bytes=65_000_000),
     )(lengths[None, :], queries, new_key, new_value, key_cache, value_cache, out_weight, ids.T)
 
 
-def stream_kernel(parts_ref, residual_ref, table_ref, stream_ref, outgoing_ref):
+def own_rows(ref, k, other):
+    place = lax.axis_index("expert")
+    expert = (place // 2 + k) % 4 * 2 + (place + other) % 2
+    return ref[pl.ds(pl.multiple_of(expert * CAP, CAP), CAP), :]
+
+
+def stream_kernel(parts_ref, residual_ref, table_ref, stream_ref, *block_refs):
     total = residual_ref[...].astype(f32)
     projected = parts_ref[0].astype(f32)
     for n in range(1, parts_ref.shape[0]):
         projected = projected + parts_ref[n].astype(f32)
     stream = (total + projected).astype(bf16)
     stream_ref[...] = stream
-    outgoing_ref[...] = dot(table_ref[...], stream, ((1,), (0,))).astype(bf16)
+    for k, block_ref in enumerate(block_refs):
+        rows = jnp.concatenate([own_rows(table_ref, k, 0), own_rows(table_ref, k, 1)], axis=0)
+        block_ref[...] = dot(rows, stream, ((1,), (0,))).astype(bf16)
 
 
 def make_stream(parts, own_residual, table):
@@ -150,101 +161,238 @@
         stream_kernel,
         name="make_stream",
         in_specs=[VMEM] * 3,
+        out_specs=[VMEM] * 5,
+        out_shape=[jax.ShapeDtypeStruct((requests, columns), bf16)]
+        + [jax.ShapeDtypeStruct((2 * CAP, columns), bf16)] * 4,
+        compiler_params=pltpu.CompilerParams(vmem_limit_bytes=8 << 20),
+    )(parts, own_residual, table)
+
+
+def load_kernel(gate_hbm, up_hbm, after, gate_w, up_w, done_ref, sems):
+    rows = gate_w.shape[0]
+    count = sems.shape[1]
+    step = rows // count // 16 * 16
+    copies = []
+    for i, (source, target) in enumerate(((gate_hbm, gate_w), (up_hbm, up_w))):
+        for c in range(count):
+            at = pl.ds(c * step, step if c < count - 1 else rows - step * (count - 1))
+            copies.append(pltpu.make_async_copy(source.at[at], target.at[at], sems.at[i, c]))
+    for copy in copies:
+        copy.start()
+    done_ref[...] = jnp.zeros(done_ref.shape, f32)
+    for copy in copies:
+        copy.wait()
+
+
+def load_weights(gate_weight, up_weight, after):
+    width, hidden = gate_weight.shape
+    return pl.pallas_call(
+        load_kernel,
+        name="load_weights",
+        in_specs=[ANY] * 3,
+        out_specs=[VMEM] * 3,
+        out_shape=[pltpu.VMEM((hidden, width), bf16)] * 2
+        + [jax.ShapeDtypeStruct((8, 128), f32)],
+        scratch_shapes=[pltpu.SemaphoreType.DMA((2, 2))],
+        cost_estimate=pl.CostEstimate(
+            flops=0, bytes_accessed=8 * hidden * width, transcendentals=0
+        ),
+        compiler_params=pltpu.CompilerParams(vmem_limit_bytes=49 << 20),
+    )(gate_weight.T, up_weight.T, after)
+
+
+def prepare_kernel(*refs):
+    kept, passed = refs[:4], refs[4:8]
+    gain_ref, _, first_ref, second_ref = refs[8:]
+    piece = kept[0].shape[1]
+    half = piece // 2
+    x = jnp.concatenate(
+        [part for k in range(4) for part in (kept[k][:CAP], passed[k][...])], axis=0
+    )
+    rows = x.shape[0]
+    wide = x.astype(f32)
+    start = pl.multiple_of(lax.axis_index("hidden") * piece, piece)
+    gain = gain_ref[:, pl.ds(start, piece)].astype(f32)
+    turned = wide.T
+    squares = jnp.sum(turned * turned, axis=0, keepdims=True)
+    high = squares.astype(bf16).astype(f32)
+    low = squares - high
+    line = lax.broadcasted_iota(jnp.int32, (STATS, rows), 0)
+    stats = jnp.where(line == 0, high, jnp.where(line == 1, low, 0.0))
+    scaled = (wide * gain).T
+    first_ref[0] = scaled[:half].astype(bf16)
+    second_ref[0, :half] = scaled[half:].astype(bf16)
+    second_ref[0, half:] = stats.astype(bf16)
+
+
+def prepare(kept, passed, gain, loaded):
+    piece = kept[0].shape[1]
+    half = piece // 2
+    rows = EXPERTS * CAP
+    return pl.pallas_call(
+        prepare_kernel,
+        name="prepare",
+        in_specs=[VMEM] * 10,
         out_specs=[VMEM, VMEM],
         out_shape=[
-            jax.ShapeDtypeStruct((requests, columns), bf16),
-            jax.ShapeDtypeStruct((table.shape[0], columns), bf16),
+            jax.ShapeDtypeStruct((1, half, rows), bf16),
+            jax.ShapeDtypeStruct((1, half + STATS, rows), bf16),
         ],
         compiler_params=pltpu.CompilerParams(vmem_limit_bytes=8 << 20),
-    )(parts, own_residual, table)
-
-
-def expert_kernel(
-    x_ref, gain_ref, gate_hbm, up_hbm, down_hbm, out_ref,
-    gate_w, up_w, down_w, normed, gate_sem, up_sem, down_sem,
+    )(*kept, *passed, gain[None, :], loaded)
+
+
+def partial_products(k, first_ref, second_ref, gate_w, up_w):
+    half, rows = first_ref.shape[1:]
+    hidden = lax.axis_index("hidden")
+    x_at, y_at = hidden // 4, hidden % 4
+
+    def taken(weight, offset, owners):
+        return jnp.concatenate(
+            [
+                weight[:, pl.ds(pl.multiple_of(owner * 2 * half + offset, half), half)]
+                for owner in owners
+            ],
+            axis=1,
+        )
+
+    def owner(kx, ky):
+        return (x_at + 4 - kx) % 4 * 4 + (y_at + 4 - ky) % 4
+
+    owners = [owner(other, k) for other in STEPS]
+    x = first_ref[...].reshape(4 * half, rows)
+    gate = dot(taken(gate_w, 0, owners), x, ((1,), (0,)))
+    up = dot(taken(up_w, 0, owners), x, ((1,), (0,)))
+    owners = [owner(k, other) for other in STEPS]
+    x = second_ref[:, :half, :].reshape(4 * half, rows)
+    gate = gate + dot(taken(gate_w, half, owners), x, ((1,), (0,)))
+    up = up + dot(taken(up_w, half, owners), x, ((1,), (0,)))
+    stats = second_ref[0, half:].astype(f32)
+    for j in range(1, 4):
+        stats = stats + second_ref[j, half:].astype(f32)
+    return gate, up, jnp.sum(stats, axis=0, keepdims=True)
+
+
+def begin_kernel(first_ref, second_ref, gate_w, up_w, gate_ref, up_ref, squares_ref):
+    gate_ref[...], up_ref[...], squares_ref[...] = partial_products(
+        0, first_ref, second_ref, gate_w, up_w
+    )
+
+
+def go_on_kernel(
+    k, first_ref, second_ref, gate_w, up_w, gate_in, up_in, squares_in, gate_ref, up_ref, squares_ref
 ):
-    parts, rows, piece = x_ref.shape
-    width = parts * piece
-    chunks = gate_sem.shape[0]
-    span = width // chunks
-    gates, ups, downs = [], [], []
-    for c in range(chunks):
-        at = (slice(None), pl.ds(c * span, span))
-        gates.append(pltpu.make_async_copy(gate_hbm.at[at], gate_w.at[at], gate_sem.at[c]))
-        ups.append(pltpu.make_async_copy(up_hbm.at[at], up_w.at[at], up_sem.at[c]))
-        gates[c].start()
-        ups[c].start()
-    for c in range(chunks):
-        at = (slice(None), pl.ds(c * span, span))
-        downs.append(pltpu.make_async_copy(down_hbm.at[at], down_w.at[at], down_sem.at[c]))
-        downs[c].start()
-    squares = jnp.zeros((rows, piece), f32)
-    for n in range(parts):
-        wide = x_ref[n].astype(f32)
-        squares = squares + wide * wide
-    mean = jnp.sum(squares, axis=1, keepdims=True) * (1.0 / width)
-    factor = lax.rsqrt(mean + epsilon)
-    for n in range(parts):
-        lanes = slice(n * piece, (n + 1) * piece)
-        gain = gain_ref[:, lanes].astype(f32)
-        normed[:, lanes] = (x_ref[n].astype(f32) * factor * gain).astype(bf16)
-    gate = up = None
-    for c in range(chunks):
-        lanes = slice(c * span, (c + 1) * span)
-        gates[c].wait()
-        part = dot(gate_w[:, lanes], normed[:, lanes], ((1,), (1,)))
-        gate = part if gate is None else gate + part
-        ups[c].wait()
-        part = dot(up_w[:, lanes], normed[:, lanes], ((1,), (1,)))
-        up = part if up is None else up + part
+    gate, up, squares = partial_products(k, first_ref, second_ref, gate_w, up_w)
+    gate_ref[...] = gate_in[...] + gate
+    up_ref[...] = up_in[...] + up
+    squares_ref[...] = squares_in[...] + squares
+
+
+def finish_kernel(
+    k, first_ref, second_ref, gate_w, up_w, gate_in, up_in, squares_in, down_w, *out_refs
+):
+    first_outs, second_outs = out_refs[:4], out_refs[4:]
+    _, rows, piece = first_outs[0].shape
+    gate, up, squares = partial_products(k, first_ref, second_ref, gate_w, up_w)
+    squares = squares + squares_in[...]
+    factor = lax.rsqrt(squares * (1.0 / (16 * piece)) + epsilon)
+    gate = (gate + gate_in[...]) * factor
+    up = (up + up_in[...]) * factor
     inner = (gate / (1.0 + jnp.exp(-gate)) * up).astype(bf16)
-    per = parts // chunks
-    for c in range(chunks):
-        downs[c].wait()
-        for n in range(c * per, (c + 1) * per):
-            part = dot(inner, down_w[:, n * piece : (n + 1) * piece], ((0,), (0,)))
-            out_ref[n] = part.astype(bf16)
-
-
-def run_expert(x, gain, gate_weight, up_weight, down_weight):
-    parts, rows, piece = x.shape
-    hidden, width = down_weight.shape
-    chunks = 4
-    return pl.pallas_call(
-        expert_kernel,
-        name="run_expert",
-        in_specs=[VMEM, VMEM, ANY, ANY, ANY],
+    hidden = lax.axis_index("hidden")
+    for kx in range(4):
+        for ky in range(4):
+            owner = (hidden // 4 + kx) % 4 * 4 + (hidden % 4 + ky) % 4
+            weight = down_w[:, pl.ds(pl.multiple_of(owner * piece, piece), piece)]
+            part = dot(inner, weight, ((0,), (0,))).astype(bf16)
+            first_outs[kx][ky] = part[:rows]
+            second_outs[ky][kx] = part[rows:]
+
+
+def run_expert(firsts, seconds, gate_w, up_w, down_w):
+    _, half, rows = firsts[0].shape
+    hidden, _ = down_w.shape
+    cost = pl.CostEstimate(
+        flops=16 * hidden * 4 * half * rows, bytes_accessed=1 << 22, transcendentals=0
+    )
+    params = pltpu.CompilerParams(vmem_limit_bytes=16 << 20)
+    sums = [jax.ShapeDtypeStruct((hidden, rows), f32)] * 2 + [jax.ShapeDtypeStruct((1, rows), f32)]
+    state = pl.pallas_call(
+        begin_kernel,
+        name="expert_begin",
+        in_specs=[VMEM] * 4,
+        out_specs=[VMEM] * 3,
+        out_shape=sums,
+        cost_estimate=cost,
+        compiler_params=params,
+    )(firsts[0], seconds[0], gate_w, up_w)
+    for i in (1, 2):
+        state = pl.pallas_call(
+            functools.partial(go_on_kernel, STEPS[i]),
+            name="expert_go_on",
+            in_specs=[VMEM] * 7,
+            out_specs=[VMEM] * 3,
+            out_shape=sums,
+            cost_estimate=cost,
+            input_output_aliases={4: 0, 5: 1, 6: 2},
+            compiler_params=params,
+        )(firsts[i], seconds[i], gate_w, up_w, *state)
+    return pl.pallas_call(
+        functools.partial(finish_kernel, STEPS[3]),
+        name="expert_finish",
+        in_specs=[VMEM] * 8,
+        out_specs=[VMEM] * 8,
+        out_shape=[jax.ShapeDtypeStruct((4, rows // 2, 2 * half), bf16)] * 8,
+        cost_estimate=cost,
+        compiler_params=params,
+    )(firsts[3], seconds[3], gate_w, up_w, *state, down_w)
+
+
+def add_kernel(*refs):
+    parts, out_refs = refs[:4], refs[4:]
+    for j, out_ref in enumerate(out_refs):
+        total = parts[0][j].astype(f32)
+        for part in parts[1:]:
+            total = total + part[j].astype(f32)
+        out_ref[...] = total.astype(bf16)
+
+
+def add_parts(parts):
+    count, rows, piece = parts[0].shape
+    return list(pl.pallas_call(
+        add_kernel,
+        name="add_parts",
+        in_specs=[VMEM] * 4,
+        out_specs=[VMEM] * count,
+        out_shape=[jax.ShapeDtypeStruct((rows, piece), bf16)] * count,
+        compiler_params=pltpu.CompilerParams(vmem_limit_bytes=8 << 20),
+    )(*parts))
+
+
+def total_kernel(*refs):
+    out_ref = refs[8]
+    place = lax.axis_index("expert")
+    for h in range(2):
+        total = refs[h * 4][...].astype(f32)
+        for part in refs[h * 4 + 1 : h * 4 + 4]:
+            total = total + part[...].astype(f32)
+        total = total.astype(bf16)
+        for i in range(4):
+            k, other = h * 2 + i // 2, i % 2
+            block = (place // 2 + 4 - k) % 4 * 2 + (place + other) % 2
+            out_ref[block] = total[i * CAP : (i + 1) * CAP]
+
+
+def total_parts(firsts, seconds):
+    piece = firsts[0].shape[1]
+    return pl.pallas_call(
+        total_kernel,
+        name="total_parts",
+        in_specs=[VMEM] * 8,
         out_specs=VMEM,
-        out_shape=jax.ShapeDtypeStruct(x.shape, bf16),
-        scratch_shapes=[
-            pltpu.VMEM((hidden, width), bf16),
-            pltpu.VMEM((hidden, width), bf16),
-            pltpu.VMEM((hidden, width), bf16),
-            pltpu.VMEM((rows, width), bf16),
-            pltpu.SemaphoreType.DMA((chunks,)),
-            pltpu.SemaphoreType.DMA((chunks,)),
-            pltpu.SemaphoreType.DMA((chunks,)),
-        ],
-        compiler_params=pltpu.CompilerParams(vmem_limit_bytes=40 << 20),
-    )(x, gain[None, :], gate_weight.T, up_weight.T, down_weight)
-
-
-def sum_kernel(parts_ref, out_ref):
-    total = parts_ref[0].astype(f32)
-    for n in range(1, parts_ref.shape[0]):
-        total = total + parts_ref[n].astype(f32)
-    out_ref[...] = total.astype(bf16)
-
-
-def sum_parts(parts):
-    return pl.pallas_call(
-        sum_kernel,
-        name="sum_parts",
-        in_specs=[VMEM],
-        out_specs=VMEM,
-        out_shape=jax.ShapeDtypeStruct(parts.shape[1:], bf16),
+        out_shape=jax.ShapeDtypeStruct((EXPERTS, CAP, piece), bf16),
         compiler_params=pltpu.CompilerParams(vmem_limit_bytes=8 << 20),
-    )(parts)
+    )(*firsts, *seconds)
 
 
 def combine_kernel(stream_ref, returned_ref, table_ref, out_ref):
@@ -267,11 +415,33 @@
     return lax.all_to_all(parts, axis, 0, 0, tiled=True)
 
 
+def along_expert(blocks):
+    kept = [blocks[0]] + [None] * 3
+    for k in (2, 1, 3):
+        pairs = [
+            (z * 2 + c, (z + k) % 4 * 2 + c) for z in range(4) for c in range(2)
+        ]
+        kept[k] = lax.ppermute(blocks[k], "expert", pairs)
+    pairs = [(z * 2 + c, z * 2 + 1 - c) for z in range(4) for c in range(2)]
+    passed = [lax.ppermute(block[CAP:], "expert", pairs) for block in kept]
+    return kept, passed
+
+
+def swapped(parts, axis):
+    return lax.all_to_all(parts, axis, 0, 0, tiled=True)
+
+
+def shifted(array, dx, dy):
+    pairs = [
+        (x * 4 + y, (x + dx) % 4 * 4 + (y + dy) % 4) for x in range(4) for y in range(4)
+    ]
+    return lax.ppermute(array, "hidden", pairs)
+
+
 def per_device(
     queries, new_key, new_value, key_cache, value_cache, cache_lengths, residual,
     out_weight, norm_gain, expert_ids, gate_weight, up_weight, down_weight,
 ):
-    requests = queries.shape[0]
     hidden_count = lax.axis_size("hidden")
     columns = out_weight.shape[1] // hidden_count
     partial_value, table = attend_project(
@@ -281,14 +451,20 @@
     own_residual = lax.dynamic_slice_in_dim(
         residual, lax.axis_index("hidden") * columns, columns, 1
     )
-    stream, outgoing = make_stream(swapped(partial_value, "hidden"), own_residual, table)
-    incoming = swapped(outgoing.reshape(EXPERTS, CAP, columns), "expert")
-    incoming = incoming.reshape(EXPERTS * CAP, columns)
-    copies = jnp.broadcast_to(incoming, (hidden_count, *incoming.shape))
-    gathered = swapped(copies, "hidden")
-    expert_part = run_expert(gathered, norm_gain, gate_weight[0], up_weight[0], down_weight[0])
-    expert_out = sum_parts(swapped(expert_part, "hidden"))
-    returned = swapped(expert_out.reshape(EXPERTS, CAP, columns), "expert")
+    stream, *blocks = make_stream(swapped(partial_value, "hidden"), own_residual, table)
+    gate_w, up_w, loaded = load_weights(gate_weight[0], up_weight[0], stream)
+    kept, passed = along_expert(blocks)
+    first, second = prepare(kept, passed, norm_gain, loaded)
+    first = jnp.concatenate([first] + [shifted(first, k, 0) for k in STEPS[1:]], axis=0)
+    second = jnp.concatenate([second] + [shifted(second, 0, k) for k in STEPS[1:]], axis=0)
+    firsts = [first] + [shifted(first, 0, k) for k in STEPS[1:]]
+    seconds = [second] + [shifted(second, k, 0) for k in STEPS[1:]]
+    parts = list(run_expert(firsts, seconds, gate_w, up_w, down_weight[0]))
+    firsts = add_parts(parts[:1] + [shifted(parts[k], k, 0) for k in range(1, 4)])
+    seconds = add_parts(parts[4:5] + [shifted(parts[4 + k], 0, k) for k in range(1, 4)])
+    firsts = firsts[:1] + [shifted(firsts[k], 0, k) for k in range(1, 4)]
+    seconds = seconds[:1] + [shifted(seconds[k], k, 0) for k in range(1, 4)]
+    returned = swapped(total_parts(firsts, seconds), "expert")
     return combine(stream, returned.reshape(EXPERTS * CAP, columns), table)
 
 

time: 135 us -> 114 us (0.84)
  blocking collectives: 54 us -> 18.5 us
  starting transfers between devices: 11.4 us -> 45.2 us
  local copies, waits for them, and re-layouts: 12.6 us -> 2.24 us
  waiting for transfers between devices: 38.9 us -> 29 us
    ppermute x0 -> x31, starting transfers between devices: none -> 37.6 us  [the longest x24 26.1 us: shifted(): return lax.ppermute(array, 'hidden', pairs)]
    all_to_all x3 -> x1, blocking collectives: 54 us -> 18.5 us  [swapped(): return lax.all_to_all(parts, axis, 0, 0, tiled=True)]
    all_to_all x2 -> x1, waiting for transfers between devices: 38.9 us -> 10.3 us  [swapped(): return lax.all_to_all(parts, axis, 0, 0, tiled=True)]
    ppermute x0 -> x31, waiting for transfers between devices: none -> 18.7 us  [the longest x24 18.7 us: shifted(): return lax.ppermute(array, 'hidden', pairs)]
    unnamed x22 -> x24, local copies, waits for them, and re-layouts: 11 us -> 2.19 us
    all_to_all x2 -> x1, starting transfers between devices: 11.4 us -> 7.58 us  [swapped(): return lax.all_to_all(parts, axis, 0, 0, tiled=True)]
    broadcast_in_dim x2 -> x1, local copies, waits for them, and re-layouts: 1.55 us -> 0.01 us  [prepare(): gain[None, :]]
    pallas_call x2 -> x9, Pallas kernels: 11.6 us -> 11.2 us  [the longest x1 4.91 us: load_weights(): pl.pallas_call(load_kernel, name='load_weights', in_specs=[ANY] * 3, out_...]
  transfers between devices with their start and end apart: 2 -> 32, of which waited for: 2 -> 12; matrix products, arithmetic and copies ran while one was open for 0% -> 0% of each run, Pallas kernels for 0% -> 7%
where the time goes in v2:
time: 114 us
  starting transfers between devices  45.2 us (40%)
  waiting for transfers between devices  29 us (25%)
  blocking collectives  18.5 us (16%)
  Pallas kernels  18.4 us (16%)
  local copies, waits for them, and re-layouts  2.24 us (2%)
    ppermute x24, starting transfers between devices, shifted(): return lax.ppermute(array, 'hidden', pairs)  26.1 us
    ppermute x24, waiting for transfers between devices, shifted(): return lax.ppermute(array, 'hidden', pairs)  18.7 us
    all_to_all x1, blocking collectives, swapped(): return lax.all_to_all(parts, axis, 0, 0, tiled=True)  18.5 us
    all_to_all x1, waiting for transfers between devices, swapped(): return lax.all_to_all(parts, axis, 0, 0, tiled=True)  10.3 us
    all_to_all x1, starting transfers between devices, swapped(): return lax.all_to_all(parts, axis, 0, 0, tiled=True)  7.58 us
    pallas_call x1, Pallas kernels, attend_project(): pl.pallas_call(attend_kernel, name='attend_project', in_specs=[ANY] * 8,...  6.15 us
    ppermute x4, starting transfers between devices, along_expert(): passed = [lax.ppermute(block[CAP:], 'expert', pairs) for block in kept]  5.81 us
    ppermute x3, starting transfers between devices, along_expert(): kept[k] = lax.ppermute(blocks[k], 'expert', pairs)  5.67 us
  transfers between devices with their start and end apart: 32, of which 12 were waited for; matrix products, arithmetic and copies ran while one was open for 0% of the time, Pallas kernels for 7%

profile of v2, /device:TPU:1, one launch (start us, length us, event | category | flops | bytes accessed | tf_op | source)
XLA Modules:
  0.0 113.7 jit_solution(17687017047359970400)
XLA Ops:
  0.0 6.1 %attend_project.1 = (bf16[16,64,256]{2,1,0:T(8,128)(2,1)}, bf16[256,64]{1,0:T(8,128)(2,1)}) custom-call(s32[1,64]{1,0:T(1,128)} %bitcast.17, bf16[64,256]{1,0:T(8,128)(2,1)} %q_hbm.1, bf16[64,256]{1,0:T(8,128)(2,1)} %nk_hbm.1, bf16[64,256]{1,0:T(8,128)(2,1)} %nv_hbm.1, bf16[64,2,64,128]{3,2,1,0:T(8,128)(2,1)} %k_hbm.1, bf16[64,2,64,128]{3,2,1,0:T(8,128)(2,1)} %v_hbm.1, ...), custom_call_target="tpu_custom_call" | custom-call | tf_op jit(solution)/shard_map/attend_project/pallas_call | solution.py:112
  6.2 7.6 %all-to-all-start = ((bf16[16,64,256]{2,1,0:T(8,128)(2,1)}), bf16[16,64,256]{2,1,0:T(8,128)(2,1)S(1)}, u32[]{:S(2)}, u32[]{:S(2)}) async-start(bf16[16,64,256]{2,1,0:T(8,128)(2,1)} %get-tuple-element.42), calls=%async_computation | async-start | bytes 1048576 | tf_op jit(solution)/shard_map/all_to_all | solution.py:431
  13.8 10.3 %all-to-all-done.parts_ref = bf16[16,64,256]{2,1,0:T(8,128)(2,1)S(1)} async-done(((bf16[16,64,256]{2,1,0:T(8,128)(2,1)}), bf16[16,64,256]{2,1,0:T(8,128)(2,1)S(1)}, u32[]{:S(2)}, u32[]{:S(2)}) %all-to-all-start) | async-done | bytes 524320 | tf_op jit(solution)/shard_map/all_to_all | solution.py:431
  25.8 1.6 %collective-permute-start = (bf16[64,256]{1,0:T(8,128)(2,1)S(1)}, bf16[64,256]{1,0:T(8,128)(2,1)S(1)}, u32[]{:S(2)}, u32[]{:S(2)}) collective-permute-start(bf16[64,256]{1,0:T(8,128)(2,1)S(1)} %get-tuple-element.46), channel_id=1, source_target_pairs={{0,32},{16,48},{32,64},{48,80},{64,96},{80,112},{96,0},{112,16},{1... | collective-permute-start | bytes 98312 | tf_op jit(solution)/shard_map/ppermute | solution.py:424
  27.5 3.3 %collective-permute-start.1 = (bf16[64,256]{1,0:T(8,128)(2,1)S(1)}, bf16[64,256]{1,0:T(8,128)(2,1)S(1)}, u32[]{:S(2)}, u32[]{:S(2)}) collective-permute-start(bf16[64,256]{1,0:T(8,128)(2,1)S(1)} %get-tuple-element.47), channel_id=1, source_target_pairs={{0,64},{16,80},{32,96},{48,112},{64,0},{80,16},{96,32},{112,48},{1... | collective-permute-start | bytes 98312 | tf_op jit(solution)/shard_map/ppermute | solution.py:424
  31.5 2.9 %collective-permute-start.3 = (bf16[32,256]{1,0:T(8,128)(2,1)S(1)}, bf16[32,256]{1,0:T(8,128)(2,1)S(1)}, u32[]{:S(2)}, u32[]{:S(2)}) collective-permute-start(bf16[32,256]{1,0:T(8,128)(2,1)S(1)} %slice.12), channel_id=1, source_target_pairs={{0,16},{16,0},{32,48},{48,32},{64,80},{80,64},{96,112},{112,96},{1... | collective-permute-start | bytes 49160 | tf_op jit(solution)/shard_map/ppermute | solution.py:426
  34.5 1.1 collective-permute-start.5
  35.6 1.7 %collective-permute-start.6 = (bf16[32,256]{1,0:T(8,128)(2,1)S(1)}, bf16[32,256]{1,0:T(8,128)(2,1)S(1)}, u32[]{:S(2)}, u32[]{:S(2)}) collective-permute-start(bf16[32,256]{1,0:T(8,128)(2,1)S(1)} %slice.18), channel_id=1, source_target_pairs={{0,16},{16,0},{32,48},{48,32},{64,80},{80,64},{96,112},{112,96},{1... | collective-permute-start | bytes 49160 | tf_op jit(solution)/shard_map/ppermute | solution.py:426
  37.3 4.9 %load_weights.1 = (bf16[688,4096]{1,0:T(8,128)(2,1)S(1)}, bf16[688,4096]{1,0:T(8,128)(2,1)S(1)}, f32[8,128]{1,0:T(8,128)}) custom-call(bf16[688,4096]{1,0:T(8,128)(2,1)} %bitcast.14, bf16[688,4096]{1,0:T(8,128)(2,1)} %bitcast.15, bf16[64,256]{1,0:T(8,128)(2,1)} %copy-done.3), custom_call_target="tpu_custom_call" | custom-call | bytes 22544384 | tf_op jit(solution)/shard_map/load_weights/pallas_call | solution.py:189
  43.5 2.4 %collective-permute-start.12 = (bf16[1,144,256]{2,1,0:T(8,128)(2,1)S(1)}, bf16[1,144,256]{2,1,0:T(8,128)(2,1)S(1)}, u32[]{:S(2)}, u32[]{:S(2)}) collective-permute-start(bf16[1,144,256]{2,1,0:T(8,128)(2,1)S(1)} %get-tuple-element.51), channel_id=1, source_target_pairs={{0,3},{1,0},{2,1},{3,2},{4,7},{5,4},{6,5},{7,6},{8,11},{9,8},{10,9... | collective-permute-start | bytes 221192 | tf_op jit(solution)/shard_map/ppermute | solution.py:438
  45.9 2.7 %collective-permute-start.8 = (bf16[1,128,256]{2,1,0:T(8,128)(2,1)S(1)}, bf16[1,128,256]{2,1,0:T(8,128)(2,1)S(1)}, u32[]{:S(2)}, u32[]{:S(2)}) collective-permute-start(bf16[1,128,256]{2,1,0:T(8,128)(2,1)S(1)} %get-tuple-element.50), channel_id=1, source_target_pairs={{0,12},{1,13},{2,14},{3,15},{4,0},{5,1},{6,2},{7,3},{8,4},{9,5},{1... | collective-permute-start | bytes 196616 | tf_op jit(solution)/shard_map/ppermute | solution.py:438
  48.6 1.6 %collective-permute-done.7 = bf16[1,128,256]{2,1,0:T(8,128)(2,1)S(1)} collective-permute-done((bf16[1,128,256]{2,1,0:T(8,128)(2,1)S(1)}, bf16[1,128,256]{2,1,0:T(8,128)(2,1)S(1)}, u32[]{:S(2)}, u32[]{:S(2)}) %collective-permute-start.7) | collective-permute-done | bytes 65568 | tf_op jit(solution)/shard_map/ppermute | solution.py:438
  50.6 4.3 %collective-permute-done.9 = bf16[1,128,256]{2,1,0:T(8,128)(2,1)S(1)} collective-permute-done((bf16[1,128,256]{2,1,0:T(8,128)(2,1)S(1)}, bf16[1,128,256]{2,1,0:T(8,128)(2,1)S(1)}, u32[]{:S(2)}, u32[]{:S(2)}) %collective-permute-start.9) | collective-permute-done | bytes 65568 | tf_op jit(solution)/shard_map/ppermute | solution.py:438
  55.7 1.9 %collective-permute-start.15 = (bf16[4,128,256]{2,1,0:T(8,128)(2,1)S(1)}, bf16[4,128,256]{2,1,0:T(8,128)(2,1)S(1)}, u32[]{:S(2)}, u32[]{:S(2)}) collective-permute-start(bf16[4,128,256]{2,1,0:T(8,128)(2,1)S(1)} %constant_dynamic-update-slice_fusion.first_ref), channel_id=1, source_target_pairs={{0,3},{1,0},{2,1},{3,2},{4,7},{5,4},{6,5},{7,6},{8,11},{9,8},{10,9... | collective-permute-start | bytes 786440 | tf_op jit(solution)/shard_map/ppermute | solution.py:438
  58.1 0.9 expert_begin.1
  59.0 2.6 %collective-permute-done.17.first_ref = bf16[4,128,256]{2,1,0:T(8,128)(2,1)S(1)} collective-permute-done((bf16[4,128,256]{2,1,0:T(8,128)(2,1)S(1)}, bf16[4,128,256]{2,1,0:T(8,128)(2,1)S(1)}, u32[]{:S(2)}, u32[]{:S(2)}) %collective-permute-start.17) | collective-permute-done | bytes 262176 | tf_op jit(solution)/shard_map/ppermute | solution.py:438
  61.6 1.8 %collective-permute-start.10 = (bf16[4,128,256]{2,1,0:T(8,128)(2,1)S(1)}, bf16[4,128,256]{2,1,0:T(8,128)(2,1)S(1)}, u32[]{:S(2)}, u32[]{:S(2)}) collective-permute-start(bf16[4,128,256]{2,1,0:T(8,128)(2,1)S(1)} %constant_dynamic-update-slice_fusion.first_ref), channel_id=1, source_target_pairs={{0,2},{1,3},{2,0},{3,1},{4,6},{5,7},{6,4},{7,5},{8,10},{9,11},{10,... | collective-permute-start | bytes 786440 | tf_op jit(solution)/shard_map/ppermute | solution.py:438
  63.4 1.0 expert_go_on.2
  64.5 1.0 expert_go_on.3
  65.5 3.2 %collective-permute-done.10.first_ref = bf16[4,128,256]{2,1,0:T(8,128)(2,1)S(1)} collective-permute-done((bf16[4,128,256]{2,1,0:T(8,128)(2,1)S(1)}, bf16[4,128,256]{2,1,0:T(8,128)(2,1)S(1)}, u32[]{:S(2)}, u32[]{:S(2)}) %collective-permute-start.10) | collective-permute-done | bytes 262176 | tf_op jit(solution)/shard_map/ppermute | solution.py:438
  68.7 2.9 %expert_finish.1 = (bf16[4,128,256]{2,1,0:T(8,128)(2,1)S(1)}, bf16[4,128,256]{2,1,0:T(8,128)(2,1)S(1)}, bf16[4,128,256]{2,1,0:T(8,128)(2,1)S(1)}, bf16[4,128,256...) custom-call(bf16[4,128,256]{2,1,0:T(8,128)(2,1)S(1)} %collective-per, ...), custom_call_target="tpu_custom_call" | custom-call | flops 1442840576 | bytes 4194304 | tf_op jit(solution)/shard_map/expert_finish/pallas_call | solution.py:340
  71.6 1.2 %collective-permute-start.25 = (bf16[4,128,256]{2,1,0:T(8,128)(2,1)S(1)}, bf16[4,128,256]{2,1,0:T(8,128)(2,1)S(1)}, u32[]{:S(2)}, u32[]{:S(2)}) collective-permute-start(bf16[4,128,256]{2,1,0:T(8,128)(2,1)S(1)} %get-tuple-element.72), channel_id=1, source_target_pairs={{0,1},{1,2},{2,3},{3,0},{4,5},{5,6},{6,7},{7,4},{8,9},{9,10},{10,1... | collective-permute-start | bytes 786440 | tf_op jit(solution)/shard_map/ppermute | solution.py:438
  72.8 2.3 %collective-permute-start.26 = (bf16[4,128,256]{2,1,0:T(8,128)(2,1)S(1)}, bf16[4,128,256]{2,1,0:T(8,128)(2,1)S(1)}, u32[]{:S(2)}, u32[]{:S(2)}) collective-permute-start(bf16[4,128,256]{2,1,0:T(8,128)(2,1)S(1)} %get-tuple-element.73), channel_id=1, source_target_pairs={{0,2},{1,3},{2,0},{3,1},{4,6},{5,7},{6,4},{7,5},{8,10},{9,11},{10,... | collective-permute-start | bytes 786440 | tf_op jit(solution)/shard_map/ppermute | solution.py:438
  75.6 2.1 %collective-permute-start.20 = (bf16[4,128,256]{2,1,0:T(8,128)(2,1)S(1)}, bf16[4,128,256]{2,1,0:T(8,128)(2,1)S(1)}, u32[]{:S(2)}, u32[]{:S(2)}) collective-permute-start(bf16[4,128,256]{2,1,0:T(8,128)(2,1)S(1)} %get-tuple-element.65), channel_id=1, source_target_pairs={{0,8},{1,9},{2,10},{3,11},{4,12},{5,13},{6,14},{7,15},{8,0},{9,1},... | collective-permute-start | bytes 786440 | tf_op jit(solution)/shard_map/ppermute | solution.py:438
  78.8 3.0 %collective-permute-done.26.refs_2_ = bf16[4,128,256]{2,1,0:T(8,128)(2,1)S(1)} collective-permute-done((bf16[4,128,256]{2,1,0:T(8,128)(2,1)S(1)}, bf16[4,128,256]{2,1,0:T(8,128)(2,1)S(1)}, u32[]{:S(2)}, u32[]{:S(2)}) %collective-permute-start.26) | collective-permute-done | bytes 262176 | tf_op jit(solution)/shard_map/ppermute | solution.py:438
  82.1 1.7 %collective-permute-start.29 = (bf16[128,256]{1,0:T(8,128)(2,1)S(1)}, bf16[128,256]{1,0:T(8,128)(2,1)S(1)}, u32[]{:S(2)}, u32[]{:S(2)}) collective-permute-start(bf16[128,256]{1,0:T(8,128)(2,1)S(1)} %get-tuple-element.77), channel_id=1, source_target_pairs={{0,8},{1,9},{2,10},{3,11},{4,12},{5,13},{6,14},{7,15},{8,0},{9,1},... | collective-permute-start | bytes 196616 | tf_op jit(solution)/shard_map/ppermute | solution.py:438
  83.8 1.3 %collective-permute-done.19.refs_1_ = bf16[4,128,256]{2,1,0:T(8,128)(2,1)S(1)} collective-permute-done((bf16[4,128,256]{2,1,0:T(8,128)(2,1)S(1)}, bf16[4,128,256]{2,1,0:T(8,128)(2,1)S(1)}, u32[]{:S(2)}, u32[]{:S(2)}) %collective-permute-start.19) | collective-permute-done | bytes 262176 | tf_op jit(solution)/shard_map/ppermute | solution.py:438
  85.8 1.1 collective-permute-start.22
  86.9 1.3 %collective-permute-start.23 = (bf16[128,256]{1,0:T(8,128)(2,1)S(1)}, bf16[128,256]{1,0:T(8,128)(2,1)S(1)}, u32[]{:S(2)}, u32[]{:S(2)}) collective-permute-start(bf16[128,256]{1,0:T(8,128)(2,1)S(1)} %get-tuple-element.69), channel_id=1, source_target_pairs={{0,2},{1,3},{2,0},{3,1},{4,6},{5,7},{6,4},{7,5},{8,10},{9,11},{10,... | collective-permute-start | bytes 196616 | tf_op jit(solution)/shard_map/ppermute | solution.py:438
  88.2 4.8 %collective-permute-start.24 = (bf16[128,256]{1,0:T(8,128)(2,1)S(1)}, bf16[128,256]{1,0:T(8,128)(2,1)S(1)}, u32[]{:S(2)}, u32[]{:S(2)}) collective-permute-start(bf16[128,256]{1,0:T(8,128)(2,1)S(1)} %get-tuple-element.70), channel_id=1, source_target_pairs={{0,3},{1,0},{2,1},{3,2},{4,7},{5,4},{6,5},{7,6},{8,11},{9,8},{10,9... | collective-permute-start | bytes 196616 | tf_op jit(solution)/shard_map/ppermute | solution.py:438
  93.0 1.3 %collective-permute-done.24.refs_3_ = bf16[128,256]{1,0:T(8,128)(2,1)S(1)} collective-permute-done((bf16[128,256]{1,0:T(8,128)(2,1)S(1)}, bf16[128,256]{1,0:T(8,128)(2,1)S(1)}, u32[]{:S(2)}, u32[]{:S(2)}) %collective-permute-start.24) | collective-permute-done | bytes 65568 | tf_op jit(solution)/shard_map/ppermute | solution.py:438
  94.3 18.5 %all_to_all.10 = bf16[8,32,256]{2,1,0:T(8,128)(2,1)S(1)} all-to-all(bf16[8,32,256]{2,1,0:T(8,128)(2,1)S(1)} %total_parts.1), channel_id=1, replica_groups=mesh['expert'=8,'hidden'=16] {'expert'}, dimensions={0} | all-to-all | bytes 262144 | tf_op jit(solution)/shard_map/all_to_all | solution.py:431
  (78 shorter events, 9.0 us)
Async XLA Ops:
  6.2 18.0 %all-to-all-start = ((bf16[16,64,256]{2,1,0:T(8,128)(2,1)}), bf16[16,64,256]{2,1,0:T(8,128)(2,1)S(1)}, u32[]{:S(2)}, u32[]{:S(2)}) async-start(bf16[16,64,256]{2,1,0:T(8,128)(2,1)} %get-tuple-element.42), calls=%async_computation | async-start | bytes 1048576 | tf_op jit(solution)/shard_map/all_to_all | solution.py:431
  25.8 8.6 %collective-permute-start = (bf16[64,256]{1,0:T(8,128)(2,1)S(1)}, bf16[64,256]{1,0:T(8,128)(2,1)S(1)}, u32[]{:S(2)}, u32[]{:S(2)}) collective-permute-start(bf16[64,256]{1,0:T(8,128)(2,1)S(1)} %get-tuple-element.46), channel_id=1, source_target_pairs={{0,32},{16,48},{32,64},{48,80},{64,96},{80,112},{96,0},{112,16},{1... | collective-permute-start | bytes 98312 | tf_op jit(solution)/shard_map/ppermute | solution.py:424
  27.5 7.1 %collective-permute-start.1 = (bf16[64,256]{1,0:T(8,128)(2,1)S(1)}, bf16[64,256]{1,0:T(8,128)(2,1)S(1)}, u32[]{:S(2)}, u32[]{:S(2)}) collective-permute-start(bf16[64,256]{1,0:T(8,128)(2,1)S(1)} %get-tuple-element.47), channel_id=1, source_target_pairs={{0,64},{16,80},{32,96},{48,112},{64,0},{80,16},{96,32},{112,48},{1... | collective-permute-start | bytes 98312 | tf_op jit(solution)/shard_map/ppermute | solution.py:424
  30.8 4.9 %collective-permute-start.2 = (bf16[64,256]{1,0:T(8,128)(2,1)S(1)}, bf16[64,256]{1,0:T(8,128)(2,1)S(1)}, u32[]{:S(2)}, u32[]{:S(2)}) collective-permute-start(bf16[64,256]{1,0:T(8,128)(2,1)S(1)} %get-tuple-element.48), channel_id=1, source_target_pairs={{0,96},{16,112},{32,0},{48,16},{64,32},{80,48},{96,64},{112,80},{1... | collective-permute-start | bytes 98312 | tf_op jit(solution)/shard_map/ppermute | solution.py:424
  31.5 10.8 %collective-permute-start.3 = (bf16[32,256]{1,0:T(8,128)(2,1)S(1)}, bf16[32,256]{1,0:T(8,128)(2,1)S(1)}, u32[]{:S(2)}, u32[]{:S(2)}) collective-permute-start(bf16[32,256]{1,0:T(8,128)(2,1)S(1)} %slice.12), channel_id=1, source_target_pairs={{0,16},{16,0},{32,48},{48,32},{64,80},{80,64},{96,112},{112,96},{1... | collective-permute-start | bytes 49160 | tf_op jit(solution)/shard_map/ppermute | solution.py:426
  34.4 7.9 %collective-permute-start.4 = (bf16[32,256]{1,0:T(8,128)(2,1)S(1)}, bf16[32,256]{1,0:T(8,128)(2,1)S(1)}, u32[]{:S(2)}, u32[]{:S(2)}) collective-permute-start(bf16[32,256]{1,0:T(8,128)(2,1)S(1)} %slice.16), channel_id=1, source_target_pairs={{0,16},{16,0},{32,48},{48,32},{64,80},{80,64},{96,112},{112,96},{1... | collective-permute-start | bytes 49160 | tf_op jit(solution)/shard_map/ppermute | solution.py:426
  34.5 7.8 %collective-permute-start.5 = (bf16[32,256]{1,0:T(8,128)(2,1)S(1)}, bf16[32,256]{1,0:T(8,128)(2,1)S(1)}, u32[]{:S(2)}, u32[]{:S(2)}) collective-permute-start(bf16[32,256]{1,0:T(8,128)(2,1)S(1)} %slice.17), channel_id=1, source_target_pairs={{0,16},{16,0},{32,48},{48,32},{64,80},{80,64},{96,112},{112,96},{1... | collective-permute-start | bytes 49160 | tf_op jit(solution)/shard_map/ppermute | solution.py:426
  35.6 6.6 %collective-permute-start.6 = (bf16[32,256]{1,0:T(8,128)(2,1)S(1)}, bf16[32,256]{1,0:T(8,128)(2,1)S(1)}, u32[]{:S(2)}, u32[]{:S(2)}) collective-permute-start(bf16[32,256]{1,0:T(8,128)(2,1)S(1)} %slice.18), channel_id=1, source_target_pairs={{0,16},{16,0},{32,48},{48,32},{64,80},{80,64},{96,112},{112,96},{1... | collective-permute-start | bytes 49160 | tf_op jit(solution)/shard_map/ppermute | solution.py:426
  43.1 7.1 %collective-permute-start.11 = (bf16[1,144,256]{2,1,0:T(8,128)(2,1)S(1)}, bf16[1,144,256]{2,1,0:T(8,128)(2,1)S(1)}, u32[]{:S(2)}, u32[]{:S(2)}) collective-permute-start(bf16[1,144,256]{2,1,0:T(8,128)(2,1)S(1)} %get-tuple-element.51), channel_id=1, source_target_pairs={{0,1},{1,2},{2,3},{3,0},{4,5},{5,6},{6,7},{7,4},{8,9},{9,10},{10,1... | collective-permute-start | bytes 221192 | tf_op jit(solution)/shard_map/ppermute | solution.py:438
  43.5 6.8 %collective-permute-start.12 = (bf16[1,144,256]{2,1,0:T(8,128)(2,1)S(1)}, bf16[1,144,256]{2,1,0:T(8,128)(2,1)S(1)}, u32[]{:S(2)}, u32[]{:S(2)}) collective-permute-start(bf16[1,144,256]{2,1,0:T(8,128)(2,1)S(1)} %get-tuple-element.51), channel_id=1, source_target_pairs={{0,3},{1,0},{2,1},{3,2},{4,7},{5,4},{6,5},{7,6},{8,11},{9,8},{10,9... | collective-permute-start | bytes 221192 | tf_op jit(solution)/shard_map/ppermute | solution.py:438
  45.9 4.7 %collective-permute-start.13 = (bf16[1,144,256]{2,1,0:T(8,128)(2,1)S(1)}, bf16[1,144,256]{2,1,0:T(8,128)(2,1)S(1)}, u32[]{:S(2)}, u32[]{:S(2)}) collective-permute-start(bf16[1,144,256]{2,1,0:T(8,128)(2,1)S(1)} %get-tuple-element.51), channel_id=1, source_target_pairs={{0,2},{1,3},{2,0},{3,1},{4,6},{5,7},{6,4},{7,5},{8,10},{9,11},{10,... | collective-permute-start | bytes 221192 | tf_op jit(solution)/shard_map/ppermute | solution.py:438
  45.9 4.3 %collective-permute-start.7 = (bf16[1,128,256]{2,1,0:T(8,128)(2,1)S(1)}, bf16[1,128,256]{2,1,0:T(8,128)(2,1)S(1)}, u32[]{:S(2)}, u32[]{:S(2)}) collective-permute-start(bf16[1,128,256]{2,1,0:T(8,128)(2,1)S(1)} %get-tuple-element.50), channel_id=1, source_target_pairs={{0,4},{1,5},{2,6},{3,7},{4,8},{5,9},{6,10},{7,11},{8,12},{9,13},{1... | collective-permute-start | bytes 196616 | tf_op jit(solution)/shard_map/ppermute | solution.py:438
  45.9 4.3 %collective-permute-start.8 = (bf16[1,128,256]{2,1,0:T(8,128)(2,1)S(1)}, bf16[1,128,256]{2,1,0:T(8,128)(2,1)S(1)}, u32[]{:S(2)}, u32[]{:S(2)}) collective-permute-start(bf16[1,128,256]{2,1,0:T(8,128)(2,1)S(1)} %get-tuple-element.50), channel_id=1, source_target_pairs={{0,12},{1,13},{2,14},{3,15},{4,0},{5,1},{6,2},{7,3},{8,4},{9,5},{1... | collective-permute-start | bytes 196616 | tf_op jit(solution)/shard_map/ppermute | solution.py:438
  50.2 4.7 %collective-permute-start.9 = (bf16[1,128,256]{2,1,0:T(8,128)(2,1)S(1)}, bf16[1,128,256]{2,1,0:T(8,128)(2,1)S(1)}, u32[]{:S(2)}, u32[]{:S(2)}) collective-permute-start(bf16[1,128,256]{2,1,0:T(8,128)(2,1)S(1)} %get-tuple-element.50), channel_id=1, source_target_pairs={{0,8},{1,9},{2,10},{3,11},{4,12},{5,13},{6,14},{7,15},{8,0},{9,1},... | collective-permute-start | bytes 196616 | tf_op jit(solution)/shard_map/ppermute | solution.py:438
  50.6 12.8 %collective-permute-start.18 = (bf16[4,144,256]{2,1,0:T(8,128)(2,1)S(1)}, bf16[4,144,256]{2,1,0:T(8,128)(2,1)S(1)}, u32[]{:S(2)}, u32[]{:S(2)}) collective-permute-start(bf16[4,144,256]{2,1,0:T(8,128)(2,1)S(1)} %constant_dynamic-update-slice_fusion.4.second_ref), channel_id=1, source_target_pairs={{0,4},{1,5},{2,6},{3,7},{4,8},{5,9},{6,10},{7,11},{8,12},{9,13},{1... | collective-permute-start | bytes 884744 | tf_op jit(solution)/shard_map/ppermute | solution.py:438
  54.9 6.7 %collective-permute-start.17 = (bf16[4,128,256]{2,1,0:T(8,128)(2,1)S(1)}, bf16[4,128,256]{2,1,0:T(8,128)(2,1)S(1)}, u32[]{:S(2)}, u32[]{:S(2)}) collective-permute-start(bf16[4,128,256]{2,1,0:T(8,128)(2,1)S(1)} %constant_dynamic-update-slice_fusion.first_ref), channel_id=1, source_target_pairs={{0,1},{1,2},{2,3},{3,0},{4,5},{5,6},{6,7},{7,4},{8,9},{9,10},{10,1... | collective-permute-start | bytes 786440 | tf_op jit(solution)/shard_map/ppermute | solution.py:438
  55.7 8.8 %collective-permute-start.16 = (bf16[4,144,256]{2,1,0:T(8,128)(2,1)S(1)}, bf16[4,144,256]{2,1,0:T(8,128)(2,1)S(1)}, u32[]{:S(2)}, u32[]{:S(2)}) collective-permute-start(bf16[4,144,256]{2,1,0:T(8,128)(2,1)S(1)} %constant_dynamic-update-slice_fusion.4.second_ref), channel_id=1, source_target_pairs={{0,12},{1,13},{2,14},{3,15},{4,0},{5,1},{6,2},{7,3},{8,4},{9,5},{1... | collective-permute-start | bytes 884744 | tf_op jit(solution)/shard_map/ppermute | solution.py:438
  55.7 8.8 %collective-permute-start.15 = (bf16[4,128,256]{2,1,0:T(8,128)(2,1)S(1)}, bf16[4,128,256]{2,1,0:T(8,128)(2,1)S(1)}, u32[]{:S(2)}, u32[]{:S(2)}) collective-permute-start(bf16[4,128,256]{2,1,0:T(8,128)(2,1)S(1)} %constant_dynamic-update-slice_fusion.first_ref), channel_id=1, source_target_pairs={{0,3},{1,0},{2,1},{3,2},{4,7},{5,4},{6,5},{7,6},{8,11},{9,8},{10,9... | collective-permute-start | bytes 786440 | tf_op jit(solution)/shard_map/ppermute | solution.py:438
  57.6 11.1 %collective-permute-start.14 = (bf16[4,144,256]{2,1,0:T(8,128)(2,1)S(1)}, bf16[4,144,256]{2,1,0:T(8,128)(2,1)S(1)}, u32[]{:S(2)}, u32[]{:S(2)}) collective-permute-start(bf16[4,144,256]{2,1,0:T(8,128)(2,1)S(1)} %constant_dynamic-update-slice_fusion.4.second_ref), channel_id=1, source_target_pairs={{0,8},{1,9},{2,10},{3,11},{4,12},{5,13},{6,14},{7,15},{8,0},{9,1},... | collective-permute-start | bytes 884744 | tf_op jit(solution)/shard_map/ppermute | solution.py:438
  61.6 7.1 %collective-permute-start.10 = (bf16[4,128,256]{2,1,0:T(8,128)(2,1)S(1)}, bf16[4,128,256]{2,1,0:T(8,128)(2,1)S(1)}, u32[]{:S(2)}, u32[]{:S(2)}) collective-permute-start(bf16[4,128,256]{2,1,0:T(8,128)(2,1)S(1)} %constant_dynamic-update-slice_fusion.first_ref), channel_id=1, source_target_pairs={{0,2},{1,3},{2,0},{3,1},{4,6},{5,7},{6,4},{7,5},{8,10},{9,11},{10,... | collective-permute-start | bytes 786440 | tf_op jit(solution)/shard_map/ppermute | solution.py:438
  71.6 6.5 %collective-permute-start.25 = (bf16[4,128,256]{2,1,0:T(8,128)(2,1)S(1)}, bf16[4,128,256]{2,1,0:T(8,128)(2,1)S(1)}, u32[]{:S(2)}, u32[]{:S(2)}) collective-permute-start(bf16[4,128,256]{2,1,0:T(8,128)(2,1)S(1)} %get-tuple-element.72), channel_id=1, source_target_pairs={{0,1},{1,2},{2,3},{3,0},{4,5},{5,6},{6,7},{7,4},{8,9},{9,10},{10,1... | collective-permute-start | bytes 786440 | tf_op jit(solution)/shard_map/ppermute | solution.py:438
  72.8 9.0 %collective-permute-start.26 = (bf16[4,128,256]{2,1,0:T(8,128)(2,1)S(1)}, bf16[4,128,256]{2,1,0:T(8,128)(2,1)S(1)}, u32[]{:S(2)}, u32[]{:S(2)}) collective-permute-start(bf16[4,128,256]{2,1,0:T(8,128)(2,1)S(1)} %get-tuple-element.73), channel_id=1, source_target_pairs={{0,2},{1,3},{2,0},{3,1},{4,6},{5,7},{6,4},{7,5},{8,10},{9,11},{10,... | collective-permute-start | bytes 786440 | tf_op jit(solution)/shard_map/ppermute | solution.py:438
  75.0 6.8 %collective-permute-start.27 = (bf16[4,128,256]{2,1,0:T(8,128)(2,1)S(1)}, bf16[4,128,256]{2,1,0:T(8,128)(2,1)S(1)}, u32[]{:S(2)}, u32[]{:S(2)}) collective-permute-start(bf16[4,128,256]{2,1,0:T(8,128)(2,1)S(1)} %get-tuple-element.74), channel_id=1, source_target_pairs={{0,3},{1,0},{2,1},{3,2},{4,7},{5,4},{6,5},{7,6},{8,11},{9,8},{10,9... | collective-permute-start | bytes 786440 | tf_op jit(solution)/shard_map/ppermute | solution.py:438
  75.5 9.5 %collective-permute-start.19 = (bf16[4,128,256]{2,1,0:T(8,128)(2,1)S(1)}, bf16[4,128,256]{2,1,0:T(8,128)(2,1)S(1)}, u32[]{:S(2)}, u32[]{:S(2)}) collective-permute-start(bf16[4,128,256]{2,1,0:T(8,128)(2,1)S(1)} %get-tuple-element.64), channel_id=1, source_target_pairs={{0,4},{1,5},{2,6},{3,7},{4,8},{5,9},{6,10},{7,11},{8,12},{9,13},{1... | collective-permute-start | bytes 786440 | tf_op jit(solution)/shard_map/ppermute | solution.py:438
  75.6 9.4 %collective-permute-start.20 = (bf16[4,128,256]{2,1,0:T(8,128)(2,1)S(1)}, bf16[4,128,256]{2,1,0:T(8,128)(2,1)S(1)}, u32[]{:S(2)}, u32[]{:S(2)}) collective-permute-start(bf16[4,128,256]{2,1,0:T(8,128)(2,1)S(1)} %get-tuple-element.65), channel_id=1, source_target_pairs={{0,8},{1,9},{2,10},{3,11},{4,12},{5,13},{6,14},{7,15},{8,0},{9,1},... | collective-permute-start | bytes 786440 | tf_op jit(solution)/shard_map/ppermute | solution.py:438
  78.1 7.5 %collective-permute-start.21 = (bf16[4,128,256]{2,1,0:T(8,128)(2,1)S(1)}, bf16[4,128,256]{2,1,0:T(8,128)(2,1)S(1)}, u32[]{:S(2)}, u32[]{:S(2)}) collective-permute-start(bf16[4,128,256]{2,1,0:T(8,128)(2,1)S(1)} %get-tuple-element.66), channel_id=1, source_target_pairs={{0,12},{1,13},{2,14},{3,15},{4,0},{5,1},{6,2},{7,3},{8,4},{9,5},{1... | collective-permute-start | bytes 786440 | tf_op jit(solution)/shard_map/ppermute | solution.py:438
  82.0 6.2 %collective-permute-start.28 = (bf16[128,256]{1,0:T(8,128)(2,1)S(1)}, bf16[128,256]{1,0:T(8,128)(2,1)S(1)}, u32[]{:S(2)}, u32[]{:S(2)}) collective-permute-start(bf16[128,256]{1,0:T(8,128)(2,1)S(1)} %get-tuple-element.76), channel_id=1, source_target_pairs={{0,4},{1,5},{2,6},{3,7},{4,8},{5,9},{6,10},{7,11},{8,12},{9,13},{1... | collective-permute-start | bytes 196616 | tf_op jit(solution)/shard_map/ppermute | solution.py:438
  82.1 10.9 %collective-permute-start.29 = (bf16[128,256]{1,0:T(8,128)(2,1)S(1)}, bf16[128,256]{1,0:T(8,128)(2,1)S(1)}, u32[]{:S(2)}, u32[]{:S(2)}) collective-permute-start(bf16[128,256]{1,0:T(8,128)(2,1)S(1)} %get-tuple-element.77), channel_id=1, source_target_pairs={{0,8},{1,9},{2,10},{3,11},{4,12},{5,13},{6,14},{7,15},{8,0},{9,1},... | collective-permute-start | bytes 196616 | tf_op jit(solution)/shard_map/ppermute | solution.py:438
  85.0 7.9 %collective-permute-start.30 = (bf16[128,256]{1,0:T(8,128)(2,1)S(1)}, bf16[128,256]{1,0:T(8,128)(2,1)S(1)}, u32[]{:S(2)}, u32[]{:S(2)}) collective-permute-start(bf16[128,256]{1,0:T(8,128)(2,1)S(1)} %get-tuple-element.78), channel_id=1, source_target_pairs={{0,12},{1,13},{2,14},{3,15},{4,0},{5,1},{6,2},{7,3},{8,4},{9,5},{1... | collective-permute-start | bytes 196616 | tf_op jit(solution)/shard_map/ppermute | solution.py:438
  85.8 7.2 %collective-permute-start.22 = (bf16[128,256]{1,0:T(8,128)(2,1)S(1)}, bf16[128,256]{1,0:T(8,128)(2,1)S(1)}, u32[]{:S(2)}, u32[]{:S(2)}) collective-permute-start(bf16[128,256]{1,0:T(8,128)(2,1)S(1)} %get-tuple-element.68), channel_id=1, source_target_pairs={{0,1},{1,2},{2,3},{3,0},{4,5},{5,6},{6,7},{7,4},{8,9},{9,10},{10,1... | collective-permute-start | bytes 196616 | tf_op jit(solution)/shard_map/ppermute | solution.py:438
  86.9 6.1 %collective-permute-start.23 = (bf16[128,256]{1,0:T(8,128)(2,1)S(1)}, bf16[128,256]{1,0:T(8,128)(2,1)S(1)}, u32[]{:S(2)}, u32[]{:S(2)}) collective-permute-start(bf16[128,256]{1,0:T(8,128)(2,1)S(1)} %get-tuple-element.69), channel_id=1, source_target_pairs={{0,2},{1,3},{2,0},{3,1},{4,6},{5,7},{6,4},{7,5},{8,10},{9,11},{10,... | collective-permute-start | bytes 196616 | tf_op jit(solution)/shard_map/ppermute | solution.py:438
  88.2 6.1 %collective-permute-start.24 = (bf16[128,256]{1,0:T(8,128)(2,1)S(1)}, bf16[128,256]{1,0:T(8,128)(2,1)S(1)}, u32[]{:S(2)}, u32[]{:S(2)}) collective-permute-start(bf16[128,256]{1,0:T(8,128)(2,1)S(1)} %get-tuple-element.70), channel_id=1, source_target_pairs={{0,3},{1,0},{2,1},{3,2},{4,7},{5,4},{6,5},{7,6},{8,11},{9,8},{10,9... | collective-permute-start | bytes 196616 | tf_op jit(solution)/shard_map/ppermute | solution.py:438
  (9 other events, 151.0 us)

commit v3 on v2

v3 whole, which is shorter than its diff:
```python
import functools
import math

import jax
import jax.numpy as jnp
from jax import lax
from jax.experimental import pallas as pl
from jax.experimental.pallas import tpu as pltpu
from jax.sharding import PartitionSpec as P

epsilon = 1e-05
bf16 = jnp.bfloat16
f32 = jnp.float32
ANY = pl.BlockSpec(memory_space=pl.ANY)
VMEM = pl.BlockSpec(memory_space=pltpu.VMEM)

EXPERTS = 8
CAP = 32
GROUP = 16
STATS = 16
STEPS = (0, 1, 3, 2)


def dot(a, b, dims):
    return lax.dot_general(a, b, (dims, ((), ())), preferred_element_type=f32)


def hidden_at():
    hidden = lax.axis_index("hidden")
    return hidden // 4, hidden % 4


def lanes_of(n, size, offset=0, width=None):
    step = math.gcd(size, offset) if offset else size
    return pl.ds(pl.multiple_of(n * size + offset, step), width or size)


def half_lanes(c, j, k, piece):
    x_at, y_at = hidden_at()
    owner = jnp.where(c == 0, j * 4 + (y_at + k) % 4, (x_at + k) % 4 * 4 + j)
    return pl.ds(pl.multiple_of(owner * piece + c * (piece // 2), piece // 2), piece // 2)


def core_at():
    return lax.axis_index("expert") % 2


def attend_kernel(
    lens_hbm, q_hbm, nk_hbm, nv_hbm, k_hbm, v_hbm, w_hbm, residual_hbm, ids_hbm,
    attended, given, own_residual, w_half,
    lens, q, nk, nv, k, v, ids, small_sem, k_sem, v_sem, w_sem, residual_sem,
):
    requests, head_count, positions, size = k.shape
    groups = requests // GROUP
    small = [
        pltpu.make_async_copy(src, dst, small_sem.at[i])
        for i, (src, dst) in enumerate(
            ((lens_hbm, lens), (q_hbm, q), (nk_hbm, nk), (nv_hbm, nv), (ids_hbm, ids))
        )
    ]
    for copy in small:
        copy.start()
    keys, values = [], []
    for g in range(groups):
        rows = pl.ds(g * GROUP, GROUP)
        keys.append(pltpu.make_async_copy(k_hbm.at[rows], k.at[rows], k_sem.at[g]))
        values.append(pltpu.make_async_copy(v_hbm.at[rows], v.at[rows], v_sem.at[g]))
        keys[g].start()
        values[g].start()
    c = core_at()
    piece = 2 * size
    others = []
    for j in range(4):
        here = pl.ds(j * size, size)
        there = pl.ds(piece + j * size, size)
        others.append(
            pltpu.make_async_copy(
                residual_hbm.at[:, half_lanes(c, j, 0, piece)],
                own_residual.at[:, here],
                residual_sem.at[j],
            )
        )
        others.append(
            pltpu.make_async_copy(
                residual_hbm.at[:, half_lanes(1 - c, j, 0, piece)],
                given.at[pl.ds(0, requests), there],
                residual_sem.at[4 + j],
            )
        )
    for n in range(w_half.shape[1] // size):
        source = pl.ds(pl.multiple_of(n * piece + c * size, size), size)
        others.append(
            pltpu.make_async_copy(
                w_hbm.at[:, source], w_half.at[:, pl.ds(n * size, size)], w_sem.at[n]
            )
        )
    for copy in others:
        copy.start()
    for copy in small:
        copy.wait()

    scale = 1.0 / math.sqrt(size)
    row = lax.broadcasted_iota(jnp.int32, (requests, requests), 0)
    col = lax.broadcasted_iota(jnp.int32, (requests, requests), 1)
    length = jnp.sum(jnp.where(row == col, lens[...], 0), axis=1, keepdims=True)
    place = lax.broadcasted_iota(jnp.int32, (GROUP, GROUP * positions), 1)
    first = lax.broadcasted_iota(jnp.int32, (GROUP, GROUP * positions), 0) * positions
    for g in range(groups):
        rows = slice(g * GROUP, (g + 1) * GROUP)
        keys[g].wait()
        values[g].wait()
        valid = (place >= first) & (place < first + length[rows])
        for h in range(head_count):
            lanes = slice(h * size, (h + 1) * size)
            query = q[rows, lanes]
            own_score = (
                jnp.sum(query.astype(f32) * nk[rows, lanes].astype(f32), axis=1, keepdims=True)
                * scale
            )
            key_rows = k[rows, h].reshape(GROUP * positions, size)
            scores = dot(query, key_rows, ((1,), (1,))) * scale
            masked = jnp.where(valid, scores, f32(-1e30))
            highest = jnp.maximum(jnp.max(masked, axis=1, keepdims=True), own_score)
            weights = jnp.where(valid, jnp.exp(masked - highest), f32(0.0))
            own_weight = jnp.exp(own_score - highest)
            total = jnp.sum(weights, axis=1, keepdims=True) + own_weight
            value_rows = v[rows, h].reshape(GROUP * positions, size)
            mixed = dot(weights.astype(bf16), value_rows, ((1,), (0,)))
            own_rounded = own_weight.astype(bf16).astype(f32)
            mixed = mixed + own_rounded * nv[rows, lanes].astype(f32)
            attended[rows, lanes] = (mixed / total).astype(bf16)
    for copy in others:
        copy.wait()
    given[:requests, :piece] = attended[...]
    given[requests:, :] = jnp.zeros((given.shape[0] - requests, given.shape[1]), bf16)
    given[requests : requests + 2, :requests] = ids[...].astype(f32).astype(bf16)


def attend(queries, new_key, new_value, key_cache, value_cache, lengths, out_weight, residual, ids):
    requests, _, _, size = key_cache.shape
    groups = requests // GROUP
    width = out_weight.shape[1]
    return pl.pallas_call(
        attend_kernel,
        name="attend",
        in_specs=[ANY] * 9,
        out_specs=[VMEM] * 4,
        out_shape=[
            pltpu.VMEM(queries.shape, bf16),
            pltpu.VMEM((requests + STATS, queries.shape[1] + width // 8), bf16),
            pltpu.VMEM((requests, width // 8), bf16),
            pltpu.VMEM((out_weight.shape[0], width // 2), bf16),
        ],
        scratch_shapes=[
            pltpu.VMEM((1, requests), jnp.int32),
            pltpu.VMEM(queries.shape, bf16),
            pltpu.VMEM(queries.shape, bf16),
            pltpu.VMEM(queries.shape, bf16),
            pltpu.VMEM(key_cache.shape, bf16),
            pltpu.VMEM(value_cache.shape, bf16),
            pltpu.VMEM(ids.shape, jnp.int32),
            pltpu.SemaphoreType.DMA((5,)),
            pltpu.SemaphoreType.DMA((groups,)),
            pltpu.SemaphoreType.DMA((groups,)),
            pltpu.SemaphoreType.DMA((width // 2 // size,)),
            pltpu.SemaphoreType.DMA((8,)),
        ],
        compiler_params=pltpu.CompilerParams(vmem_limit_bytes=65_000_000),
    )(lengths[None, :], queries, new_key, new_value, key_cache, value_cache, out_weight, residual, ids)


def in_core_order(own, other):
    first = core_at() == 0
    return jnp.concatenate([jnp.where(first, own, other), jnp.where(first, other, own)], axis=0)


def project_kernel(attended_ref, got_ref, w_half, *out_refs):
    piece = attended_ref.shape[1]
    half = piece // 2
    c = core_at()
    x_at, y_at = hidden_at()
    rows = in_core_order(
        attended_ref[...].astype(f32), got_ref[: attended_ref.shape[0], :piece].astype(f32)
    ).astype(bf16)
    for k, out_ref in enumerate(out_refs):
        weight = jnp.concatenate(
            [
                w_half[
                    :,
                    lanes_of(
                        jnp.where(c == 0, j * 4 + (y_at + k) % 4, (x_at + k) % 4 * 4 + j), half
                    ),
                ]
                for j in range(4)
            ],
            axis=1,
        )
        out_ref[...] = dot(rows, weight, ((1,), (0,))).astype(bf16)


def project(attended, got, w_half):
    requests = attended.shape[0]
    return list(
        pl.pallas_call(
            project_kernel,
            name="project",
            in_specs=[VMEM] * 3,
            out_specs=[VMEM] * 4,
            out_shape=[pltpu.VMEM((2 * requests, w_half.shape[1] // 4), bf16)] * 4,
            compiler_params=pltpu.CompilerParams(vmem_limit_bytes=8 << 20),
        )(attended, got, w_half)
    )


def table_kernel(ids_ref, got_ref, *table_refs):
    requests = ids_ref.shape[1]
    first = core_at() == 0
    slots = EXPERTS * CAP
    slot = lax.broadcasted_iota(jnp.int32, (slots, requests), 0)
    expert = slot // CAP
    earlier = (
        lax.broadcasted_iota(jnp.int32, (requests, requests), 0)
        < lax.broadcasted_iota(jnp.int32, (requests, requests), 1)
    )
    earlier = jnp.where(earlier, 1.0, 0.0).astype(bf16)
    own = ids_ref[...]
    other = got_ref[requests : requests + 2, :requests].astype(f32).astype(jnp.int32)
    for i, table_ref in enumerate(table_refs):
        ids = jnp.where(first, own, other) if i == 0 else jnp.where(first, other, own)
        named = (ids[0:1, :] == expert) | (ids[1:2, :] == expert)
        count = dot(jnp.where(named, 1.0, 0.0).astype(bf16), earlier, ((1,), (0,)))
        taken = named & (count.astype(jnp.int32) == slot - expert * CAP)
        table_ref[...] = jnp.where(taken, 1.0, 0.0).astype(bf16)


def tables_of(ids, got):
    return pl.pallas_call(
        table_kernel,
        name="tables_of",
        in_specs=[VMEM] * 2,
        out_specs=[VMEM] * 2,
        out_shape=[pltpu.VMEM((EXPERTS * CAP, ids.shape[1]), bf16)] * 2,
        compiler_params=pltpu.CompilerParams(vmem_limit_bytes=8 << 20),
    )(ids, got)


def stream_kernel(*refs):
    parts = refs[:4]
    residual_ref, got_ref, first_table, second_table = refs[4:8]
    own_ref, given_ref = refs[8:10]
    block_refs, held = refs[10:14], refs[14]
    rows, span = parts[0].shape
    requests, half = rows // 2, span // 4
    c = core_at()
    z = lax.axis_index("expert") // 2
    x_at, y_at = hidden_at()
    projected = parts[0][...].astype(f32)
    for part in parts[1:]:
        projected = projected + part[...].astype(f32)
    residual = in_core_order(
        residual_ref[...].astype(f32), got_ref[:requests, 2 * half :].astype(f32)
    )
    held[...] = (residual + projected).astype(bf16)
    home = lanes_of(jnp.where(c == 0, x_at, y_at), half)
    own_ref[...] = held[pl.ds(pl.multiple_of(c * requests, requests), requests), home]
    given_ref[...] = held[pl.ds(pl.multiple_of((1 - c) * requests, requests), requests), home]
    for k, block_ref in enumerate(block_refs):
        for block, table in enumerate((first_table, second_table)):
            start = pl.multiple_of((z + k) % 4 * (2 * CAP), 2 * CAP)
            chosen = dot(
                table[pl.ds(start, 2 * CAP), :],
                held[block * requests : (block + 1) * requests],
                ((1,), (0,)),
            ).astype(bf16)
            for parity in range(2):
                at = parity * 2 * CAP + block * CAP
                block_ref[at : at + CAP] = chosen[parity * CAP : (parity + 1) * CAP]


def make_stream(parts, own_residual, got, tables):
    rows, span = parts[0].shape
    return pl.pallas_call(
        stream_kernel,
        name="make_stream",
        in_specs=[VMEM] * 8,
        out_specs=[VMEM] * 6,
        out_shape=[jax.ShapeDtypeStruct((rows // 2, span // 4), bf16)] * 2
        + [pltpu.VMEM((4 * CAP, span), bf16)] * 4,
        scratch_shapes=[pltpu.VMEM((rows, span), bf16)],
        compiler_params=pltpu.CompilerParams(vmem_limit_bytes=8 << 20),
    )(*parts, own_residual, got, *tables)


def plus_kernel(*refs):
    total = refs[0][...].astype(f32)
    for part in refs[1:-1]:
        total = total + part[...].astype(f32)
    refs[-1][...] = total.astype(bf16)


def plus(parts):
    return pl.pallas_call(
        plus_kernel,
        name="plus",
        in_specs=[VMEM] * len(parts),
        out_specs=VMEM,
        out_shape=jax.ShapeDtypeStruct(parts[0].shape, bf16),
        compiler_params=pltpu.CompilerParams(vmem_limit_bytes=8 << 20),
    )(*parts)


def load_kernel(source, target, sems):
    rows = target.shape[0]
    count = sems.shape[0]
    step = rows // count // 16 * 16
    copies = []
    for c in range(count):
        at = pl.ds(c * step, step if c < count - 1 else rows - step * (count - 1))
        copies.append(pltpu.make_async_copy(source.at[at], target.at[at], sems.at[c]))
    for copy in copies:
        copy.start()
    for copy in copies:
        copy.wait()


def load_weight(weight):
    return pl.pallas_call(
        load_kernel,
        name="load_weight",
        in_specs=[ANY],
        out_specs=VMEM,
        out_shape=pltpu.VMEM(weight.shape, bf16),
        scratch_shapes=[pltpu.SemaphoreType.DMA((4,))],
        cost_estimate=pl.CostEstimate(
            flops=0, bytes_accessed=4 * weight.size, transcendentals=0
        ),
        compiler_params=pltpu.CompilerParams(vmem_limit_bytes=49 << 20),
    )(weight)


def prepare_kernel(*refs):
    kept, gain_ref, out_ref = refs[:4], refs[4], refs[6]
    span = kept[0].shape[1]
    half = span // 4
    rows = EXPERTS * CAP
    c = core_at()
    ones = jnp.ones((STATS, span), bf16)
    line = lax.broadcasted_iota(jnp.int32, (STATS, rows), 0)
    gain = jnp.concatenate(
        [gain_ref[:, half_lanes(c, j, 0, 2 * half)] for j in range(4)], axis=1
    ).astype(f32)
    for i in range(2):
        start = pl.multiple_of((c + i) % 2 * (2 * CAP), 2 * CAP)
        x = jnp.concatenate([part[pl.ds(start, 2 * CAP), :] for part in kept], axis=0)
        wide = x.astype(f32)
        out_ref[i, :span] = (wide * gain).T.astype(bf16)
        squares = wide * wide
        coarse = squares.astype(bf16)
        fine = (squares - coarse.astype(f32)).astype(bf16)
        sums = dot(ones, coarse, ((1,), (1,))) + dot(ones, fine, ((1,), (1,)))
        high = sums.astype(bf16).astype(f32)
        stats = jnp.where(line == 0, high, jnp.where(line == 1, sums - high, 0.0))
        out_ref[i, span:] = stats.astype(bf16)


def prepare(kept, gain, after):
    span = kept[0].shape[1]
    return pl.pallas_call(
        prepare_kernel,
        name="prepare",
        in_specs=[VMEM] * 6,
        out_specs=VMEM,
        out_shape=pltpu.VMEM((2, span + STATS, EXPERTS * CAP), bf16),
        compiler_params=pltpu.CompilerParams(vmem_limit_bytes=8 << 20),
    )(*kept, gain[None, :], after)


def partial_products(k, own_ref, got_ref, gate_w, up_w):
    span = own_ref.shape[1] - STATS
    half = span // 4
    c = core_at()
    gate = up = None
    for x, h in ((own_ref[0, :span], c), (got_ref[:span], 1 - c)):
        lanes = [half_lanes(h, j, 4 - k, 2 * half) for j in range(4)]
        part = dot(jnp.concatenate([gate_w[:, at] for at in lanes], axis=1), x, ((1,), (0,)))
        gate = part if gate is None else gate + part
        part = dot(jnp.concatenate([up_w[:, at] for at in lanes], axis=1), x, ((1,), (0,)))
        up = part if up is None else up + part
    stats = own_ref[0, span:].astype(f32) + got_ref[span:].astype(f32)
    return gate, up, jnp.sum(stats, axis=0, keepdims=True)


def begin_kernel(first_ref, second_ref, gate_w, up_w, gate_ref, up_ref, squares_ref):
    gate_ref[...], up_ref[...], squares_ref[...] = partial_products(
        0, first_ref, second_ref, gate_w, up_w
    )


def go_on_kernel(
    k, first_ref, second_ref, gate_w, up_w, gate_in, up_in, squares_in, gate_ref, up_ref, squares_ref
):
    gate, up, squares = partial_products(k, first_ref, second_ref, gate_w, up_w)
    gate_ref[...] = gate_in[...] + gate
    up_ref[...] = up_in[...] + up
    squares_ref[...] = squares_in[...] + squares


def finish_kernel(
    k, first_ref, second_ref, gate_w, up_w, gate_in, up_in, squares_in, down_w, *out_refs
):
    first_outs, second_outs = out_refs[:4], out_refs[4:]
    _, rows, piece = first_outs[0].shape
    gate, up, squares = partial_products(k, first_ref, second_ref, gate_w, up_w)
    squares = squares + squares_in[...]
    factor = lax.rsqrt(squares * (1.0 / (16 * piece)) + epsilon)
    gate = (gate + gate_in[...]) * factor
    up = (up + up_in[...]) * factor
    inner = (gate / (1.0 + jnp.exp(-gate)) * up).astype(bf16)
    hidden = lax.axis_index("hidden")
    for kx in range(4):
        for ky in range(4):
            owner = (hidden // 4 + kx) % 4 * 4 + (hidden % 4 + ky) % 4
            weight = down_w[:, pl.ds(pl.multiple_of(owner * piece, piece), piece)]
            part = dot(inner, weight, ((0,), (0,))).astype(bf16)
            first_outs[kx][ky] = part[:rows]
            second_outs[ky][kx] = part[rows:]


def run_expert(firsts, seconds, gate_w, up_w, down_w):
    _, lines, rows = firsts[0].shape
    half = (lines - STATS) // 4
    hidden, _ = down_w.shape
    cost = pl.CostEstimate(
        flops=16 * hidden * 4 * half * rows, bytes_accessed=1 << 22, transcendentals=0
    )
    params = pltpu.CompilerParams(vmem_limit_bytes=16 << 20)
    sums = [jax.ShapeDtypeStruct((hidden, rows), f32)] * 2 + [jax.ShapeDtypeStruct((1, rows), f32)]
    state = pl.pallas_call(
        begin_kernel,
        name="expert_begin",
        in_specs=[VMEM] * 4,
        out_specs=[VMEM] * 3,
        out_shape=sums,
        cost_estimate=cost,
        compiler_params=params,
    )(firsts[0], seconds[0], gate_w, up_w)
    for i in (1, 2):
        state = pl.pallas_call(
            functools.partial(go_on_kernel, STEPS[i]),
            name="expert_go_on",
            in_specs=[VMEM] * 7,
            out_specs=[VMEM] * 3,
            out_shape=sums,
            cost_estimate=cost,
            input_output_aliases={4: 0, 5: 1, 6: 2},
            compiler_params=params,
        )(firsts[i], seconds[i], gate_w, up_w, *state)
    return pl.pallas_call(
        functools.partial(finish_kernel, STEPS[3]),
        name="expert_finish",
        in_specs=[VMEM] * 8,
        out_specs=[VMEM] * 8,
        out_shape=[jax.ShapeDtypeStruct((4, rows // 2, 2 * half), bf16)] * 8,
        cost_estimate=cost,
        compiler_params=params,
    )(firsts[3], seconds[3], gate_w, up_w, *state, down_w)


def add_kernel(*refs):
    parts, out_refs = refs[:4], refs[4:]
    for j, out_ref in enumerate(out_refs):
        total = parts[0][j].astype(f32)
        for part in parts[1:]:
            total = total + part[j].astype(f32)
        out_ref[...] = total.astype(bf16)


def add_parts(parts):
    count, rows, piece = parts[0].shape
    return list(pl.pallas_call(
        add_kernel,
        name="add_parts",
        in_specs=[VMEM] * 4,
        out_specs=[VMEM] * count,
        out_shape=[jax.ShapeDtypeStruct((rows, piece), bf16)] * count,
        compiler_params=pltpu.CompilerParams(vmem_limit_bytes=8 << 20),
    )(*parts))


def total_kernel(*refs):
    out_ref = refs[8]
    place = lax.axis_index("expert")
    for h in range(2):
        total = refs[h * 4][...].astype(f32)
        for part in refs[h * 4 + 1 : h * 4 + 4]:
            total = total + part[...].astype(f32)
        total = total.astype(bf16)
        for i in range(4):
            block = (place // 2 + 4 - (h * 2 + i // 2)) % 4 * 2 + i % 2
            out_ref[block] = total[i * CAP : (i + 1) * CAP]


def total_parts(firsts, seconds):
    piece = firsts[0].shape[1]
    return pl.pallas_call(
        total_kernel,
        name="total_parts",
        in_specs=[VMEM] * 8,
        out_specs=VMEM,
        out_shape=jax.ShapeDtypeStruct((EXPERTS, CAP, piece), bf16),
        compiler_params=pltpu.CompilerParams(vmem_limit_bytes=8 << 20),
    )(*firsts, *seconds)


def combine_kernel(own_ref, other_ref, returned_ref, first_table, second_table, out_ref):
    first = core_at() == 0
    half = own_ref.shape[1]
    own, other = own_ref[...].astype(f32), other_ref[...].astype(f32)
    table = jnp.where(
        first, first_table[...].astype(f32), second_table[...].astype(f32)
    ).astype(bf16)
    mixed = 0.5 * dot(table, returned_ref[...], ((0,), (0,)))
    out_ref[:, :half] = (jnp.where(first, own, other) + mixed[:, :half]).astype(bf16)
    out_ref[:, half:] = (jnp.where(first, other, own) + mixed[:, half:]).astype(bf16)


def combine(own, other, returned, tables):
    return pl.pallas_call(
        combine_kernel,
        name="combine",
        in_specs=[VMEM] * 5,
        out_specs=VMEM,
        out_shape=jax.ShapeDtypeStruct((own.shape[0], returned.shape[1]), bf16),
        compiler_params=pltpu.CompilerParams(vmem_limit_bytes=8 << 20),
    )(own, other, returned, *tables)


def swapped(parts, axis):
    return lax.all_to_all(parts, axis, 0, 0, tiled=True)


def along_expert(blocks):
    kept = [blocks[0]] + [None] * 3
    for k in STEPS[1:]:
        pairs = [(z * 2 + c, (z + k) % 4 * 2 + c) for z in range(4) for c in range(2)]
        kept[k] = lax.ppermute(blocks[k], "expert", pairs)
    return kept


def to_partner(array):
    pairs = [(z * 2 + c, z * 2 + 1 - c) for z in range(4) for c in range(2)]
    return lax.ppermute(array, "expert", pairs)


def split_shift(array, k, x_core):
    pairs = []
    for place in range(128):
        c, x, y = place // 16 % 2, place // 4 % 4, place % 4
        x, y = ((x + k) % 4, y) if c == x_core else (x, (y + k) % 4)
        pairs.append((place, place // 16 * 16 + x * 4 + y))
    return lax.ppermute(array, ("expert", "hidden"), pairs)


def shifted(array, dx, dy):
    pairs = [
        (x * 4 + y, (x + dx) % 4 * 4 + (y + dy) % 4) for x in range(4) for y in range(4)
    ]
    return lax.ppermute(array, "hidden", pairs)


def per_device(
    queries, new_key, new_value, key_cache, value_cache, cache_lengths, residual,
    out_weight, norm_gain, expert_ids, gate_weight, up_weight, down_weight,
):
    hidden_count = lax.axis_size("hidden")
    columns = out_weight.shape[1] // hidden_count
    ids = expert_ids.T
    attended, given, own_residual, w_half = attend(
        queries, new_key, new_value, key_cache, value_cache, cache_lengths,
        out_weight, residual, ids,
    )
    got = to_partner(given)
    tables = tables_of(ids, got)
    parts = project(attended, got, w_half)
    gate_w = load_weight(gate_weight[0].T)
    arrived = parts[:1]
    for k in STEPS[1:]:
        arrived.append(split_shift(parts[k], k, 1))
    part = plus(arrived)
    up_w = load_weight(up_weight[0].T)
    parts = [part]
    for k in STEPS[1:]:
        parts.append(split_shift(part, k, 0))
    own_stream, given, *blocks = make_stream(parts, own_residual, got, tables)
    kept = along_expert(blocks)
    other_stream = to_partner(given)
    piece = prepare(kept, norm_gain, other_stream)
    pieces = [piece] + [split_shift(piece, k, 1) for k in STEPS[1:]]
    gots = [to_partner(piece[1]) for piece in pieces]
    parts = list(run_expert(pieces, gots, gate_w, up_w, down_weight[0]))
    firsts = add_parts(parts[:1] + [shifted(parts[k], k, 0) for k in STEPS[1:]])
    seconds = add_parts(parts[4:5] + [shifted(parts[4 + k], 0, k) for k in STEPS[1:]])
    firsts = firsts[:1] + [shifted(firsts[k], 0, k) for k in STEPS[1:]]
    seconds = seconds[:1] + [shifted(seconds[k], k, 0) for k in STEPS[1:]]
    returned = swapped(total_parts(firsts, seconds), "expert")
    return combine(
        own_stream, other_stream, returned.reshape(EXPERTS * CAP, columns), tables
    )


def solution(mesh):
    return jax.shard_map(
        per_device,
        mesh=mesh,
        in_specs=(
            P("expert", "hidden"),
            P("expert", "hidden"),
            P("expert", "hidden"),
            P("expert", "hidden", None, None),
            P("expert", "hidden", None, None),
            P("expert"),
            P("expert", None),
            P("hidden", None),
            P(),
            P("expert", None),
            P("expert", None, "hidden"),
            P("expert", None, "hidden"),
            P("expert", "hidden", None),
        ),
        out_specs=P("expert", "hidden"),
        check_vma=False,
    )
```

time: 114 us -> 112 us (0.982)
  blocking collectives: 18.5 us -> 12.7 us
  waiting for transfers between devices: 29 us -> 34.5 us
  local copies, waits for them, and re-layouts: 2.24 us -> 0.85 us
  starting transfers between devices: 45.2 us -> 44 us
    ppermute x4 -> x15, starting transfers between devices: 5.81 us -> 26.2 us  [the longest x6 15.4 us: to_partner(): return lax.ppermute(array, 'expert', pairs)]
    ppermute x4 -> x15, waiting for transfers between devices: 0.01 us -> 16.2 us  [the longest x9 14.3 us: split_shift(): return lax.ppermute(array, ('expert', 'hidden'), pairs)]
    ppermute x24 -> x12, starting transfers between devices: 26.1 us -> 12.7 us  [shifted(): return lax.ppermute(array, 'hidden', pairs)]
    all_to_all x1 -> x0, waiting for transfers between devices: 10.3 us -> none  [swapped(): return lax.all_to_all(parts, axis, 0, 0, tiled=True)]
    all_to_all x1 -> x0, starting transfers between devices: 7.58 us -> none  [swapped(): return lax.all_to_all(parts, axis, 0, 0, tiled=True)]
    all_to_all x1, blocking collectives: 18.5 us -> 12.7 us  [swapped(): return lax.all_to_all(parts, axis, 0, 0, tiled=True)]
    unnamed x24 -> x8, local copies, waits for them, and re-layouts: 2.19 us -> 0.76 us
    pallas_call x5 -> x9, Pallas kernels: 12.2 us -> 13.3 us  [the longest x1 5.6 us: attend(): pl.pallas_call(attend_kernel, name='attend', in_specs=[ANY] * 9, out_spec...]
  transfers between devices with their start and end apart: 32 -> 30, of which waited for: 12 -> 15; matrix products, arithmetic and copies ran while one was open for 0% -> 0% of each run, Pallas kernels for 7% -> 8%
where the time goes in v3:
time: 112 us
  starting transfers between devices  44 us (39%)
  waiting for transfers between devices  34.5 us (31%)
  Pallas kernels  19.5 us (17%)
  blocking collectives  12.7 us (11%)
    ppermute x12, waiting for transfers between devices, shifted(): return lax.ppermute(array, 'hidden', pairs)  18.3 us
    ppermute x6, starting transfers between devices, to_partner(): return lax.ppermute(array, 'expert', pairs)  15.4 us
    ppermute x9, waiting for transfers between devices, split_shift(): return lax.ppermute(array, ('expert', 'hidden'), pairs)  14.3 us
    all_to_all x1, blocking collectives, swapped(): return lax.all_to_all(parts, axis, 0, 0, tiled=True)  12.7 us
    ppermute x12, starting transfers between devices, shifted(): return lax.ppermute(array, 'hidden', pairs)  12.7 us
    ppermute x9, starting transfers between devices, split_shift(): return lax.ppermute(array, ('expert', 'hidden'), pairs)  10.9 us
    pallas_call x1, Pallas kernels, attend(): pl.pallas_call(attend_kernel, name='attend', in_specs=[ANY] * 9, out_spec...  5.6 us
    pallas_call x2, Pallas kernels, load_weight(): pl.pallas_call(load_kernel, name='load_weight', in_specs=[ANY], out_specs...  5.36 us
  transfers between devices with their start and end apart: 30, of which 15 were waited for; matrix products, arithmetic and copies ran while one was open for 0% of the time, Pallas kernels for 8%

profile of v3, /device:TPU:1, one launch (start us, length us, event | category | flops | bytes accessed | tf_op | source)
XLA Modules:
  0.0 111.9 jit_solution(13370740893541481542)
XLA Ops:
  0.0 5.6 %attend.1 = (bf16[64,256]{1,0:T(8,128)(2,1)S(1)}, bf16[80,768]{1,0:T(8,128)(2,1)S(1)}, bf16[64,512]{1,0:T(8,128)(2,1)S(1)}, bf16[256,2048]{1,0:T(8,128)(2,1)S(1)}) custom-call(s32[1,64]{1,0:T(1,128)} %bitcast.26, bf16[64,256]{1,0:T(8,128)(2,1)} %q_hbm.1, bf16[64,256]{1,0:T(8,128)(2,1)} %nk_hbm.1, bf16[64,256]{1,0:T(8,128)(2,1)} %nv_hbm.1, ...), custom_call_target="tpu_custom_call" | custom-call | tf_op jit(solution)/shard_map/attend/pallas_call | solution.py:143
  5.6 1.5 %collective-permute-start = (bf16[80,768]{1,0:T(8,128)(2,1)S(1)}, bf16[80,768]{1,0:T(8,128)(2,1)S(1)}, u32[]{:S(2)}, u32[]{:S(2)}) collective-permute-start(bf16[80,768]{1,0:T(8,128)(2,1)S(1)} %get-tuple-element.47), channel_id=1, source_target_pairs={{0,16},{16,0},{32,48},{48,32},{64,80},{80,64},{96,112},{112,96},{1... | collective-permute-start | bytes 368648 | tf_op jit(solution)/shard_map/ppermute | solution.py:552
  8.5 1.4 %collective-permute-start.1 = (bf16[128,512]{1,0:T(8,128)(2,1)S(1)}, bf16[128,512]{1,0:T(8,128)(2,1)S(1)}, u32[]{:S(2)}, u32[]{:S(2)}) collective-permute-start(bf16[128,512]{1,0:T(8,128)(2,1)S(1)} %get-tuple-element.50), channel_id=1, source_target_pairs={{0,1},{1,2},{2,3},{3,0},{4,5},{5,6},{6,7},{7,4},{8,9},{9,10},{10,1... | collective-permute-start | bytes 393224 | tf_op jit(solution)/shard_map/ppermute | solution.py:561
  9.9 1.4 %collective-permute-start.2 = (bf16[128,512]{1,0:T(8,128)(2,1)S(1)}, bf16[128,512]{1,0:T(8,128)(2,1)S(1)}, u32[]{:S(2)}, u32[]{:S(2)}) collective-permute-start(bf16[128,512]{1,0:T(8,128)(2,1)S(1)} %get-tuple-element.51), channel_id=1, source_target_pairs={{0,3},{1,0},{2,1},{3,2},{4,7},{5,4},{6,5},{7,6},{8,11},{9,8},{10,9... | collective-permute-start | bytes 393224 | tf_op jit(solution)/shard_map/ppermute | solution.py:561
  11.3 1.6 %collective-permute-start.3 = (bf16[128,512]{1,0:T(8,128)(2,1)S(1)}, bf16[128,512]{1,0:T(8,128)(2,1)S(1)}, u32[]{:S(2)}, u32[]{:S(2)}) collective-permute-start(bf16[128,512]{1,0:T(8,128)(2,1)S(1)} %get-tuple-element.52), channel_id=1, source_target_pairs={{0,2},{1,3},{2,0},{3,1},{4,6},{5,7},{6,4},{7,5},{8,10},{9,11},{10,... | collective-permute-start | bytes 393224 | tf_op jit(solution)/shard_map/ppermute | solution.py:561
  14.1 2.9 %collective-permute-done.3.refs_3_ = bf16[128,512]{1,0:T(8,128)(2,1)S(1)} collective-permute-done((bf16[128,512]{1,0:T(8,128)(2,1)S(1)}, bf16[128,512]{1,0:T(8,128)(2,1)S(1)}, u32[]{:S(2)}, u32[]{:S(2)}) %collective-permute-start.3) | collective-permute-done | bytes 131104 | tf_op jit(solution)/shard_map/ppermute | solution.py:561
  17.0 1.2 %collective-permute-start.4 = (bf16[128,512]{1,0:T(8,128)(2,1)S(1)}, bf16[128,512]{1,0:T(8,128)(2,1)S(1)}, u32[]{:S(2)}, u32[]{:S(2)}) collective-permute-start(bf16[128,512]{1,0:T(8,128)(2,1)S(1)} %plus.1.refs_0_), channel_id=1, source_target_pairs={{0,4},{1,5},{2,6},{3,7},{4,8},{5,9},{6,10},{7,11},{8,12},{9,13},{1... | collective-permute-start | bytes 393224 | tf_op jit(solution)/shard_map/ppermute | solution.py:561
  18.2 1.8 %collective-permute-start.5 = (bf16[128,512]{1,0:T(8,128)(2,1)S(1)}, bf16[128,512]{1,0:T(8,128)(2,1)S(1)}, u32[]{:S(2)}, u32[]{:S(2)}) collective-permute-start(bf16[128,512]{1,0:T(8,128)(2,1)S(1)} %plus.1.refs_0_), channel_id=1, source_target_pairs={{0,12},{1,13},{2,14},{3,15},{4,0},{5,1},{6,2},{7,3},{8,4},{9,5},{1... | collective-permute-start | bytes 393224 | tf_op jit(solution)/shard_map/ppermute | solution.py:561
  20.0 1.3 %collective-permute-start.6 = (bf16[128,512]{1,0:T(8,128)(2,1)S(1)}, bf16[128,512]{1,0:T(8,128)(2,1)S(1)}, u32[]{:S(2)}, u32[]{:S(2)}) collective-permute-start(bf16[128,512]{1,0:T(8,128)(2,1)S(1)} %plus.1.refs_0_), channel_id=1, source_target_pairs={{0,8},{1,9},{2,10},{3,11},{4,12},{5,13},{6,14},{7,15},{8,0},{9,1},... | collective-permute-start | bytes 393224 | tf_op jit(solution)/shard_map/ppermute | solution.py:561
  22.3 3.0 %collective-permute-done.6.refs_3_ = bf16[128,512]{1,0:T(8,128)(2,1)S(1)} collective-permute-done((bf16[128,512]{1,0:T(8,128)(2,1)S(1)}, bf16[128,512]{1,0:T(8,128)(2,1)S(1)}, u32[]{:S(2)}, u32[]{:S(2)}) %collective-permute-start.6) | collective-permute-done | bytes 131104 | tf_op jit(solution)/shard_map/ppermute | solution.py:561
  25.7 3.8 %collective-permute-start.10 = (bf16[128,512]{1,0:T(8,128)(2,1)S(1)}, bf16[128,512]{1,0:T(8,128)(2,1)S(1)}, u32[]{:S(2)}, u32[]{:S(2)}) collective-permute-start(bf16[128,512]{1,0:T(8,128)(2,1)S(1)} %get-tuple-element.61), channel_id=1, source_target_pairs={{0,96},{16,112},{32,0},{48,16},{64,32},{80,48},{96,64},{112,80},{1... | collective-permute-start | bytes 393224 | tf_op jit(solution)/shard_map/ppermute | solution.py:546
  29.5 1.3 %collective-permute-start.9 = (bf16[128,512]{1,0:T(8,128)(2,1)S(1)}, bf16[128,512]{1,0:T(8,128)(2,1)S(1)}, u32[]{:S(2)}, u32[]{:S(2)}) collective-permute-start(bf16[128,512]{1,0:T(8,128)(2,1)S(1)} %get-tuple-element.60), channel_id=1, source_target_pairs={{0,64},{16,80},{32,96},{48,112},{64,0},{80,16},{96,32},{112,48},{1... | collective-permute-start | bytes 393224 | tf_op jit(solution)/shard_map/ppermute | solution.py:546
  30.8 4.2 %collective-permute-start.7 = (bf16[64,128]{1,0:T(8,128)(2,1)S(1)}, bf16[64,128]{1,0:T(8,128)(2,1)S(1)}, u32[]{:S(2)}, u32[]{:S(2)}) collective-permute-start(bf16[64,128]{1,0:T(8,128)(2,1)S(1)} %get-tuple-element.57), channel_id=1, source_target_pairs={{0,16},{16,0},{32,48},{48,32},{64,80},{80,64},{96,112},{112,96},{1... | collective-permute-start | bytes 49160 | tf_op jit(solution)/shard_map/ppermute | solution.py:552
  36.7 5.1 %collective-permute-start.17 = (bf16[528,256]{1,0:T(8,128)(2,1)S(1)}, bf16[528,256]{1,0:T(8,128)(2,1)S(1)}, u32[]{:S(2)}, u32[]{:S(2)}) collective-permute-start(bf16[528,256]{1,0:T(8,128)(2,1)S(1)} %slice_bitcast_fusion), channel_id=1, source_target_pairs={{0,16},{16,0},{32,48},{48,32},{64,80},{80,64},{96,112},{112,96},{1... | collective-permute-start | bytes 811016 | tf_op jit(solution)/shard_map/ppermute | solution.py:552
  41.9 1.3 %collective-permute-start.13 = (bf16[2,528,256]{2,1,0:T(8,128)(2,1)S(1)}, bf16[2,528,256]{2,1,0:T(8,128)(2,1)S(1)}, u32[]{:S(2)}, u32[]{:S(2)}) collective-permute-start(bf16[2,528,256]{2,1,0:T(8,128)(2,1)S(1)} %prepare.1.first_ref), channel_id=1, source_target_pairs={{0,3},{1,0},{2,1},{3,2},{4,7},{5,4},{6,5},{7,6},{8,11},{9,8},{10,9... | collective-permute-start | bytes 1622024 | tf_op jit(solution)/shard_map/ppermute | solution.py:561
  43.1 2.7 %load_weight.2.gate_w = bf16[688,4096]{1,0:T(8,128)(2,1)S(1)} custom-call(bf16[688,4096]{1,0:T(8,128)(2,1)} %bitcast.24), custom_call_target="tpu_custom_call" | custom-call | bytes 11272192 | tf_op jit(solution)/shard_map/load_weight/pallas_call | solution.py:327
  45.8 2.7 %load_weight.3.up_w = bf16[688,4096]{1,0:T(8,128)(2,1)S(1)} custom-call(bf16[688,4096]{1,0:T(8,128)(2,1)} %bitcast.25), custom_call_target="tpu_custom_call" | custom-call | bytes 11272192 | tf_op jit(solution)/shard_map/load_weight/pallas_call | solution.py:327
  50.1 1.9 %collective-permute-start.16 = (bf16[528,256]{1,0:T(8,128)(2,1)S(1)}, bf16[528,256]{1,0:T(8,128)(2,1)S(1)}, u32[]{:S(2)}, u32[]{:S(2)}) collective-permute-start(bf16[528,256]{1,0:T(8,128)(2,1)S(1)} %slice_bitcast_fusion.1), channel_id=1, source_target_pairs={{0,16},{16,0},{32,48},{48,32},{64,80},{80,64},{96,112},{112,96},{1... | collective-permute-start | bytes 811016 | tf_op jit(solution)/shard_map/ppermute | solution.py:552
  52.1 6.5 %collective-permute-done.11.first_ref = bf16[2,528,256]{2,1,0:T(8,128)(2,1)S(1)} collective-permute-done((bf16[2,528,256]{2,1,0:T(8,128)(2,1)S(1)}, bf16[2,528,256]{2,1,0:T(8,128)(2,1)S(1)}, u32[]{:S(2)}, u32[]{:S(2)}) %collective-permute-start.11) | collective-permute-done | bytes 540704 | tf_op jit(solution)/shard_map/ppermute | solution.py:561
  58.6 2.6 %collective-permute-start.12 = (bf16[528,256]{1,0:T(8,128)(2,1)S(1)}, bf16[528,256]{1,0:T(8,128)(2,1)S(1)}, u32[]{:S(2)}, u32[]{:S(2)}) collective-permute-start(bf16[528,256]{1,0:T(8,128)(2,1)S(1)} %slice_bitcast_fusion.3), channel_id=1, source_target_pairs={{0,16},{16,0},{32,48},{48,32},{64,80},{80,64},{96,112},{112,96},{1... | collective-permute-start | bytes 811016 | tf_op jit(solution)/shard_map/ppermute | solution.py:552
  62.3 1.0 expert_go_on.3
  64.1 2.9 %expert_finish.1 = (bf16[4,128,256]{2,1,0:T(8,128)(2,1)S(1)}, bf16[4,128,256]{2,1,0:T(8,128)(2,1)S(1)}, bf16[4,128,256]{2,1,0:T(8,128)(2,1)S(1)}, bf16[4,128,256...) custom-call(bf16[2,528,256]{2,1,0:T(8,128)(2,1)S(1)} %collective-per, ...), custom_call_target="tpu_custom_call" | custom-call | flops 1442840576 | bytes 4194304 | tf_op jit(solution)/shard_map/expert_finish/pallas_call | solution.py:458
  67.0 2.7 %collective-permute-start.25 = (bf16[4,128,256]{2,1,0:T(8,128)(2,1)S(1)}, bf16[4,128,256]{2,1,0:T(8,128)(2,1)S(1)}, u32[]{:S(2)}, u32[]{:S(2)}) collective-permute-start(bf16[4,128,256]{2,1,0:T(8,128)(2,1)S(1)} %get-tuple-element.81), channel_id=1, source_target_pairs={{0,3},{1,0},{2,1},{3,2},{4,7},{5,4},{6,5},{7,6},{8,11},{9,8},{10,9... | collective-permute-start | bytes 786440 | tf_op jit(solution)/shard_map/ppermute | solution.py:568
  69.7 2.7 %collective-permute-start.19 = (bf16[4,128,256]{2,1,0:T(8,128)(2,1)S(1)}, bf16[4,128,256]{2,1,0:T(8,128)(2,1)S(1)}, u32[]{:S(2)}, u32[]{:S(2)}) collective-permute-start(bf16[4,128,256]{2,1,0:T(8,128)(2,1)S(1)} %get-tuple-element.73), channel_id=1, source_target_pairs={{0,12},{1,13},{2,14},{3,15},{4,0},{5,1},{6,2},{7,3},{8,4},{9,5},{1... | collective-permute-start | bytes 786440 | tf_op jit(solution)/shard_map/ppermute | solution.py:568
  72.4 9.3 %collective-permute-done.24.refs_1_ = bf16[4,128,256]{2,1,0:T(8,128)(2,1)S(1)} collective-permute-done((bf16[4,128,256]{2,1,0:T(8,128)(2,1)S(1)}, bf16[4,128,256]{2,1,0:T(8,128)(2,1)S(1)}, u32[]{:S(2)}, u32[]{:S(2)}) %collective-permute-start.24) | collective-permute-done | bytes 262176 | tf_op jit(solution)/shard_map/ppermute | solution.py:568
  81.7 1.5 %collective-permute-start.20 = (bf16[4,128,256]{2,1,0:T(8,128)(2,1)S(1)}, bf16[4,128,256]{2,1,0:T(8,128)(2,1)S(1)}, u32[]{:S(2)}, u32[]{:S(2)}) collective-permute-start(bf16[4,128,256]{2,1,0:T(8,128)(2,1)S(1)} %get-tuple-element.74), channel_id=1, source_target_pairs={{0,8},{1,9},{2,10},{3,11},{4,12},{5,13},{6,14},{7,15},{8,0},{9,1},... | collective-permute-start | bytes 786440 | tf_op jit(solution)/shard_map/ppermute | solution.py:568
  83.8 2.4 %collective-permute-start.28 = (bf16[128,256]{1,0:T(8,128)(2,1)S(1)}, bf16[128,256]{1,0:T(8,128)(2,1)S(1)}, u32[]{:S(2)}, u32[]{:S(2)}) collective-permute-start(bf16[128,256]{1,0:T(8,128)(2,1)S(1)} %get-tuple-element.85), channel_id=1, source_target_pairs={{0,12},{1,13},{2,14},{3,15},{4,0},{5,1},{6,2},{7,3},{8,4},{9,5},{1... | collective-permute-start | bytes 196616 | tf_op jit(solution)/shard_map/ppermute | solution.py:568
  86.4 3.9 %collective-permute-done.20.refs_3_ = bf16[4,128,256]{2,1,0:T(8,128)(2,1)S(1)} collective-permute-done((bf16[4,128,256]{2,1,0:T(8,128)(2,1)S(1)}, bf16[4,128,256]{2,1,0:T(8,128)(2,1)S(1)}, u32[]{:S(2)}, u32[]{:S(2)}) %collective-permute-start.20) | collective-permute-done | bytes 262176 | tf_op jit(solution)/shard_map/ppermute | solution.py:568
  90.5 2.7 %collective-permute-start.22 = (bf16[128,256]{1,0:T(8,128)(2,1)S(1)}, bf16[128,256]{1,0:T(8,128)(2,1)S(1)}, u32[]{:S(2)}, u32[]{:S(2)}) collective-permute-start(bf16[128,256]{1,0:T(8,128)(2,1)S(1)} %get-tuple-element.77), channel_id=1, source_target_pairs={{0,3},{1,0},{2,1},{3,2},{4,7},{5,4},{6,5},{7,6},{8,11},{9,8},{10,9... | collective-permute-start | bytes 196616 | tf_op jit(solution)/shard_map/ppermute | solution.py:568
  93.6 1.2 %collective-permute-done.21.refs_1_ = bf16[128,256]{1,0:T(8,128)(2,1)S(1)} collective-permute-done((bf16[128,256]{1,0:T(8,128)(2,1)S(1)}, bf16[128,256]{1,0:T(8,128)(2,1)S(1)}, u32[]{:S(2)}, u32[]{:S(2)}) %collective-permute-start.21) | collective-permute-done | bytes 65568 | tf_op jit(solution)/shard_map/ppermute | solution.py:568
  95.0 3.2 %collective-permute-done.23.refs_3_ = bf16[128,256]{1,0:T(8,128)(2,1)S(1)} collective-permute-done((bf16[128,256]{1,0:T(8,128)(2,1)S(1)}, bf16[128,256]{1,0:T(8,128)(2,1)S(1)}, u32[]{:S(2)}, u32[]{:S(2)}) %collective-permute-start.23) | collective-permute-done | bytes 65568 | tf_op jit(solution)/shard_map/ppermute | solution.py:568
  98.3 12.7 %all_to_all.5 = bf16[8,32,256]{2,1,0:T(8,128)(2,1)S(1)} all-to-all(bf16[8,32,256]{2,1,0:T(8,128)(2,1)S(1)} %total_parts.1), channel_id=1, replica_groups=mesh['expert'=8,'hidden'=16] {'expert'}, dimensions={0} | all-to-all | bytes 262144 | tf_op jit(solution)/shard_map/all_to_all | solution.py:539
  (59 shorter events, 11.9 us)
Async XLA Ops:
  0.0 21.3 %copy-start = (s32[64,2]{0,1:T(2,128)S(1)}, s32[64,2]{0,1:T(2,128)}, u32[]{:S(2)}) copy-start(s32[64,2]{0,1:T(2,128)} %param.22) | copy-start | bytes 1540
  0.0 35.0 %copy-start.1 = (bf16[4096]{0:T(1024)(128)(2,1)S(1)}, bf16[4096]{0:T(1024)(128)(2,1)}, u32[]{:S(2)}) copy-start(bf16[4096]{0:T(1024)(128)(2,1)} %param.21) | copy-start | bytes 24580
  5.6 2.4 %collective-permute-start = (bf16[80,768]{1,0:T(8,128)(2,1)S(1)}, bf16[80,768]{1,0:T(8,128)(2,1)S(1)}, u32[]{:S(2)}, u32[]{:S(2)}) collective-permute-start(bf16[80,768]{1,0:T(8,128)(2,1)S(1)} %get-tuple-element.47), channel_id=1, source_target_pairs={{0,16},{16,0},{32,48},{48,32},{64,80},{80,64},{96,112},{112,96},{1... | collective-permute-start | bytes 368648 | tf_op jit(solution)/shard_map/ppermute | solution.py:552
  8.5 5.4 %collective-permute-start.1 = (bf16[128,512]{1,0:T(8,128)(2,1)S(1)}, bf16[128,512]{1,0:T(8,128)(2,1)S(1)}, u32[]{:S(2)}, u32[]{:S(2)}) collective-permute-start(bf16[128,512]{1,0:T(8,128)(2,1)S(1)} %get-tuple-element.50), channel_id=1, source_target_pairs={{0,1},{1,2},{2,3},{3,0},{4,5},{5,6},{6,7},{7,4},{8,9},{9,10},{10,1... | collective-permute-start | bytes 393224 | tf_op jit(solution)/shard_map/ppermute | solution.py:561
  9.9 4.1 %collective-permute-start.2 = (bf16[128,512]{1,0:T(8,128)(2,1)S(1)}, bf16[128,512]{1,0:T(8,128)(2,1)S(1)}, u32[]{:S(2)}, u32[]{:S(2)}) collective-permute-start(bf16[128,512]{1,0:T(8,128)(2,1)S(1)} %get-tuple-element.51), channel_id=1, source_target_pairs={{0,3},{1,0},{2,1},{3,2},{4,7},{5,4},{6,5},{7,6},{8,11},{9,8},{10,9... | collective-permute-start | bytes 393224 | tf_op jit(solution)/shard_map/ppermute | solution.py:561
  11.3 5.6 %collective-permute-start.3 = (bf16[128,512]{1,0:T(8,128)(2,1)S(1)}, bf16[128,512]{1,0:T(8,128)(2,1)S(1)}, u32[]{:S(2)}, u32[]{:S(2)}) collective-permute-start(bf16[128,512]{1,0:T(8,128)(2,1)S(1)} %get-tuple-element.52), channel_id=1, source_target_pairs={{0,2},{1,3},{2,0},{3,1},{4,6},{5,7},{6,4},{7,5},{8,10},{9,11},{10,... | collective-permute-start | bytes 393224 | tf_op jit(solution)/shard_map/ppermute | solution.py:561
  17.0 5.3 %collective-permute-start.4 = (bf16[128,512]{1,0:T(8,128)(2,1)S(1)}, bf16[128,512]{1,0:T(8,128)(2,1)S(1)}, u32[]{:S(2)}, u32[]{:S(2)}) collective-permute-start(bf16[128,512]{1,0:T(8,128)(2,1)S(1)} %plus.1.refs_0_), channel_id=1, source_target_pairs={{0,4},{1,5},{2,6},{3,7},{4,8},{5,9},{6,10},{7,11},{8,12},{9,13},{1... | collective-permute-start | bytes 393224 | tf_op jit(solution)/shard_map/ppermute | solution.py:561
  18.2 4.1 %collective-permute-start.5 = (bf16[128,512]{1,0:T(8,128)(2,1)S(1)}, bf16[128,512]{1,0:T(8,128)(2,1)S(1)}, u32[]{:S(2)}, u32[]{:S(2)}) collective-permute-start(bf16[128,512]{1,0:T(8,128)(2,1)S(1)} %plus.1.refs_0_), channel_id=1, source_target_pairs={{0,12},{1,13},{2,14},{3,15},{4,0},{5,1},{6,2},{7,3},{8,4},{9,5},{1... | collective-permute-start | bytes 393224 | tf_op jit(solution)/shard_map/ppermute | solution.py:561
  20.0 5.3 %collective-permute-start.6 = (bf16[128,512]{1,0:T(8,128)(2,1)S(1)}, bf16[128,512]{1,0:T(8,128)(2,1)S(1)}, u32[]{:S(2)}, u32[]{:S(2)}) collective-permute-start(bf16[128,512]{1,0:T(8,128)(2,1)S(1)} %plus.1.refs_0_), channel_id=1, source_target_pairs={{0,8},{1,9},{2,10},{3,11},{4,12},{5,13},{6,14},{7,15},{8,0},{9,1},... | collective-permute-start | bytes 393224 | tf_op jit(solution)/shard_map/ppermute | solution.py:561
  25.7 10.2 %collective-permute-start.10 = (bf16[128,512]{1,0:T(8,128)(2,1)S(1)}, bf16[128,512]{1,0:T(8,128)(2,1)S(1)}, u32[]{:S(2)}, u32[]{:S(2)}) collective-permute-start(bf16[128,512]{1,0:T(8,128)(2,1)S(1)} %get-tuple-element.61), channel_id=1, source_target_pairs={{0,96},{16,112},{32,0},{48,16},{64,32},{80,48},{96,64},{112,80},{1... | collective-permute-start | bytes 393224 | tf_op jit(solution)/shard_map/ppermute | solution.py:546
  29.5 6.4 %collective-permute-start.8 = (bf16[128,512]{1,0:T(8,128)(2,1)S(1)}, bf16[128,512]{1,0:T(8,128)(2,1)S(1)}, u32[]{:S(2)}, u32[]{:S(2)}) collective-permute-start(bf16[128,512]{1,0:T(8,128)(2,1)S(1)} %get-tuple-element.59), channel_id=1, source_target_pairs={{0,32},{16,48},{32,64},{48,80},{64,96},{80,112},{96,0},{112,16},{1... | collective-permute-start | bytes 393224 | tf_op jit(solution)/shard_map/ppermute | solution.py:546
  29.5 6.4 %collective-permute-start.9 = (bf16[128,512]{1,0:T(8,128)(2,1)S(1)}, bf16[128,512]{1,0:T(8,128)(2,1)S(1)}, u32[]{:S(2)}, u32[]{:S(2)}) collective-permute-start(bf16[128,512]{1,0:T(8,128)(2,1)S(1)} %get-tuple-element.60), channel_id=1, source_target_pairs={{0,64},{16,80},{32,96},{48,112},{64,0},{80,16},{96,32},{112,48},{1... | collective-permute-start | bytes 393224 | tf_op jit(solution)/shard_map/ppermute | solution.py:546
  30.8 5.0 %collective-permute-start.7 = (bf16[64,128]{1,0:T(8,128)(2,1)S(1)}, bf16[64,128]{1,0:T(8,128)(2,1)S(1)}, u32[]{:S(2)}, u32[]{:S(2)}) collective-permute-start(bf16[64,128]{1,0:T(8,128)(2,1)S(1)} %get-tuple-element.57), channel_id=1, source_target_pairs={{0,16},{16,0},{32,48},{48,32},{64,80},{80,64},{96,112},{112,96},{1... | collective-permute-start | bytes 49160 | tf_op jit(solution)/shard_map/ppermute | solution.py:552
  36.4 13.7 %collective-permute-start.15 = (bf16[2,528,256]{2,1,0:T(8,128)(2,1)S(1)}, bf16[2,528,256]{2,1,0:T(8,128)(2,1)S(1)}, u32[]{:S(2)}, u32[]{:S(2)}) collective-permute-start(bf16[2,528,256]{2,1,0:T(8,128)(2,1)S(1)} %prepare.1.first_ref), channel_id=1, source_target_pairs={{0,1},{1,2},{2,3},{3,0},{4,5},{5,6},{6,7},{7,4},{8,9},{9,10},{10,1... | collective-permute-start | bytes 1622024 | tf_op jit(solution)/shard_map/ppermute | solution.py:561
  36.7 12.4 %collective-permute-start.17 = (bf16[528,256]{1,0:T(8,128)(2,1)S(1)}, bf16[528,256]{1,0:T(8,128)(2,1)S(1)}, u32[]{:S(2)}, u32[]{:S(2)}) collective-permute-start(bf16[528,256]{1,0:T(8,128)(2,1)S(1)} %slice_bitcast_fusion), channel_id=1, source_target_pairs={{0,16},{16,0},{32,48},{48,32},{64,80},{80,64},{96,112},{112,96},{1... | collective-permute-start | bytes 811016 | tf_op jit(solution)/shard_map/ppermute | solution.py:552
  41.9 10.1 %collective-permute-start.13 = (bf16[2,528,256]{2,1,0:T(8,128)(2,1)S(1)}, bf16[2,528,256]{2,1,0:T(8,128)(2,1)S(1)}, u32[]{:S(2)}, u32[]{:S(2)}) collective-permute-start(bf16[2,528,256]{2,1,0:T(8,128)(2,1)S(1)} %prepare.1.first_ref), channel_id=1, source_target_pairs={{0,3},{1,0},{2,1},{3,2},{4,7},{5,4},{6,5},{7,6},{8,11},{9,8},{10,9... | collective-permute-start | bytes 1622024 | tf_op jit(solution)/shard_map/ppermute | solution.py:561
  48.5 10.1 %collective-permute-start.11 = (bf16[2,528,256]{2,1,0:T(8,128)(2,1)S(1)}, bf16[2,528,256]{2,1,0:T(8,128)(2,1)S(1)}, u32[]{:S(2)}, u32[]{:S(2)}) collective-permute-start(bf16[2,528,256]{2,1,0:T(8,128)(2,1)S(1)} %prepare.1.first_ref), channel_id=1, source_target_pairs={{0,2},{1,3},{2,0},{3,1},{4,6},{5,7},{6,4},{7,5},{8,10},{9,11},{10,... | collective-permute-start | bytes 1622024 | tf_op jit(solution)/shard_map/ppermute | solution.py:561
  50.1 11.2 %collective-permute-start.16 = (bf16[528,256]{1,0:T(8,128)(2,1)S(1)}, bf16[528,256]{1,0:T(8,128)(2,1)S(1)}, u32[]{:S(2)}, u32[]{:S(2)}) collective-permute-start(bf16[528,256]{1,0:T(8,128)(2,1)S(1)} %slice_bitcast_fusion.1), channel_id=1, source_target_pairs={{0,16},{16,0},{32,48},{48,32},{64,80},{80,64},{96,112},{112,96},{1... | collective-permute-start | bytes 811016 | tf_op jit(solution)/shard_map/ppermute | solution.py:552
  51.9 10.3 %collective-permute-start.14 = (bf16[528,256]{1,0:T(8,128)(2,1)S(1)}, bf16[528,256]{1,0:T(8,128)(2,1)S(1)}, u32[]{:S(2)}, u32[]{:S(2)}) collective-permute-start(bf16[528,256]{1,0:T(8,128)(2,1)S(1)} %slice_bitcast_fusion.2), channel_id=1, source_target_pairs={{0,16},{16,0},{32,48},{48,32},{64,80},{80,64},{96,112},{112,96},{1... | collective-permute-start | bytes 811016 | tf_op jit(solution)/shard_map/ppermute | solution.py:552
  58.6 4.7 %collective-permute-start.12 = (bf16[528,256]{1,0:T(8,128)(2,1)S(1)}, bf16[528,256]{1,0:T(8,128)(2,1)S(1)}, u32[]{:S(2)}, u32[]{:S(2)}) collective-permute-start(bf16[528,256]{1,0:T(8,128)(2,1)S(1)} %slice_bitcast_fusion.3), channel_id=1, source_target_pairs={{0,16},{16,0},{32,48},{48,32},{64,80},{80,64},{96,112},{112,96},{1... | collective-permute-start | bytes 811016 | tf_op jit(solution)/shard_map/ppermute | solution.py:552
  67.0 14.7 %collective-permute-start.24 = (bf16[4,128,256]{2,1,0:T(8,128)(2,1)S(1)}, bf16[4,128,256]{2,1,0:T(8,128)(2,1)S(1)}, u32[]{:S(2)}, u32[]{:S(2)}) collective-permute-start(bf16[4,128,256]{2,1,0:T(8,128)(2,1)S(1)} %get-tuple-element.80), channel_id=1, source_target_pairs={{0,1},{1,2},{2,3},{3,0},{4,5},{5,6},{6,7},{7,4},{8,9},{9,10},{10,1... | collective-permute-start | bytes 786440 | tf_op jit(solution)/shard_map/ppermute | solution.py:568
  67.0 16.2 %collective-permute-start.25 = (bf16[4,128,256]{2,1,0:T(8,128)(2,1)S(1)}, bf16[4,128,256]{2,1,0:T(8,128)(2,1)S(1)}, u32[]{:S(2)}, u32[]{:S(2)}) collective-permute-start(bf16[4,128,256]{2,1,0:T(8,128)(2,1)S(1)} %get-tuple-element.81), channel_id=1, source_target_pairs={{0,3},{1,0},{2,1},{3,2},{4,7},{5,4},{6,5},{7,6},{8,11},{9,8},{10,9... | collective-permute-start | bytes 786440 | tf_op jit(solution)/shard_map/ppermute | solution.py:568
  69.7 13.5 %collective-permute-start.26 = (bf16[4,128,256]{2,1,0:T(8,128)(2,1)S(1)}, bf16[4,128,256]{2,1,0:T(8,128)(2,1)S(1)}, u32[]{:S(2)}, u32[]{:S(2)}) collective-permute-start(bf16[4,128,256]{2,1,0:T(8,128)(2,1)S(1)} %get-tuple-element.82), channel_id=1, source_target_pairs={{0,2},{1,3},{2,0},{3,1},{4,6},{5,7},{6,4},{7,5},{8,10},{9,11},{10,... | collective-permute-start | bytes 786440 | tf_op jit(solution)/shard_map/ppermute | solution.py:568
  69.7 16.4 %collective-permute-start.18 = (bf16[4,128,256]{2,1,0:T(8,128)(2,1)S(1)}, bf16[4,128,256]{2,1,0:T(8,128)(2,1)S(1)}, u32[]{:S(2)}, u32[]{:S(2)}) collective-permute-start(bf16[4,128,256]{2,1,0:T(8,128)(2,1)S(1)} %get-tuple-element.72), channel_id=1, source_target_pairs={{0,4},{1,5},{2,6},{3,7},{4,8},{5,9},{6,10},{7,11},{8,12},{9,13},{1... | collective-permute-start | bytes 786440 | tf_op jit(solution)/shard_map/ppermute | solution.py:568
  69.7 16.6 %collective-permute-start.19 = (bf16[4,128,256]{2,1,0:T(8,128)(2,1)S(1)}, bf16[4,128,256]{2,1,0:T(8,128)(2,1)S(1)}, u32[]{:S(2)}, u32[]{:S(2)}) collective-permute-start(bf16[4,128,256]{2,1,0:T(8,128)(2,1)S(1)} %get-tuple-element.73), channel_id=1, source_target_pairs={{0,12},{1,13},{2,14},{3,15},{4,0},{5,1},{6,2},{7,3},{8,4},{9,5},{1... | collective-permute-start | bytes 786440 | tf_op jit(solution)/shard_map/ppermute | solution.py:568
  81.7 8.5 %collective-permute-start.20 = (bf16[4,128,256]{2,1,0:T(8,128)(2,1)S(1)}, bf16[4,128,256]{2,1,0:T(8,128)(2,1)S(1)}, u32[]{:S(2)}, u32[]{:S(2)}) collective-permute-start(bf16[4,128,256]{2,1,0:T(8,128)(2,1)S(1)} %get-tuple-element.74), channel_id=1, source_target_pairs={{0,8},{1,9},{2,10},{3,11},{4,12},{5,13},{6,14},{7,15},{8,0},{9,1},... | collective-permute-start | bytes 786440 | tf_op jit(solution)/shard_map/ppermute | solution.py:568
  83.4 10.1 %collective-permute-start.27 = (bf16[128,256]{1,0:T(8,128)(2,1)S(1)}, bf16[128,256]{1,0:T(8,128)(2,1)S(1)}, u32[]{:S(2)}, u32[]{:S(2)}) collective-permute-start(bf16[128,256]{1,0:T(8,128)(2,1)S(1)} %get-tuple-element.84), channel_id=1, source_target_pairs={{0,4},{1,5},{2,6},{3,7},{4,8},{5,9},{6,10},{7,11},{8,12},{9,13},{1... | collective-permute-start | bytes 196616 | tf_op jit(solution)/shard_map/ppermute | solution.py:568
  83.8 9.8 %collective-permute-start.28 = (bf16[128,256]{1,0:T(8,128)(2,1)S(1)}, bf16[128,256]{1,0:T(8,128)(2,1)S(1)}, u32[]{:S(2)}, u32[]{:S(2)}) collective-permute-start(bf16[128,256]{1,0:T(8,128)(2,1)S(1)} %get-tuple-element.85), channel_id=1, source_target_pairs={{0,12},{1,13},{2,14},{3,15},{4,0},{5,1},{6,2},{7,3},{8,4},{9,5},{1... | collective-permute-start | bytes 196616 | tf_op jit(solution)/shard_map/ppermute | solution.py:568
  86.1 7.4 %collective-permute-start.29 = (bf16[128,256]{1,0:T(8,128)(2,1)S(1)}, bf16[128,256]{1,0:T(8,128)(2,1)S(1)}, u32[]{:S(2)}, u32[]{:S(2)}) collective-permute-start(bf16[128,256]{1,0:T(8,128)(2,1)S(1)} %get-tuple-element.86), channel_id=1, source_target_pairs={{0,8},{1,9},{2,10},{3,11},{4,12},{5,13},{6,14},{7,15},{8,0},{9,1},... | collective-permute-start | bytes 196616 | tf_op jit(solution)/shard_map/ppermute | solution.py:568
  90.4 4.4 %collective-permute-start.21 = (bf16[128,256]{1,0:T(8,128)(2,1)S(1)}, bf16[128,256]{1,0:T(8,128)(2,1)S(1)}, u32[]{:S(2)}, u32[]{:S(2)}) collective-permute-start(bf16[128,256]{1,0:T(8,128)(2,1)S(1)} %get-tuple-element.76), channel_id=1, source_target_pairs={{0,1},{1,2},{2,3},{3,0},{4,5},{5,6},{6,7},{7,4},{8,9},{9,10},{10,1... | collective-permute-start | bytes 196616 | tf_op jit(solution)/shard_map/ppermute | solution.py:568
  90.5 4.6 %collective-permute-start.22 = (bf16[128,256]{1,0:T(8,128)(2,1)S(1)}, bf16[128,256]{1,0:T(8,128)(2,1)S(1)}, u32[]{:S(2)}, u32[]{:S(2)}) collective-permute-start(bf16[128,256]{1,0:T(8,128)(2,1)S(1)} %get-tuple-element.77), channel_id=1, source_target_pairs={{0,3},{1,0},{2,1},{3,2},{4,7},{5,4},{6,5},{7,6},{8,11},{9,8},{10,9... | collective-permute-start | bytes 196616 | tf_op jit(solution)/shard_map/ppermute | solution.py:568
  93.5 4.7 %collective-permute-start.23 = (bf16[128,256]{1,0:T(8,128)(2,1)S(1)}, bf16[128,256]{1,0:T(8,128)(2,1)S(1)}, u32[]{:S(2)}, u32[]{:S(2)}) collective-permute-start(bf16[128,256]{1,0:T(8,128)(2,1)S(1)} %get-tuple-element.78), channel_id=1, source_target_pairs={{0,2},{1,3},{2,0},{3,1},{4,6},{5,7},{6,4},{7,5},{8,10},{9,11},{10,... | collective-permute-start | bytes 196616 | tf_op jit(solution)/shard_map/ppermute | solution.py:568
  (2 other events, 4.0 us)

commit v4 on v3

--- a/solution.py
+++ b/solution.py
@@ -323,7 +323,7 @@
         copy.wait()
 
 
-def load_weight(weight):
+def load_weight(weight, grant):
     return pl.pallas_call(
         load_kernel,
         name="load_weight",
@@ -334,12 +334,12 @@
         cost_estimate=pl.CostEstimate(
             flops=0, bytes_accessed=4 * weight.size, transcendentals=0
         ),
-        compiler_params=pltpu.CompilerParams(vmem_limit_bytes=49 << 20),
+        compiler_params=pltpu.CompilerParams(vmem_limit_bytes=grant << 20),
     )(weight)
 
 
 def prepare_kernel(*refs):
-    kept, gain_ref, out_ref = refs[:4], refs[4], refs[6]
+    kept, gain_ref, out_ref = refs[:4], refs[4], refs[5]
     span = kept[0].shape[1]
     half = span // 4
     rows = EXPERTS * CAP
@@ -363,16 +363,16 @@
         out_ref[i, span:] = stats.astype(bf16)
 
 
-def prepare(kept, gain, after):
+def prepare(kept, gain):
     span = kept[0].shape[1]
     return pl.pallas_call(
         prepare_kernel,
         name="prepare",
-        in_specs=[VMEM] * 6,
+        in_specs=[VMEM] * 5,
         out_specs=VMEM,
         out_shape=pltpu.VMEM((2, span + STATS, EXPERTS * CAP), bf16),
         compiler_params=pltpu.CompilerParams(vmem_limit_bytes=8 << 20),
-    )(*kept, gain[None, :], after)
+    )(*kept, gain[None, :])
 
 
 def partial_products(k, own_ref, got_ref, gate_w, up_w):
@@ -406,30 +406,63 @@
 
 
 def finish_kernel(
-    k, first_ref, second_ref, gate_w, up_w, gate_in, up_in, squares_in, down_w, *out_refs
+    k, width, own_ref, got_ref, gate_w, up_w, gate_in, up_in, squares_in, inner_ref
 ):
-    first_outs, second_outs = out_refs[:4], out_refs[4:]
-    _, rows, piece = first_outs[0].shape
-    gate, up, squares = partial_products(k, first_ref, second_ref, gate_w, up_w)
+    gate, up, squares = partial_products(k, own_ref, got_ref, gate_w, up_w)
     squares = squares + squares_in[...]
-    factor = lax.rsqrt(squares * (1.0 / (16 * piece)) + epsilon)
+    factor = lax.rsqrt(squares * (1.0 / width) + epsilon)
     gate = (gate + gate_in[...]) * factor
     up = (up + up_in[...]) * factor
-    inner = (gate / (1.0 + jnp.exp(-gate)) * up).astype(bf16)
-    hidden = lax.axis_index("hidden")
-    for kx in range(4):
-        for ky in range(4):
-            owner = (hidden // 4 + kx) % 4 * 4 + (hidden % 4 + ky) % 4
-            weight = down_w[:, pl.ds(pl.multiple_of(owner * piece, piece), piece)]
-            part = dot(inner, weight, ((0,), (0,))).astype(bf16)
-            first_outs[kx][ky] = part[:rows]
-            second_outs[ky][kx] = part[rows:]
-
-
-def run_expert(firsts, seconds, gate_w, up_w, down_w):
+    inner_ref[...] = (gate / (1.0 + jnp.exp(-gate)) * up).astype(bf16)
+
+
+def down_kernel(k, inner_ref, down_w, kept_ref, given_ref):
+    half = kept_ref.shape[2] // 4
+    c = core_at()
+    inner = inner_ref[...]
+    for h, out_ref, at in ((c, kept_ref, (0,)), (1 - c, given_ref, ())):
+        weight = jnp.concatenate(
+            [down_w[:, half_lanes(h, j, k, 2 * half)] for j in range(4)], axis=1
+        )
+        out_ref[at if at else ...] = dot(inner, weight, ((0,), (0,))).astype(bf16)
+
+
+def down_part(k, inner, down_w):
+    hidden, rows = inner.shape
+    span = down_w.shape[1] // 8
+    return pl.pallas_call(
+        functools.partial(down_kernel, k),
+        name="down_part",
+        in_specs=[VMEM] * 2,
+        out_specs=[VMEM] * 2,
+        out_shape=[pltpu.VMEM((2, rows, span), bf16), pltpu.VMEM((rows, span), bf16)],
+        cost_estimate=pl.CostEstimate(
+            flops=4 * hidden * rows * span, bytes_accessed=1 << 20, transcendentals=0
+        ),
+        compiler_params=pltpu.CompilerParams(vmem_limit_bytes=16 << 20),
+    )(inner, down_w)
+
+
+def join_kernel(kept_ref, got_ref, out_ref):
+    out_ref[1] = got_ref[...]
+
+
+def join(kept, got):
+    return pl.pallas_call(
+        join_kernel,
+        name="join",
+        in_specs=[ANY, VMEM],
+        out_specs=VMEM,
+        out_shape=pltpu.VMEM(kept.shape, bf16),
+        input_output_aliases={0: 0},
+        compiler_params=pltpu.CompilerParams(vmem_limit_bytes=8 << 20),
+    )(kept, got)
+
+
+def run_expert(firsts, seconds, gate_w, up_w, width):
     _, lines, rows = firsts[0].shape
     half = (lines - STATS) // 4
-    hidden, _ = down_w.shape
+    hidden = gate_w.shape[0]
     cost = pl.CostEstimate(
         flops=16 * hidden * 4 * half * rows, bytes_accessed=1 << 22, transcendentals=0
     )
@@ -445,7 +478,7 @@
         compiler_params=params,
     )(firsts[0], seconds[0], gate_w, up_w)
     for i in (1, 2):
-        state = pl.pallas_call(
+        go_on = pl.pallas_call(
             functools.partial(go_on_kernel, STEPS[i]),
             name="expert_go_on",
             in_specs=[VMEM] * 7,
@@ -454,95 +487,138 @@
             cost_estimate=cost,
             input_output_aliases={4: 0, 5: 1, 6: 2},
             compiler_params=params,
-        )(firsts[i], seconds[i], gate_w, up_w, *state)
-    return pl.pallas_call(
-        functools.partial(finish_kernel, STEPS[3]),
+        )
+        state = go_on(firsts[i], seconds[i], gate_w, up_w, *state)
+    return pl.pallas_call(
+        functools.partial(finish_kernel, STEPS[3], width),
         name="expert_finish",
-        in_specs=[VMEM] * 8,
-        out_specs=[VMEM] * 8,
-        out_shape=[jax.ShapeDtypeStruct((4, rows // 2, 2 * half), bf16)] * 8,
+        in_specs=[VMEM] * 7,
+        out_specs=VMEM,
+        out_shape=jax.ShapeDtypeStruct((hidden, rows), bf16),
         cost_estimate=cost,
         compiler_params=params,
-    )(firsts[3], seconds[3], gate_w, up_w, *state, down_w)
-
-
-def add_kernel(*refs):
+    )(firsts[3], seconds[3], gate_w, up_w, *state)
+
+
+def spread_kernel(*refs):
+    parts, got_ref, out_refs = refs[:4], refs[4], refs[5:]
+    half = out_refs[0].shape[2]
+    c = core_at()
+    x_at, y_at = hidden_at()
+    for k, out_ref in enumerate(out_refs):
+        lanes = lanes_of(jnp.where(c == 0, (x_at + k) % 4, (y_at + k) % 4), half)
+        for i in range(2):
+            total = (parts[0][0, :, lanes] if i == 0 else got_ref[:, lanes]).astype(f32)
+            for part in parts[1:]:
+                total = total + part[i, :, lanes].astype(f32)
+            out_ref[i] = total.astype(bf16)
+
+
+def spread_sum(parts, got):
+    _, rows, span = parts[0].shape
+    return list(
+        pl.pallas_call(
+            spread_kernel,
+            name="spread_sum",
+            in_specs=[VMEM] * 5,
+            out_specs=[VMEM] * 4,
+            out_shape=[jax.ShapeDtypeStruct((2, rows, span // 4), bf16)] * 4,
+            compiler_params=pltpu.CompilerParams(vmem_limit_bytes=8 << 20),
+        )(*parts, got)
+    )
+
+
+def total_kernel(*refs):
     parts, out_refs = refs[:4], refs[4:]
-    for j, out_ref in enumerate(out_refs):
-        total = parts[0][j].astype(f32)
-        for part in parts[1:]:
-            total = total + part[j].astype(f32)
-        out_ref[...] = total.astype(bf16)
-
-
-def add_parts(parts):
-    count, rows, piece = parts[0].shape
-    return list(pl.pallas_call(
-        add_kernel,
-        name="add_parts",
-        in_specs=[VMEM] * 4,
-        out_specs=[VMEM] * count,
-        out_shape=[jax.ShapeDtypeStruct((rows, piece), bf16)] * count,
+    c = core_at()
+    for k, out_ref in enumerate(out_refs):
+        rows = slice(k * 2 * CAP, (k + 1) * 2 * CAP)
+        totals = []
+        for parity in range(2):
+            i = (c + parity) % 2
+            total = parts[0][i, rows].astype(f32)
+            for part in parts[1:]:
+                total = total + part[i, rows].astype(f32)
+            totals.append(total.astype(bf16))
+        for block in range(2):
+            for parity in range(2):
+                at = (2 * block + parity) * CAP
+                out_ref[at : at + CAP] = totals[parity][block * CAP : (block + 1) * CAP]
+
+
+def total_parts(parts):
+    half = parts[0].shape[2]
+    return list(
+        pl.pallas_call(
+            total_kernel,
+            name="total_parts",
+            in_specs=[VMEM] * 4,
+            out_specs=[VMEM] * 4,
+            out_shape=[jax.ShapeDtypeStruct((4 * CAP, half), bf16)] * 4,
+            compiler_params=pltpu.CompilerParams(vmem_limit_bytes=8 << 20),
+        )(*parts)
+    )
+
+
+def combine_kernel(own_ref, other_ref, *refs):
+    returned, first_table, second_table = refs[:4], refs[4], refs[5]
+    out_ref, given_ref = refs[6:]
+    c = core_at()
+    z = lax.axis_index("expert") // 2
+    mixed = []
+    for block, table in enumerate((first_table, second_table)):
+        rows = jnp.concatenate(
+            [
+                table[pl.ds(pl.multiple_of((z + k) % 4 * (2 * CAP), 2 * CAP), 2 * CAP), :]
+                for k in range(4)
+            ],
+            axis=0,
+        )
+        values = jnp.concatenate(
+            [part[block * 2 * CAP : (block + 1) * 2 * CAP] for part in returned], axis=0
+        )
+        mixed.append(0.5 * dot(rows, values, ((0,), (0,))))
+    own = jnp.where(c == 0, mixed[0], mixed[1]) + own_ref[...].astype(f32)
+    out_ref[...] = own.astype(bf16)
+    other = jnp.where(c == 0, mixed[1], mixed[0]) + other_ref[...].astype(f32)
+    given_ref[...] = other.astype(bf16)
+
+
+def combine(own, other, returned, tables):
+    return pl.pallas_call(
+        combine_kernel,
+        name="combine",
+        in_specs=[VMEM] * 8,
+        out_specs=[VMEM] * 2,
+        out_shape=[jax.ShapeDtypeStruct(own.shape, bf16)] * 2,
         compiler_params=pltpu.CompilerParams(vmem_limit_bytes=8 << 20),
-    )(*parts))
-
-
-def total_kernel(*refs):
-    out_ref = refs[8]
-    place = lax.axis_index("expert")
-    for h in range(2):
-        total = refs[h * 4][...].astype(f32)
-        for part in refs[h * 4 + 1 : h * 4 + 4]:
-            total = total + part[...].astype(f32)
-        total = total.astype(bf16)
-        for i in range(4):
-            block = (place // 2 + 4 - (h * 2 + i // 2)) % 4 * 2 + i % 2
-            out_ref[block] = total[i * CAP : (i + 1) * CAP]
-
-
-def total_parts(firsts, seconds):
-    piece = firsts[0].shape[1]
-    return pl.pallas_call(
-        total_kernel,
-        name="total_parts",
-        in_specs=[VMEM] * 8,
-        out_specs=VMEM,
-        out_shape=jax.ShapeDtypeStruct((EXPERTS, CAP, piece), bf16),
-        compiler_params=pltpu.CompilerParams(vmem_limit_bytes=8 << 20),
-    )(*firsts, *seconds)
-
-
-def combine_kernel(own_ref, other_ref, returned_ref, first_table, second_table, out_ref):
+    )(own, other, *returned, *tables)
+
+
+def lay_kernel(own_ref, got_ref, out_ref):
     first = core_at() == 0
     half = own_ref.shape[1]
-    own, other = own_ref[...].astype(f32), other_ref[...].astype(f32)
-    table = jnp.where(
-        first, first_table[...].astype(f32), second_table[...].astype(f32)
-    ).astype(bf16)
-    mixed = 0.5 * dot(table, returned_ref[...], ((0,), (0,)))
-    out_ref[:, :half] = (jnp.where(first, own, other) + mixed[:, :half]).astype(bf16)
-    out_ref[:, half:] = (jnp.where(first, other, own) + mixed[:, half:]).astype(bf16)
-
-
-def combine(own, other, returned, tables):
-    return pl.pallas_call(
-        combine_kernel,
-        name="combine",
-        in_specs=[VMEM] * 5,
+    own, got = own_ref[...].astype(f32), got_ref[...].astype(f32)
+    out_ref[:, :half] = jnp.where(first, own, got).astype(bf16)
+    out_ref[:, half:] = jnp.where(first, got, own).astype(bf16)
+
+
+def lay_out(own, got):
+    rows, half = own.shape
+    return pl.pallas_call(
+        lay_kernel,
+        name="lay_out",
+        in_specs=[VMEM] * 2,
         out_specs=VMEM,
-        out_shape=jax.ShapeDtypeStruct((own.shape[0], returned.shape[1]), bf16),
+        out_shape=jax.ShapeDtypeStruct((rows, 2 * half), bf16),
         compiler_params=pltpu.CompilerParams(vmem_limit_bytes=8 << 20),
-    )(own, other, returned, *tables)
-
-
-def swapped(parts, axis):
-    return lax.all_to_all(parts, axis, 0, 0, tiled=True)
-
-
-def along_expert(blocks):
+    )(own, got)
+
+
+def along_expert(blocks, sign):
     kept = [blocks[0]] + [None] * 3
     for k in STEPS[1:]:
-        pairs = [(z * 2 + c, (z + k) % 4 * 2 + c) for z in range(4) for c in range(2)]
+        pairs = [(z * 2 + c, (z + sign * k) % 4 * 2 + c) for z in range(4) for c in range(2)]
         kept[k] = lax.ppermute(blocks[k], "expert", pairs)
     return kept
 
@@ -561,19 +637,10 @@
     return lax.ppermute(array, ("expert", "hidden"), pairs)
 
 
-def shifted(array, dx, dy):
-    pairs = [
-        (x * 4 + y, (x + dx) % 4 * 4 + (y + dy) % 4) for x in range(4) for y in range(4)
-    ]
-    return lax.ppermute(array, "hidden", pairs)
-
-
 def per_device(
     queries, new_key, new_value, key_cache, value_cache, cache_lengths, residual,
     out_weight, norm_gain, expert_ids, gate_weight, up_weight, down_weight,
 ):
-    hidden_count = lax.axis_size("hidden")
-    columns = out_weight.shape[1] // hidden_count
     ids = expert_ids.T
     attended, given, own_residual, w_half = attend(
         queries, new_key, new_value, key_cache, value_cache, cache_lengths,
@@ -582,30 +649,38 @@
     got = to_partner(given)
     tables = tables_of(ids, got)
     parts = project(attended, got, w_half)
-    gate_w = load_weight(gate_weight[0].T)
+    gate_w = load_weight(gate_weight[0].T, 49)
     arrived = parts[:1]
     for k in STEPS[1:]:
         arrived.append(split_shift(parts[k], k, 1))
     part = plus(arrived)
-    up_w = load_weight(up_weight[0].T)
+    up_w = load_weight(up_weight[0].T, 47)
     parts = [part]
     for k in STEPS[1:]:
         parts.append(split_shift(part, k, 0))
-    own_stream, given, *blocks = make_stream(parts, own_residual, got, tables)
-    kept = along_expert(blocks)
-    other_stream = to_partner(given)
-    piece = prepare(kept, norm_gain, other_stream)
-    pieces = [piece] + [split_shift(piece, k, 1) for k in STEPS[1:]]
-    gots = [to_partner(piece[1]) for piece in pieces]
-    parts = list(run_expert(pieces, gots, gate_w, up_w, down_weight[0]))
-    firsts = add_parts(parts[:1] + [shifted(parts[k], k, 0) for k in STEPS[1:]])
-    seconds = add_parts(parts[4:5] + [shifted(parts[4 + k], 0, k) for k in STEPS[1:]])
-    firsts = firsts[:1] + [shifted(firsts[k], 0, k) for k in STEPS[1:]]
-    seconds = seconds[:1] + [shifted(seconds[k], k, 0) for k in STEPS[1:]]
-    returned = swapped(total_parts(firsts, seconds), "expert")
-    return combine(
-        own_stream, other_stream, returned.reshape(EXPERTS * CAP, columns), tables
-    )
+    own_stream, other_stream, *blocks = make_stream(parts, own_residual, got, tables)
+    down_w = down_weight[0]
+    kept = along_expert(blocks, 1)
+    piece = prepare(kept, norm_gain)
+    pieces, gots = [piece], [to_partner(piece[1])]
+    for k in STEPS[1:]:
+        pieces.append(split_shift(piece, k, 1))
+    gots += [to_partner(piece[1]) for piece in pieces[1:]]
+    inner = run_expert(pieces, gots, gate_w, up_w, down_weight[0].shape[1])
+    arrived = [None]
+    for k in STEPS[1:] + STEPS[:1]:
+        kept, given = down_part(k, inner, down_w)
+        got = to_partner(given)
+        if k == 0:
+            arrived[0] = kept
+        else:
+            kept = join(kept, got)
+            arrived.append(split_shift(kept, k, 1))
+    parts = spread_sum(arrived, got)
+    parts = total_parts(parts[:1] + [split_shift(parts[k], k, 0) for k in STEPS[1:]])
+    returned = along_expert(parts, -1)
+    own, given = combine(own_stream, other_stream, returned, tables)
+    return lay_out(own, to_partner(given))
 
 
 def solution(mesh):

time: 112 us -> 104 us (0.929)
  blocking collectives: 12.7 us -> 0 us
  waiting for transfers between devices: 34.5 us -> 40.3 us
  starting transfers between devices: 44 us -> 41.8 us
    ppermute x12 -> x0, waiting for transfers between devices: 18.3 us -> none  [shifted(): return lax.ppermute(array, 'hidden', pairs)]
    ppermute x9 -> x15, waiting for transfers between devices: 14.3 us -> 29.6 us  [split_shift(): return lax.ppermute(array, ('expert', 'hidden'), pairs)]
    all_to_all x1 -> x0, blocking collectives: 12.7 us -> none  [swapped(): return lax.all_to_all(parts, axis, 0, 0, tiled=True)]
    ppermute x12 -> x0, starting transfers between devices: 12.7 us -> none  [shifted(): return lax.ppermute(array, 'hidden', pairs)]
    ppermute x3 -> x6, waiting for transfers between devices: 0.09 us -> 7.31 us  [along_expert(): kept[k] = lax.ppermute(blocks[k], 'expert', pairs)]
    ppermute x9 -> x15, starting transfers between devices: 10.9 us -> 16.9 us  [split_shift(): return lax.ppermute(array, ('expert', 'hidden'), pairs)]
    ppermute x3 -> x6, starting transfers between devices: 5.12 us -> 8.42 us  [along_expert(): kept[k] = lax.ppermute(blocks[k], 'expert', pairs)]
    ppermute x6 -> x10, waiting for transfers between devices: 1.81 us -> 3.44 us  [to_partner(): return lax.ppermute(array, 'expert', pairs)]
  transfers between devices with their start and end apart: 30 -> 31, of which waited for: 15 -> 22; matrix products, arithmetic and copies ran while one was open for 0% -> 0% of each run, Pallas kernels for 8% -> 10%
where the time goes in v4:
time: 104 us
  starting transfers between devices  41.8 us (40%)
  waiting for transfers between devices  40.3 us (39%)
  Pallas kernels  20.6 us (20%)
    ppermute x15, waiting for transfers between devices, split_shift(): return lax.ppermute(array, ('expert', 'hidden'), pairs)  29.6 us
    ppermute x15, starting transfers between devices, split_shift(): return lax.ppermute(array, ('expert', 'hidden'), pairs)  16.9 us
    ppermute x10, starting transfers between devices, to_partner(): return lax.ppermute(array, 'expert', pairs)  16.5 us
    ppermute x6, starting transfers between devices, along_expert(): kept[k] = lax.ppermute(blocks[k], 'expert', pairs)  8.42 us
    ppermute x6, waiting for transfers between devices, along_expert(): kept[k] = lax.ppermute(blocks[k], 'expert', pairs)  7.31 us
    pallas_call x1, Pallas kernels, attend(): pl.pallas_call(attend_kernel, name='attend', in_specs=[ANY] * 9, out_spec...  5.6 us
    pallas_call x2, Pallas kernels, load_weight(): pl.pallas_call(load_kernel, name='load_weight', in_specs=[ANY], out_specs...  5.36 us
    ppermute x10, waiting for transfers between devices, to_partner(): return lax.ppermute(array, 'expert', pairs)  3.44 us
  transfers between devices with their start and end apart: 31, of which 22 were waited for; matrix products, arithmetic and copies ran while one was open for 0% of the time, Pallas kernels for 10%

profile of v4, /device:TPU:1, one launch (start us, length us, event | category | flops | bytes accessed | tf_op | source)
XLA Modules:
  0.0 103.7 jit_solution(13725686236269375692)
XLA Ops:
  0.0 5.6 %attend.1 = (bf16[64,256]{1,0:T(8,128)(2,1)S(1)}, bf16[80,768]{1,0:T(8,128)(2,1)S(1)}, bf16[64,512]{1,0:T(8,128)(2,1)S(1)}, bf16[256,2048]{1,0:T(8,128)(2,1)S(1)}) custom-call(s32[1,64]{1,0:T(1,128)} %bitcast.27, bf16[64,256]{1,0:T(8,128)(2,1)} %q_hbm.1, bf16[64,256]{1,0:T(8,128)(2,1)} %nk_hbm.1, bf16[64,256]{1,0:T(8,128)(2,1)} %nv_hbm.1, ...), custom_call_target="tpu_custom_call" | custom-call | tf_op jit(solution)/shard_map/attend/pallas_call | solution.py:143
  5.6 1.5 %collective-permute-start = (bf16[80,768]{1,0:T(8,128)(2,1)S(1)}, bf16[80,768]{1,0:T(8,128)(2,1)S(1)}, u32[]{:S(2)}, u32[]{:S(2)}) collective-permute-start(bf16[80,768]{1,0:T(8,128)(2,1)S(1)} %get-tuple-element.49), channel_id=1, source_target_pairs={{0,16},{16,0},{32,48},{48,32},{64,80},{80,64},{96,112},{112,96},{1... | collective-permute-start | bytes 368648 | tf_op jit(solution)/shard_map/ppermute | solution.py:628
  8.5 1.4 %collective-permute-start.1 = (bf16[128,512]{1,0:T(8,128)(2,1)S(1)}, bf16[128,512]{1,0:T(8,128)(2,1)S(1)}, u32[]{:S(2)}, u32[]{:S(2)}) collective-permute-start(bf16[128,512]{1,0:T(8,128)(2,1)S(1)} %get-tuple-element.52), channel_id=1, source_target_pairs={{0,1},{1,2},{2,3},{3,0},{4,5},{5,6},{6,7},{7,4},{8,9},{9,10},{10,1... | collective-permute-start | bytes 393224 | tf_op jit(solution)/shard_map/ppermute | solution.py:637
  9.9 1.4 %collective-permute-start.2 = (bf16[128,512]{1,0:T(8,128)(2,1)S(1)}, bf16[128,512]{1,0:T(8,128)(2,1)S(1)}, u32[]{:S(2)}, u32[]{:S(2)}) collective-permute-start(bf16[128,512]{1,0:T(8,128)(2,1)S(1)} %get-tuple-element.53), channel_id=1, source_target_pairs={{0,3},{1,0},{2,1},{3,2},{4,7},{5,4},{6,5},{7,6},{8,11},{9,8},{10,9... | collective-permute-start | bytes 393224 | tf_op jit(solution)/shard_map/ppermute | solution.py:637
  11.3 1.6 %collective-permute-start.3 = (bf16[128,512]{1,0:T(8,128)(2,1)S(1)}, bf16[128,512]{1,0:T(8,128)(2,1)S(1)}, u32[]{:S(2)}, u32[]{:S(2)}) collective-permute-start(bf16[128,512]{1,0:T(8,128)(2,1)S(1)} %get-tuple-element.54), channel_id=1, source_target_pairs={{0,2},{1,3},{2,0},{3,1},{4,6},{5,7},{6,4},{7,5},{8,10},{9,11},{10,... | collective-permute-start | bytes 393224 | tf_op jit(solution)/shard_map/ppermute | solution.py:637
  14.1 2.9 %collective-permute-done.3.refs_3_ = bf16[128,512]{1,0:T(8,128)(2,1)S(1)} collective-permute-done((bf16[128,512]{1,0:T(8,128)(2,1)S(1)}, bf16[128,512]{1,0:T(8,128)(2,1)S(1)}, u32[]{:S(2)}, u32[]{:S(2)}) %collective-permute-start.3) | collective-permute-done | bytes 131104 | tf_op jit(solution)/shard_map/ppermute | solution.py:637
  17.0 1.2 %collective-permute-start.4 = (bf16[128,512]{1,0:T(8,128)(2,1)S(1)}, bf16[128,512]{1,0:T(8,128)(2,1)S(1)}, u32[]{:S(2)}, u32[]{:S(2)}) collective-permute-start(bf16[128,512]{1,0:T(8,128)(2,1)S(1)} %plus.1.refs_0_), channel_id=1, source_target_pairs={{0,4},{1,5},{2,6},{3,7},{4,8},{5,9},{6,10},{7,11},{8,12},{9,13},{1... | collective-permute-start | bytes 393224 | tf_op jit(solution)/shard_map/ppermute | solution.py:637
  18.2 1.8 %collective-permute-start.5 = (bf16[128,512]{1,0:T(8,128)(2,1)S(1)}, bf16[128,512]{1,0:T(8,128)(2,1)S(1)}, u32[]{:S(2)}, u32[]{:S(2)}) collective-permute-start(bf16[128,512]{1,0:T(8,128)(2,1)S(1)} %plus.1.refs_0_), channel_id=1, source_target_pairs={{0,12},{1,13},{2,14},{3,15},{4,0},{5,1},{6,2},{7,3},{8,4},{9,5},{1... | collective-permute-start | bytes 393224 | tf_op jit(solution)/shard_map/ppermute | solution.py:637
  20.0 1.3 %collective-permute-start.6 = (bf16[128,512]{1,0:T(8,128)(2,1)S(1)}, bf16[128,512]{1,0:T(8,128)(2,1)S(1)}, u32[]{:S(2)}, u32[]{:S(2)}) collective-permute-start(bf16[128,512]{1,0:T(8,128)(2,1)S(1)} %plus.1.refs_0_), channel_id=1, source_target_pairs={{0,8},{1,9},{2,10},{3,11},{4,12},{5,13},{6,14},{7,15},{8,0},{9,1},... | collective-permute-start | bytes 393224 | tf_op jit(solution)/shard_map/ppermute | solution.py:637
  22.3 3.0 %collective-permute-done.6.refs_3_ = bf16[128,512]{1,0:T(8,128)(2,1)S(1)} collective-permute-done((bf16[128,512]{1,0:T(8,128)(2,1)S(1)}, bf16[128,512]{1,0:T(8,128)(2,1)S(1)}, u32[]{:S(2)}, u32[]{:S(2)}) %collective-permute-start.6) | collective-permute-done | bytes 131104 | tf_op jit(solution)/shard_map/ppermute | solution.py:637
  25.7 1.7 %collective-permute-start.7 = (bf16[128,512]{1,0:T(8,128)(2,1)S(1)}, bf16[128,512]{1,0:T(8,128)(2,1)S(1)}, u32[]{:S(2)}, u32[]{:S(2)}) collective-permute-start(bf16[128,512]{1,0:T(8,128)(2,1)S(1)} %get-tuple-element.61), channel_id=1, source_target_pairs={{0,32},{16,48},{32,64},{48,80},{64,96},{80,112},{96,0},{112,16},{1... | collective-permute-start | bytes 393224 | tf_op jit(solution)/shard_map/ppermute | solution.py:622
  27.4 3.3 %collective-permute-start.8 = (bf16[128,512]{1,0:T(8,128)(2,1)S(1)}, bf16[128,512]{1,0:T(8,128)(2,1)S(1)}, u32[]{:S(2)}, u32[]{:S(2)}) collective-permute-start(bf16[128,512]{1,0:T(8,128)(2,1)S(1)} %get-tuple-element.62), channel_id=1, source_target_pairs={{0,64},{16,80},{32,96},{48,112},{64,0},{80,16},{96,32},{112,48},{1... | collective-permute-start | bytes 393224 | tf_op jit(solution)/shard_map/ppermute | solution.py:622
  31.9 2.6 %collective-permute-done.8.refs_2_ = bf16[128,512]{1,0:T(8,128)(2,1)S(1)} collective-permute-done((bf16[128,512]{1,0:T(8,128)(2,1)S(1)}, bf16[128,512]{1,0:T(8,128)(2,1)S(1)}, u32[]{:S(2)}, u32[]{:S(2)}) %collective-permute-start.8) | collective-permute-done | bytes 131104 | tf_op jit(solution)/shard_map/ppermute | solution.py:622
  35.6 5.1 %collective-permute-start.16 = (bf16[528,256]{1,0:T(8,128)(2,1)S(1)}, bf16[528,256]{1,0:T(8,128)(2,1)S(1)}, u32[]{:S(2)}, u32[]{:S(2)}) collective-permute-start(bf16[528,256]{1,0:T(8,128)(2,1)S(1)} %slice_bitcast_fusion), channel_id=1, source_target_pairs={{0,16},{16,0},{32,48},{48,32},{64,80},{80,64},{96,112},{112,96},{1... | collective-permute-start | bytes 811016 | tf_op jit(solution)/shard_map/ppermute | solution.py:628
  40.7 1.3 %collective-permute-start.12 = (bf16[2,528,256]{2,1,0:T(8,128)(2,1)S(1)}, bf16[2,528,256]{2,1,0:T(8,128)(2,1)S(1)}, u32[]{:S(2)}, u32[]{:S(2)}) collective-permute-start(bf16[2,528,256]{2,1,0:T(8,128)(2,1)S(1)} %prepare.1.first_ref), channel_id=1, source_target_pairs={{0,3},{1,0},{2,1},{3,2},{4,7},{5,4},{6,5},{7,6},{8,11},{9,8},{10,9... | collective-permute-start | bytes 1622024 | tf_op jit(solution)/shard_map/ppermute | solution.py:637
  42.0 2.7 %load_weight.2.gate_w = bf16[688,4096]{1,0:T(8,128)(2,1)S(1)} custom-call(bf16[688,4096]{1,0:T(8,128)(2,1)} %bitcast.25), custom_call_target="tpu_custom_call" | custom-call | bytes 11272192 | tf_op jit(solution)/shard_map/load_weight/pallas_call | solution.py:327
  44.6 2.7 %load_weight.3.up_w = bf16[688,4096]{1,0:T(8,128)(2,1)S(1)} custom-call(bf16[688,4096]{1,0:T(8,128)(2,1)} %bitcast.26), custom_call_target="tpu_custom_call" | custom-call | bytes 11272192 | tf_op jit(solution)/shard_map/load_weight/pallas_call | solution.py:327
  48.9 1.8 %collective-permute-start.15 = (bf16[528,256]{1,0:T(8,128)(2,1)S(1)}, bf16[528,256]{1,0:T(8,128)(2,1)S(1)}, u32[]{:S(2)}, u32[]{:S(2)}) collective-permute-start(bf16[528,256]{1,0:T(8,128)(2,1)S(1)} %slice_bitcast_fusion.1), channel_id=1, source_target_pairs={{0,16},{16,0},{32,48},{48,32},{64,80},{80,64},{96,112},{112,96},{1... | collective-permute-start | bytes 811016 | tf_op jit(solution)/shard_map/ppermute | solution.py:628
  50.9 6.5 %collective-permute-done.10.own_ref = bf16[2,528,256]{2,1,0:T(8,128)(2,1)S(1)} collective-permute-done((bf16[2,528,256]{2,1,0:T(8,128)(2,1)S(1)}, bf16[2,528,256]{2,1,0:T(8,128)(2,1)S(1)}, u32[]{:S(2)}, u32[]{:S(2)}) %collective-permute-start.10) | collective-permute-done | bytes 540704 | tf_op jit(solution)/shard_map/ppermute | solution.py:637
  57.4 2.6 %collective-permute-start.11 = (bf16[528,256]{1,0:T(8,128)(2,1)S(1)}, bf16[528,256]{1,0:T(8,128)(2,1)S(1)}, u32[]{:S(2)}, u32[]{:S(2)}) collective-permute-start(bf16[528,256]{1,0:T(8,128)(2,1)S(1)} %slice_bitcast_fusion.3), channel_id=1, source_target_pairs={{0,16},{16,0},{32,48},{48,32},{64,80},{80,64},{96,112},{112,96},{1... | collective-permute-start | bytes 811016 | tf_op jit(solution)/shard_map/ppermute | solution.py:628
  62.2 1.1 %expert_finish.1.inner_ref = bf16[688,256]{1,0:T(8,128)(2,1)S(1)} custom-call(bf16[2,528,256]{2,1,0:T(8,128)(2,1)S(1)} %collective-permute-done.10.own_ref, bf16[528,256]{1,0:T(8,128)(2,1)S(1)} %collective-permute-done.11.got_ref, bf16[688,4096]{1,0:T(8,128)(2,1)S(1)} %load_weight.2.gate_w, bf16[688,4096]{1,0:T(8,128)(2,1)S(1)} %load_weight.3.up_w, ...), custom_call_target="tpu_custom_call" | custom-call | flops 1442840576 | bytes 4194304 | tf_op jit(solution)/shard_map/expert_finish/pallas_call | solution.py:492
  67.0 1.6 %collective-permute-start.22 = (bf16[2,256,512]{2,1,0:T(8,128)(2,1)S(1)}, bf16[2,256,512]{2,1,0:T(8,128)(2,1)S(1)}, u32[]{:S(2)}, u32[]{:S(2)}) collective-permute-start(bf16[2,256,512]{2,1,0:T(8,128)(2,1)S(1)} %join.5), channel_id=1, source_target_pairs={{0,2},{1,3},{2,0},{3,1},{4,6},{5,7},{6,4},{7,5},{8,10},{9,11},{10,... | collective-permute-start | bytes 1572872 | tf_op jit(solution)/shard_map/ppermute | solution.py:637
  71.2 1.5 %collective-permute-done.23.refs_4_ = bf16[256,512]{1,0:T(8,128)(2,1)S(1)} collective-permute-done((bf16[256,512]{1,0:T(8,128)(2,1)S(1)}, bf16[256,512]{1,0:T(8,128)(2,1)S(1)}, u32[]{:S(2)}, u32[]{:S(2)}) %collective-permute-start.23) | collective-permute-done | bytes 262176 | tf_op jit(solution)/shard_map/ppermute | solution.py:628
  72.6 4.4 %collective-permute-done.22.refs_3_ = bf16[2,256,512]{2,1,0:T(8,128)(2,1)S(1)} collective-permute-done((bf16[2,256,512]{2,1,0:T(8,128)(2,1)S(1)}, bf16[2,256,512]{2,1,0:T(8,128)(2,1)S(1)}, u32[]{:S(2)}, u32[]{:S(2)}) %collective-permute-start.22) | collective-permute-done | bytes 524320 | tf_op jit(solution)/shard_map/ppermute | solution.py:637
  77.0 4.5 %collective-permute-done.20.refs_2_ = bf16[2,256,512]{2,1,0:T(8,128)(2,1)S(1)} collective-permute-done((bf16[2,256,512]{2,1,0:T(8,128)(2,1)S(1)}, bf16[2,256,512]{2,1,0:T(8,128)(2,1)S(1)}, u32[]{:S(2)}, u32[]{:S(2)}) %collective-permute-start.20) | collective-permute-done | bytes 524320 | tf_op jit(solution)/shard_map/ppermute | solution.py:637
  81.5 1.1 %collective-permute-done.18.refs_1_ = bf16[2,256,512]{2,1,0:T(8,128)(2,1)S(1)} collective-permute-done((bf16[2,256,512]{2,1,0:T(8,128)(2,1)S(1)}, bf16[2,256,512]{2,1,0:T(8,128)(2,1)S(1)}, u32[]{:S(2)}, u32[]{:S(2)}) %collective-permute-start.18) | collective-permute-done | bytes 524320 | tf_op jit(solution)/shard_map/ppermute | solution.py:637
  82.9 2.7 %collective-permute-start.25 = (bf16[2,256,128]{2,1,0:T(8,128)(2,1)S(1)}, bf16[2,256,128]{2,1,0:T(8,128)(2,1)S(1)}, u32[]{:S(2)}, u32[]{:S(2)}) collective-permute-start(bf16[2,256,128]{2,1,0:T(8,128)(2,1)S(1)} %get-tuple-element.83), channel_id=1, source_target_pairs={{0,12},{1,13},{2,14},{3,15},{4,0},{5,1},{6,2},{7,3},{8,4},{9,5},{1... | collective-permute-start | bytes 393224 | tf_op jit(solution)/shard_map/ppermute | solution.py:637
  85.6 2.3 %collective-permute-done.24.refs_1_ = bf16[2,256,128]{2,1,0:T(8,128)(2,1)S(1)} collective-permute-done((bf16[2,256,128]{2,1,0:T(8,128)(2,1)S(1)}, bf16[2,256,128]{2,1,0:T(8,128)(2,1)S(1)}, u32[]{:S(2)}, u32[]{:S(2)}) %collective-permute-start.24) | collective-permute-done | bytes 131104 | tf_op jit(solution)/shard_map/ppermute | solution.py:637
  88.9 2.0 %collective-permute-done.26.refs_3_ = bf16[2,256,128]{2,1,0:T(8,128)(2,1)S(1)} collective-permute-done((bf16[2,256,128]{2,1,0:T(8,128)(2,1)S(1)}, bf16[2,256,128]{2,1,0:T(8,128)(2,1)S(1)}, u32[]{:S(2)}, u32[]{:S(2)}) %collective-permute-start.26) | collective-permute-done | bytes 131104 | tf_op jit(solution)/shard_map/ppermute | solution.py:637
  91.0 2.0 %collective-permute-start.27 = (bf16[128,128]{1,0:T(8,128)(2,1)S(1)}, bf16[128,128]{1,0:T(8,128)(2,1)S(1)}, u32[]{:S(2)}, u32[]{:S(2)}) collective-permute-start(bf16[128,128]{1,0:T(8,128)(2,1)S(1)} %get-tuple-element.86), channel_id=1, source_target_pairs={{0,96},{16,112},{32,0},{48,16},{64,32},{80,48},{96,64},{112,80},{1... | collective-permute-start | bytes 98312 | tf_op jit(solution)/shard_map/ppermute | solution.py:622
  94.0 3.3 %collective-permute-done.28.refs_2_ = bf16[128,128]{1,0:T(8,128)(2,1)S(1)} collective-permute-done((bf16[128,128]{1,0:T(8,128)(2,1)S(1)}, bf16[128,128]{1,0:T(8,128)(2,1)S(1)}, u32[]{:S(2)}, u32[]{:S(2)}) %collective-permute-start.28) | collective-permute-done | bytes 32800 | tf_op jit(solution)/shard_map/ppermute | solution.py:622
  97.8 4.4 %collective-permute-start.30 = (bf16[64,128]{1,0:T(8,128)(2,1)S(1)}, bf16[64,128]{1,0:T(8,128)(2,1)S(1)}, u32[]{:S(2)}, u32[]{:S(2)}) collective-permute-start(bf16[64,128]{1,0:T(8,128)(2,1)S(1)} %get-tuple-element.90), channel_id=1, source_target_pairs={{0,16},{16,0},{32,48},{48,32},{64,80},{80,64},{96,112},{112,96},{1... | collective-permute-start | bytes 49160 | tf_op jit(solution)/shard_map/ppermute | solution.py:628
  (67 shorter events, 20.7 us)
Async XLA Ops:
  0.0 31.4 %copy-start.1 = (bf16[4096]{0:T(1024)(128)(2,1)S(1)}, bf16[4096]{0:T(1024)(128)(2,1)}, u32[]{:S(2)}) copy-start(bf16[4096]{0:T(1024)(128)(2,1)} %param.21) | copy-start | bytes 24580
  5.6 2.4 %collective-permute-start = (bf16[80,768]{1,0:T(8,128)(2,1)S(1)}, bf16[80,768]{1,0:T(8,128)(2,1)S(1)}, u32[]{:S(2)}, u32[]{:S(2)}) collective-permute-start(bf16[80,768]{1,0:T(8,128)(2,1)S(1)} %get-tuple-element.49), channel_id=1, source_target_pairs={{0,16},{16,0},{32,48},{48,32},{64,80},{80,64},{96,112},{112,96},{1... | collective-permute-start | bytes 368648 | tf_op jit(solution)/shard_map/ppermute | solution.py:628
  8.5 5.4 %collective-permute-start.1 = (bf16[128,512]{1,0:T(8,128)(2,1)S(1)}, bf16[128,512]{1,0:T(8,128)(2,1)S(1)}, u32[]{:S(2)}, u32[]{:S(2)}) collective-permute-start(bf16[128,512]{1,0:T(8,128)(2,1)S(1)} %get-tuple-element.52), channel_id=1, source_target_pairs={{0,1},{1,2},{2,3},{3,0},{4,5},{5,6},{6,7},{7,4},{8,9},{9,10},{10,1... | collective-permute-start | bytes 393224 | tf_op jit(solution)/shard_map/ppermute | solution.py:637
  9.9 4.1 %collective-permute-start.2 = (bf16[128,512]{1,0:T(8,128)(2,1)S(1)}, bf16[128,512]{1,0:T(8,128)(2,1)S(1)}, u32[]{:S(2)}, u32[]{:S(2)}) collective-permute-start(bf16[128,512]{1,0:T(8,128)(2,1)S(1)} %get-tuple-element.53), channel_id=1, source_target_pairs={{0,3},{1,0},{2,1},{3,2},{4,7},{5,4},{6,5},{7,6},{8,11},{9,8},{10,9... | collective-permute-start | bytes 393224 | tf_op jit(solution)/shard_map/ppermute | solution.py:637
  11.3 5.6 %collective-permute-start.3 = (bf16[128,512]{1,0:T(8,128)(2,1)S(1)}, bf16[128,512]{1,0:T(8,128)(2,1)S(1)}, u32[]{:S(2)}, u32[]{:S(2)}) collective-permute-start(bf16[128,512]{1,0:T(8,128)(2,1)S(1)} %get-tuple-element.54), channel_id=1, source_target_pairs={{0,2},{1,3},{2,0},{3,1},{4,6},{5,7},{6,4},{7,5},{8,10},{9,11},{10,... | collective-permute-start | bytes 393224 | tf_op jit(solution)/shard_map/ppermute | solution.py:637
  17.0 5.3 %collective-permute-start.4 = (bf16[128,512]{1,0:T(8,128)(2,1)S(1)}, bf16[128,512]{1,0:T(8,128)(2,1)S(1)}, u32[]{:S(2)}, u32[]{:S(2)}) collective-permute-start(bf16[128,512]{1,0:T(8,128)(2,1)S(1)} %plus.1.refs_0_), channel_id=1, source_target_pairs={{0,4},{1,5},{2,6},{3,7},{4,8},{5,9},{6,10},{7,11},{8,12},{9,13},{1... | collective-permute-start | bytes 393224 | tf_op jit(solution)/shard_map/ppermute | solution.py:637
  18.2 4.1 %collective-permute-start.5 = (bf16[128,512]{1,0:T(8,128)(2,1)S(1)}, bf16[128,512]{1,0:T(8,128)(2,1)S(1)}, u32[]{:S(2)}, u32[]{:S(2)}) collective-permute-start(bf16[128,512]{1,0:T(8,128)(2,1)S(1)} %plus.1.refs_0_), channel_id=1, source_target_pairs={{0,12},{1,13},{2,14},{3,15},{4,0},{5,1},{6,2},{7,3},{8,4},{9,5},{1... | collective-permute-start | bytes 393224 | tf_op jit(solution)/shard_map/ppermute | solution.py:637
  20.0 5.3 %collective-permute-start.6 = (bf16[128,512]{1,0:T(8,128)(2,1)S(1)}, bf16[128,512]{1,0:T(8,128)(2,1)S(1)}, u32[]{:S(2)}, u32[]{:S(2)}) collective-permute-start(bf16[128,512]{1,0:T(8,128)(2,1)S(1)} %plus.1.refs_0_), channel_id=1, source_target_pairs={{0,8},{1,9},{2,10},{3,11},{4,12},{5,13},{6,14},{7,15},{8,0},{9,1},... | collective-permute-start | bytes 393224 | tf_op jit(solution)/shard_map/ppermute | solution.py:637
  25.7 6.2 %collective-permute-start.7 = (bf16[128,512]{1,0:T(8,128)(2,1)S(1)}, bf16[128,512]{1,0:T(8,128)(2,1)S(1)}, u32[]{:S(2)}, u32[]{:S(2)}) collective-permute-start(bf16[128,512]{1,0:T(8,128)(2,1)S(1)} %get-tuple-element.61), channel_id=1, source_target_pairs={{0,32},{16,48},{32,64},{48,80},{64,96},{80,112},{96,0},{112,16},{1... | collective-permute-start | bytes 393224 | tf_op jit(solution)/shard_map/ppermute | solution.py:622
  27.4 7.1 %collective-permute-start.8 = (bf16[128,512]{1,0:T(8,128)(2,1)S(1)}, bf16[128,512]{1,0:T(8,128)(2,1)S(1)}, u32[]{:S(2)}, u32[]{:S(2)}) collective-permute-start(bf16[128,512]{1,0:T(8,128)(2,1)S(1)} %get-tuple-element.62), channel_id=1, source_target_pairs={{0,64},{16,80},{32,96},{48,112},{64,0},{80,16},{96,32},{112,48},{1... | collective-permute-start | bytes 393224 | tf_op jit(solution)/shard_map/ppermute | solution.py:622
  30.7 4.1 %collective-permute-start.9 = (bf16[128,512]{1,0:T(8,128)(2,1)S(1)}, bf16[128,512]{1,0:T(8,128)(2,1)S(1)}, u32[]{:S(2)}, u32[]{:S(2)}) collective-permute-start(bf16[128,512]{1,0:T(8,128)(2,1)S(1)} %get-tuple-element.63), channel_id=1, source_target_pairs={{0,96},{16,112},{32,0},{48,16},{64,32},{80,48},{96,64},{112,80},{1... | collective-permute-start | bytes 393224 | tf_op jit(solution)/shard_map/ppermute | solution.py:622
  35.2 13.7 %collective-permute-start.14 = (bf16[2,528,256]{2,1,0:T(8,128)(2,1)S(1)}, bf16[2,528,256]{2,1,0:T(8,128)(2,1)S(1)}, u32[]{:S(2)}, u32[]{:S(2)}) collective-permute-start(bf16[2,528,256]{2,1,0:T(8,128)(2,1)S(1)} %prepare.1.first_ref), channel_id=1, source_target_pairs={{0,1},{1,2},{2,3},{3,0},{4,5},{5,6},{6,7},{7,4},{8,9},{9,10},{10,1... | collective-permute-start | bytes 1622024 | tf_op jit(solution)/shard_map/ppermute | solution.py:637
  35.6 12.4 %collective-permute-start.16 = (bf16[528,256]{1,0:T(8,128)(2,1)S(1)}, bf16[528,256]{1,0:T(8,128)(2,1)S(1)}, u32[]{:S(2)}, u32[]{:S(2)}) collective-permute-start(bf16[528,256]{1,0:T(8,128)(2,1)S(1)} %slice_bitcast_fusion), channel_id=1, source_target_pairs={{0,16},{16,0},{32,48},{48,32},{64,80},{80,64},{96,112},{112,96},{1... | collective-permute-start | bytes 811016 | tf_op jit(solution)/shard_map/ppermute | solution.py:628
  40.7 10.1 %collective-permute-start.12 = (bf16[2,528,256]{2,1,0:T(8,128)(2,1)S(1)}, bf16[2,528,256]{2,1,0:T(8,128)(2,1)S(1)}, u32[]{:S(2)}, u32[]{:S(2)}) collective-permute-start(bf16[2,528,256]{2,1,0:T(8,128)(2,1)S(1)} %prepare.1.first_ref), channel_id=1, source_target_pairs={{0,3},{1,0},{2,1},{3,2},{4,7},{5,4},{6,5},{7,6},{8,11},{9,8},{10,9... | collective-permute-start | bytes 1622024 | tf_op jit(solution)/shard_map/ppermute | solution.py:637
  47.3 10.1 %collective-permute-start.10 = (bf16[2,528,256]{2,1,0:T(8,128)(2,1)S(1)}, bf16[2,528,256]{2,1,0:T(8,128)(2,1)S(1)}, u32[]{:S(2)}, u32[]{:S(2)}) collective-permute-start(bf16[2,528,256]{2,1,0:T(8,128)(2,1)S(1)} %prepare.1.first_ref), channel_id=1, source_target_pairs={{0,2},{1,3},{2,0},{3,1},{4,6},{5,7},{6,4},{7,5},{8,10},{9,11},{10,... | collective-permute-start | bytes 1622024 | tf_op jit(solution)/shard_map/ppermute | solution.py:637
  48.9 11.2 %collective-permute-start.15 = (bf16[528,256]{1,0:T(8,128)(2,1)S(1)}, bf16[528,256]{1,0:T(8,128)(2,1)S(1)}, u32[]{:S(2)}, u32[]{:S(2)}) collective-permute-start(bf16[528,256]{1,0:T(8,128)(2,1)S(1)} %slice_bitcast_fusion.1), channel_id=1, source_target_pairs={{0,16},{16,0},{32,48},{48,32},{64,80},{80,64},{96,112},{112,96},{1... | collective-permute-start | bytes 811016 | tf_op jit(solution)/shard_map/ppermute | solution.py:628
  50.8 10.3 %collective-permute-start.13 = (bf16[528,256]{1,0:T(8,128)(2,1)S(1)}, bf16[528,256]{1,0:T(8,128)(2,1)S(1)}, u32[]{:S(2)}, u32[]{:S(2)}) collective-permute-start(bf16[528,256]{1,0:T(8,128)(2,1)S(1)} %slice_bitcast_fusion.2), channel_id=1, source_target_pairs={{0,16},{16,0},{32,48},{48,32},{64,80},{80,64},{96,112},{112,96},{1... | collective-permute-start | bytes 811016 | tf_op jit(solution)/shard_map/ppermute | solution.py:628
  57.4 4.7 %collective-permute-start.11 = (bf16[528,256]{1,0:T(8,128)(2,1)S(1)}, bf16[528,256]{1,0:T(8,128)(2,1)S(1)}, u32[]{:S(2)}, u32[]{:S(2)}) collective-permute-start(bf16[528,256]{1,0:T(8,128)(2,1)S(1)} %slice_bitcast_fusion.3), channel_id=1, source_target_pairs={{0,16},{16,0},{32,48},{48,32},{64,80},{80,64},{96,112},{112,96},{1... | collective-permute-start | bytes 811016 | tf_op jit(solution)/shard_map/ppermute | solution.py:628
  65.4 1.6 %collective-permute-start.21 = (bf16[256,512]{1,0:T(8,128)(2,1)S(1)}, bf16[256,512]{1,0:T(8,128)(2,1)S(1)}, u32[]{:S(2)}, u32[]{:S(2)}) collective-permute-start(bf16[256,512]{1,0:T(8,128)(2,1)S(1)} %get-tuple-element.79), channel_id=1, source_target_pairs={{0,16},{16,0},{32,48},{48,32},{64,80},{80,64},{96,112},{112,96},{1... | collective-permute-start | bytes 786440 | tf_op jit(solution)/shard_map/ppermute | solution.py:628
  65.5 3.2 %collective-permute-start.19 = (bf16[256,512]{1,0:T(8,128)(2,1)S(1)}, bf16[256,512]{1,0:T(8,128)(2,1)S(1)}, u32[]{:S(2)}, u32[]{:S(2)}) collective-permute-start(bf16[256,512]{1,0:T(8,128)(2,1)S(1)} %get-tuple-element.77), channel_id=1, source_target_pairs={{0,16},{16,0},{32,48},{48,32},{64,80},{80,64},{96,112},{112,96},{1... | collective-permute-start | bytes 786440 | tf_op jit(solution)/shard_map/ppermute | solution.py:628
  66.7 2.9 %collective-permute-start.17 = (bf16[256,512]{1,0:T(8,128)(2,1)S(1)}, bf16[256,512]{1,0:T(8,128)(2,1)S(1)}, u32[]{:S(2)}, u32[]{:S(2)}) collective-permute-start(bf16[256,512]{1,0:T(8,128)(2,1)S(1)} %get-tuple-element.75), channel_id=1, source_target_pairs={{0,16},{16,0},{32,48},{48,32},{64,80},{80,64},{96,112},{112,96},{1... | collective-permute-start | bytes 786440 | tf_op jit(solution)/shard_map/ppermute | solution.py:628
  67.0 10.0 %collective-permute-start.22 = (bf16[2,256,512]{2,1,0:T(8,128)(2,1)S(1)}, bf16[2,256,512]{2,1,0:T(8,128)(2,1)S(1)}, u32[]{:S(2)}, u32[]{:S(2)}) collective-permute-start(bf16[2,256,512]{2,1,0:T(8,128)(2,1)S(1)} %join.5), channel_id=1, source_target_pairs={{0,2},{1,3},{2,0},{3,1},{4,6},{5,7},{6,4},{7,5},{8,10},{9,11},{10,... | collective-permute-start | bytes 1572872 | tf_op jit(solution)/shard_map/ppermute | solution.py:637
  68.7 12.8 %collective-permute-start.20 = (bf16[2,256,512]{2,1,0:T(8,128)(2,1)S(1)}, bf16[2,256,512]{2,1,0:T(8,128)(2,1)S(1)}, u32[]{:S(2)}, u32[]{:S(2)}) collective-permute-start(bf16[2,256,512]{2,1,0:T(8,128)(2,1)S(1)} %join.4), channel_id=1, source_target_pairs={{0,3},{1,0},{2,1},{3,2},{4,7},{5,4},{6,5},{7,6},{8,11},{9,8},{10,9... | collective-permute-start | bytes 1572872 | tf_op jit(solution)/shard_map/ppermute | solution.py:637
  69.6 12.9 %collective-permute-start.18 = (bf16[2,256,512]{2,1,0:T(8,128)(2,1)S(1)}, bf16[2,256,512]{2,1,0:T(8,128)(2,1)S(1)}, u32[]{:S(2)}, u32[]{:S(2)}) collective-permute-start(bf16[2,256,512]{2,1,0:T(8,128)(2,1)S(1)} %join.3), channel_id=1, source_target_pairs={{0,1},{1,2},{2,3},{3,0},{4,5},{5,6},{6,7},{7,4},{8,9},{9,10},{10,1... | collective-permute-start | bytes 1572872 | tf_op jit(solution)/shard_map/ppermute | solution.py:637
  71.0 1.6 %collective-permute-start.23 = (bf16[256,512]{1,0:T(8,128)(2,1)S(1)}, bf16[256,512]{1,0:T(8,128)(2,1)S(1)}, u32[]{:S(2)}, u32[]{:S(2)}) collective-permute-start(bf16[256,512]{1,0:T(8,128)(2,1)S(1)} %get-tuple-element.80), channel_id=1, source_target_pairs={{0,16},{16,0},{32,48},{48,32},{64,80},{80,64},{96,112},{112,96},{1... | collective-permute-start | bytes 786440 | tf_op jit(solution)/shard_map/ppermute | solution.py:628
  82.8 5.1 %collective-permute-start.24 = (bf16[2,256,128]{2,1,0:T(8,128)(2,1)S(1)}, bf16[2,256,128]{2,1,0:T(8,128)(2,1)S(1)}, u32[]{:S(2)}, u32[]{:S(2)}) collective-permute-start(bf16[2,256,128]{2,1,0:T(8,128)(2,1)S(1)} %get-tuple-element.82), channel_id=1, source_target_pairs={{0,4},{1,5},{2,6},{3,7},{4,8},{5,9},{6,10},{7,11},{8,12},{9,13},{1... | collective-permute-start | bytes 393224 | tf_op jit(solution)/shard_map/ppermute | solution.py:637
  82.9 6.0 %collective-permute-start.25 = (bf16[2,256,128]{2,1,0:T(8,128)(2,1)S(1)}, bf16[2,256,128]{2,1,0:T(8,128)(2,1)S(1)}, u32[]{:S(2)}, u32[]{:S(2)}) collective-permute-start(bf16[2,256,128]{2,1,0:T(8,128)(2,1)S(1)} %get-tuple-element.83), channel_id=1, source_target_pairs={{0,12},{1,13},{2,14},{3,15},{4,0},{5,1},{6,2},{7,3},{8,4},{9,5},{1... | collective-permute-start | bytes 393224 | tf_op jit(solution)/shard_map/ppermute | solution.py:637
  85.6 5.3 %collective-permute-start.26 = (bf16[2,256,128]{2,1,0:T(8,128)(2,1)S(1)}, bf16[2,256,128]{2,1,0:T(8,128)(2,1)S(1)}, u32[]{:S(2)}, u32[]{:S(2)}) collective-permute-start(bf16[2,256,128]{2,1,0:T(8,128)(2,1)S(1)} %get-tuple-element.84), channel_id=1, source_target_pairs={{0,8},{1,9},{2,10},{3,11},{4,12},{5,13},{6,14},{7,15},{8,0},{9,1},... | collective-permute-start | bytes 393224 | tf_op jit(solution)/shard_map/ppermute | solution.py:637
  91.0 3.1 %collective-permute-start.27 = (bf16[128,128]{1,0:T(8,128)(2,1)S(1)}, bf16[128,128]{1,0:T(8,128)(2,1)S(1)}, u32[]{:S(2)}, u32[]{:S(2)}) collective-permute-start(bf16[128,128]{1,0:T(8,128)(2,1)S(1)} %get-tuple-element.86), channel_id=1, source_target_pairs={{0,96},{16,112},{32,0},{48,16},{64,32},{80,48},{96,64},{112,80},{1... | collective-permute-start | bytes 98312 | tf_op jit(solution)/shard_map/ppermute | solution.py:622
  93.0 4.3 %collective-permute-start.28 = (bf16[128,128]{1,0:T(8,128)(2,1)S(1)}, bf16[128,128]{1,0:T(8,128)(2,1)S(1)}, u32[]{:S(2)}, u32[]{:S(2)}) collective-permute-start(bf16[128,128]{1,0:T(8,128)(2,1)S(1)} %get-tuple-element.87), channel_id=1, source_target_pairs={{0,64},{16,80},{32,96},{48,112},{64,0},{80,16},{96,32},{112,48},{1... | collective-permute-start | bytes 98312 | tf_op jit(solution)/shard_map/ppermute | solution.py:622
  93.4 4.2 %collective-permute-start.29 = (bf16[128,128]{1,0:T(8,128)(2,1)S(1)}, bf16[128,128]{1,0:T(8,128)(2,1)S(1)}, u32[]{:S(2)}, u32[]{:S(2)}) collective-permute-start(bf16[128,128]{1,0:T(8,128)(2,1)S(1)} %get-tuple-element.88), channel_id=1, source_target_pairs={{0,32},{16,48},{32,64},{48,80},{64,96},{80,112},{96,0},{112,16},{1... | collective-permute-start | bytes 98312 | tf_op jit(solution)/shard_map/ppermute | solution.py:622
  97.8 5.3 %collective-permute-start.30 = (bf16[64,128]{1,0:T(8,128)(2,1)S(1)}, bf16[64,128]{1,0:T(8,128)(2,1)S(1)}, u32[]{:S(2)}, u32[]{:S(2)}) collective-permute-start(bf16[64,128]{1,0:T(8,128)(2,1)S(1)} %get-tuple-element.90), channel_id=1, source_target_pairs={{0,16},{16,0},{32,48},{48,32},{64,80},{80,64},{96,112},{112,96},{1... | collective-permute-start | bytes 49160 | tf_op jit(solution)/shard_map/ppermute | solution.py:628
  (3 other events, 25.3 us)

commit v5 on v4

--- a/solution.py
+++ b/solution.py
@@ -16,7 +16,7 @@
 
 EXPERTS = 8
 CAP = 32
-GROUP = 16
+GROUP = 32
 STATS = 16
 STEPS = (0, 1, 3, 2)
 
@@ -94,8 +94,6 @@
                 w_hbm.at[:, source], w_half.at[:, pl.ds(n * size, size)], w_sem.at[n]
             )
         )
-    for copy in others:
-        copy.start()
     for copy in small:
         copy.wait()
 
@@ -108,7 +106,9 @@
     for g in range(groups):
         rows = slice(g * GROUP, (g + 1) * GROUP)
         keys[g].wait()
-        values[g].wait()
+        if g == 0:
+            for copy in others:
+                copy.start()
         valid = (place >= first) & (place < first + length[rows])
         for h in range(head_count):
             lanes = slice(h * size, (h + 1) * size)
@@ -124,6 +124,8 @@
             weights = jnp.where(valid, jnp.exp(masked - highest), f32(0.0))
             own_weight = jnp.exp(own_score - highest)
             total = jnp.sum(weights, axis=1, keepdims=True) + own_weight
+            if h == 0:
+                values[g].wait()
             value_rows = v[rows, h].reshape(GROUP * positions, size)
             mixed = dot(weights.astype(bf16), value_rows, ((1,), (0,)))
             own_rounded = own_weight.astype(bf16).astype(f32)
@@ -397,7 +399,7 @@
 
 
 def go_on_kernel(
-    k, first_ref, second_ref, gate_w, up_w, gate_in, up_in, squares_in, gate_ref, up_ref, squares_ref
+    k, first_ref, second_ref, gate_w, up_w, gate_in, up_in, squares_in, _, gate_ref, up_ref, squares_ref
 ):
     gate, up, squares = partial_products(k, first_ref, second_ref, gate_w, up_w)
     gate_ref[...] = gate_in[...] + gate
@@ -459,10 +461,10 @@
     )(kept, got)
 
 
-def run_expert(firsts, seconds, gate_w, up_w, width):
+def run_expert(firsts, seconds, gate_w, up_w, down_w):
     _, lines, rows = firsts[0].shape
     half = (lines - STATS) // 4
-    hidden = gate_w.shape[0]
+    hidden, width = gate_w.shape
     cost = pl.CostEstimate(
         flops=16 * hidden * 4 * half * rows, bytes_accessed=1 << 22, transcendentals=0
     )
@@ -481,14 +483,14 @@
         go_on = pl.pallas_call(
             functools.partial(go_on_kernel, STEPS[i]),
             name="expert_go_on",
-            in_specs=[VMEM] * 7,
+            in_specs=[VMEM] * 8,
             out_specs=[VMEM] * 3,
             out_shape=sums,
             cost_estimate=cost,
             input_output_aliases={4: 0, 5: 1, 6: 2},
             compiler_params=params,
         )
-        state = go_on(firsts[i], seconds[i], gate_w, up_w, *state)
+        state = go_on(firsts[i], seconds[i], gate_w, up_w, *state, down_w)
     return pl.pallas_call(
         functools.partial(finish_kernel, STEPS[3], width),
         name="expert_finish",
@@ -665,10 +667,11 @@
     pieces, gots = [piece], [to_partner(piece[1])]
     for k in STEPS[1:]:
         pieces.append(split_shift(piece, k, 1))
-    gots += [to_partner(piece[1]) for piece in pieces[1:]]
-    inner = run_expert(pieces, gots, gate_w, up_w, down_weight[0].shape[1])
+    for i in range(1, 4):
+        gots.append(to_partner(pieces[i][1]))
+    inner = run_expert(pieces, gots, gate_w, up_w, down_w)
     arrived = [None]
-    for k in STEPS[1:] + STEPS[:1]:
+    for k in (3, 1, 2, 0):
         kept, given = down_part(k, inner, down_w)
         got = to_partner(given)
         if k == 0:

time: 104 us -> 104 us (level)
  local copies, waits for them, and re-layouts: 0.8 us -> 5.41 us
  waiting for transfers between devices: 40.3 us -> 36.1 us
  starting transfers between devices: 41.8 us -> 43.1 us
  Pallas kernels: 20.6 us -> 19.5 us
    unnamed x8 -> x12, local copies, waits for them, and re-layouts: 0.71 us -> 5.33 us
    ppermute x15, waiting for transfers between devices: 29.6 us -> 25.4 us  [split_shift(): return lax.ppermute(array, ('expert', 'hidden'), pairs)]
    pallas_call x1, Pallas kernels: 5.6 us -> 4.43 us  [attend(): pl.pallas_call(attend_kernel, name='attend', in_specs=[ANY] * 9, out_spec...]
    ppermute x15, starting transfers between devices: 16.9 us -> 18 us  [split_shift(): return lax.ppermute(array, ('expert', 'hidden'), pairs)]
  transfers between devices with their start and end apart: 31 -> 31, of which waited for: 22 -> 21; matrix products, arithmetic and copies ran while one was open for 0% -> 0% of each run, Pallas kernels for 10% -> 10%
where the time goes in v5:
time: 104 us
  starting transfers between devices  43.1 us (41%)
  waiting for transfers between devices  36.1 us (35%)
  Pallas kernels  19.5 us (19%)
  local copies, waits for them, and re-layouts  5.41 us (5%)
    ppermute x15, waiting for transfers between devices, split_shift(): return lax.ppermute(array, ('expert', 'hidden'), pairs)  25.4 us
    ppermute x15, starting transfers between devices, split_shift(): return lax.ppermute(array, ('expert', 'hidden'), pairs)  18 us
    ppermute x10, starting transfers between devices, to_partner(): return lax.ppermute(array, 'expert', pairs)  16.6 us
    ppermute x6, starting transfers between devices, along_expert(): kept[k] = lax.ppermute(blocks[k], 'expert', pairs)  8.43 us
    ppermute x6, waiting for transfers between devices, along_expert(): kept[k] = lax.ppermute(blocks[k], 'expert', pairs)  7.31 us
    pallas_call x2, Pallas kernels, load_weight(): pl.pallas_call(load_kernel, name='load_weight', in_specs=[ANY], out_specs...  5.46 us
    unnamed x12, local copies, waits for them, and re-layouts  5.33 us
    pallas_call x1, Pallas kernels, attend(): pl.pallas_call(attend_kernel, name='attend', in_specs=[ANY] * 9, out_spec...  4.43 us
  transfers between devices with their start and end apart: 31, of which 21 were waited for; matrix products, arithmetic and copies ran while one was open for 0% of the time, Pallas kernels for 10%

profile of v5, /device:TPU:1, one launch (start us, length us, event | category | flops | bytes accessed | tf_op | source)
XLA Modules:
  0.0 104.4 jit_solution(2695287252738412648)
XLA Ops:
  0.0 4.4 %attend.1 = (bf16[64,256]{1,0:T(8,128)(2,1)S(1)}, bf16[80,768]{1,0:T(8,128)(2,1)S(1)}, bf16[64,512]{1,0:T(8,128)(2,1)S(1)}, bf16[256,2048]{1,0:T(8,128)(2,1)S(1)}) custom-call(s32[1,64]{1,0:T(1,128)} %bitcast.29, bf16[64,256]{1,0:T(8,128)(2,1)} %q_hbm.1, bf16[64,256]{1,0:T(8,128)(2,1)} %nk_hbm.1, bf16[64,256]{1,0:T(8,128)(2,1)} %nv_hbm.1, ...), custom_call_target="tpu_custom_call" | custom-call | tf_op jit(solution)/shard_map/attend/pallas_call | solution.py:145
  4.4 1.5 %collective-permute-start = (bf16[80,768]{1,0:T(8,128)(2,1)S(1)}, bf16[80,768]{1,0:T(8,128)(2,1)S(1)}, u32[]{:S(2)}, u32[]{:S(2)}) collective-permute-start(bf16[80,768]{1,0:T(8,128)(2,1)S(1)} %get-tuple-element.49), channel_id=1, source_target_pairs={{0,16},{16,0},{32,48},{48,32},{64,80},{80,64},{96,112},{112,96},{1... | collective-permute-start | bytes 368648 | tf_op jit(solution)/shard_map/ppermute | solution.py:630
  7.4 1.4 %collective-permute-start.1 = (bf16[128,512]{1,0:T(8,128)(2,1)S(1)}, bf16[128,512]{1,0:T(8,128)(2,1)S(1)}, u32[]{:S(2)}, u32[]{:S(2)}) collective-permute-start(bf16[128,512]{1,0:T(8,128)(2,1)S(1)} %get-tuple-element.52), channel_id=1, source_target_pairs={{0,1},{1,2},{2,3},{3,0},{4,5},{5,6},{6,7},{7,4},{8,9},{9,10},{10,1... | collective-permute-start | bytes 393224 | tf_op jit(solution)/shard_map/ppermute | solution.py:639
  8.8 1.4 %collective-permute-start.2 = (bf16[128,512]{1,0:T(8,128)(2,1)S(1)}, bf16[128,512]{1,0:T(8,128)(2,1)S(1)}, u32[]{:S(2)}, u32[]{:S(2)}) collective-permute-start(bf16[128,512]{1,0:T(8,128)(2,1)S(1)} %get-tuple-element.53), channel_id=1, source_target_pairs={{0,3},{1,0},{2,1},{3,2},{4,7},{5,4},{6,5},{7,6},{8,11},{9,8},{10,9... | collective-permute-start | bytes 393224 | tf_op jit(solution)/shard_map/ppermute | solution.py:639
  10.1 1.6 %collective-permute-start.3 = (bf16[128,512]{1,0:T(8,128)(2,1)S(1)}, bf16[128,512]{1,0:T(8,128)(2,1)S(1)}, u32[]{:S(2)}, u32[]{:S(2)}) collective-permute-start(bf16[128,512]{1,0:T(8,128)(2,1)S(1)} %get-tuple-element.54), channel_id=1, source_target_pairs={{0,2},{1,3},{2,0},{3,1},{4,6},{5,7},{6,4},{7,5},{8,10},{9,11},{10,... | collective-permute-start | bytes 393224 | tf_op jit(solution)/shard_map/ppermute | solution.py:639
  12.9 2.9 %collective-permute-done.3.refs_3_ = bf16[128,512]{1,0:T(8,128)(2,1)S(1)} collective-permute-done((bf16[128,512]{1,0:T(8,128)(2,1)S(1)}, bf16[128,512]{1,0:T(8,128)(2,1)S(1)}, u32[]{:S(2)}, u32[]{:S(2)}) %collective-permute-start.3) | collective-permute-done | bytes 131104 | tf_op jit(solution)/shard_map/ppermute | solution.py:639
  17.0 1.8 %collective-permute-start.5 = (bf16[128,512]{1,0:T(8,128)(2,1)S(1)}, bf16[128,512]{1,0:T(8,128)(2,1)S(1)}, u32[]{:S(2)}, u32[]{:S(2)}) collective-permute-start(bf16[128,512]{1,0:T(8,128)(2,1)S(1)} %plus.1.refs_0_), channel_id=1, source_target_pairs={{0,12},{1,13},{2,14},{3,15},{4,0},{5,1},{6,2},{7,3},{8,4},{9,5},{1... | collective-permute-start | bytes 393224 | tf_op jit(solution)/shard_map/ppermute | solution.py:639
  18.8 1.3 %collective-permute-start.6 = (bf16[128,512]{1,0:T(8,128)(2,1)S(1)}, bf16[128,512]{1,0:T(8,128)(2,1)S(1)}, u32[]{:S(2)}, u32[]{:S(2)}) collective-permute-start(bf16[128,512]{1,0:T(8,128)(2,1)S(1)} %plus.1.refs_0_), channel_id=1, source_target_pairs={{0,8},{1,9},{2,10},{3,11},{4,12},{5,13},{6,14},{7,15},{8,0},{9,1},... | collective-permute-start | bytes 393224 | tf_op jit(solution)/shard_map/ppermute | solution.py:639
  21.1 3.0 %collective-permute-done.6.refs_3_ = bf16[128,512]{1,0:T(8,128)(2,1)S(1)} collective-permute-done((bf16[128,512]{1,0:T(8,128)(2,1)S(1)}, bf16[128,512]{1,0:T(8,128)(2,1)S(1)}, u32[]{:S(2)}, u32[]{:S(2)}) %collective-permute-start.6) | collective-permute-done | bytes 131104 | tf_op jit(solution)/shard_map/ppermute | solution.py:639
  24.5 1.7 %collective-permute-start.7 = (bf16[128,512]{1,0:T(8,128)(2,1)S(1)}, bf16[128,512]{1,0:T(8,128)(2,1)S(1)}, u32[]{:S(2)}, u32[]{:S(2)}) collective-permute-start(bf16[128,512]{1,0:T(8,128)(2,1)S(1)} %get-tuple-element.61), channel_id=1, source_target_pairs={{0,32},{16,48},{32,64},{48,80},{64,96},{80,112},{96,0},{112,16},{1... | collective-permute-start | bytes 393224 | tf_op jit(solution)/shard_map/ppermute | solution.py:624
  26.2 3.3 %collective-permute-start.8 = (bf16[128,512]{1,0:T(8,128)(2,1)S(1)}, bf16[128,512]{1,0:T(8,128)(2,1)S(1)}, u32[]{:S(2)}, u32[]{:S(2)}) collective-permute-start(bf16[128,512]{1,0:T(8,128)(2,1)S(1)} %get-tuple-element.62), channel_id=1, source_target_pairs={{0,64},{16,80},{32,96},{48,112},{64,0},{80,16},{96,32},{112,48},{1... | collective-permute-start | bytes 393224 | tf_op jit(solution)/shard_map/ppermute | solution.py:624
  30.7 2.6 %collective-permute-done.8.refs_2_ = bf16[128,512]{1,0:T(8,128)(2,1)S(1)} collective-permute-done((bf16[128,512]{1,0:T(8,128)(2,1)S(1)}, bf16[128,512]{1,0:T(8,128)(2,1)S(1)}, u32[]{:S(2)}, u32[]{:S(2)}) %collective-permute-start.8) | collective-permute-done | bytes 131104 | tf_op jit(solution)/shard_map/ppermute | solution.py:624
  34.4 5.1 %collective-permute-start.16 = (bf16[528,256]{1,0:T(8,128)(2,1)S(1)}, bf16[528,256]{1,0:T(8,128)(2,1)S(1)}, u32[]{:S(2)}, u32[]{:S(2)}) collective-permute-start(bf16[528,256]{1,0:T(8,128)(2,1)S(1)} %slice_bitcast_fusion), channel_id=1, source_target_pairs={{0,16},{16,0},{32,48},{48,32},{64,80},{80,64},{96,112},{112,96},{1... | collective-permute-start | bytes 811016 | tf_op jit(solution)/shard_map/ppermute | solution.py:630
  39.5 1.3 %collective-permute-start.12 = (bf16[2,528,256]{2,1,0:T(8,128)(2,1)S(1)}, bf16[2,528,256]{2,1,0:T(8,128)(2,1)S(1)}, u32[]{:S(2)}, u32[]{:S(2)}) collective-permute-start(bf16[2,528,256]{2,1,0:T(8,128)(2,1)S(1)} %prepare.1.first_ref), channel_id=1, source_target_pairs={{0,3},{1,0},{2,1},{3,2},{4,7},{5,4},{6,5},{7,6},{8,11},{9,8},{10,9... | collective-permute-start | bytes 1622024 | tf_op jit(solution)/shard_map/ppermute | solution.py:639
  40.8 2.7 %load_weight.2.gate_w = bf16[688,4096]{1,0:T(8,128)(2,1)S(1)} custom-call(bf16[688,4096]{1,0:T(8,128)(2,1)} %bitcast.27), custom_call_target="tpu_custom_call" | custom-call | bytes 11272192 | tf_op jit(solution)/shard_map/load_weight/pallas_call | solution.py:329
  43.5 2.8 %load_weight.3.up_w = bf16[688,4096]{1,0:T(8,128)(2,1)S(1)} custom-call(bf16[688,4096]{1,0:T(8,128)(2,1)} %bitcast.28), custom_call_target="tpu_custom_call" | custom-call | bytes 11272192 | tf_op jit(solution)/shard_map/load_weight/pallas_call | solution.py:329
  46.3 2.4 %copy-done = bf16[688,4096]{1,0:T(8,128)(2,1)} copy-done((bf16[688,4096]{1,0:T(8,128)(2,1)}, bf16[688,4096]{1,0:T(8,128)(2,1)S(1)}, u32[]{:S(2)}) %copy-start) | copy-done | bytes 5636120
  49.3 2.9 %copy-done.1 = bf16[688,4096]{1,0:T(8,128)(2,1)S(1)} copy-done((bf16[688,4096]{1,0:T(8,128)(2,1)S(1)}, bf16[688,4096]{1,0:T(8,128)(2,1)}, u32[]{:S(2)}) %copy-start.1) | copy-done | bytes 5636120
  53.1 2.0 %collective-permute-start.15 = (bf16[528,256]{1,0:T(8,128)(2,1)S(1)}, bf16[528,256]{1,0:T(8,128)(2,1)S(1)}, u32[]{:S(2)}, u32[]{:S(2)}) collective-permute-start(bf16[528,256]{1,0:T(8,128)(2,1)S(1)} %slice_bitcast_fusion.1), channel_id=1, source_target_pairs={{0,16},{16,0},{32,48},{48,32},{64,80},{80,64},{96,112},{112,96},{1... | collective-permute-start | bytes 811016 | tf_op jit(solution)/shard_map/ppermute | solution.py:630
  55.2 3.6 %collective-permute-done.10.own_ref = bf16[2,528,256]{2,1,0:T(8,128)(2,1)S(1)} collective-permute-done((bf16[2,528,256]{2,1,0:T(8,128)(2,1)S(1)}, bf16[2,528,256]{2,1,0:T(8,128)(2,1)S(1)}, u32[]{:S(2)}, u32[]{:S(2)}) %collective-permute-start.10) | collective-permute-done | bytes 540704 | tf_op jit(solution)/shard_map/ppermute | solution.py:639
  58.8 2.6 %collective-permute-start.11 = (bf16[528,256]{1,0:T(8,128)(2,1)S(1)}, bf16[528,256]{1,0:T(8,128)(2,1)S(1)}, u32[]{:S(2)}, u32[]{:S(2)}) collective-permute-start(bf16[528,256]{1,0:T(8,128)(2,1)S(1)} %slice_bitcast_fusion.3), channel_id=1, source_target_pairs={{0,16},{16,0},{32,48},{48,32},{64,80},{80,64},{96,112},{112,96},{1... | collective-permute-start | bytes 811016 | tf_op jit(solution)/shard_map/ppermute | solution.py:630
  67.6 1.6 %collective-permute-start.22 = (bf16[2,256,512]{2,1,0:T(8,128)(2,1)S(1)}, bf16[2,256,512]{2,1,0:T(8,128)(2,1)S(1)}, u32[]{:S(2)}, u32[]{:S(2)}) collective-permute-start(bf16[2,256,512]{2,1,0:T(8,128)(2,1)S(1)} %join.5), channel_id=1, source_target_pairs={{0,2},{1,3},{2,0},{3,1},{4,6},{5,7},{6,4},{7,5},{8,10},{9,11},{10,... | collective-permute-start | bytes 1572872 | tf_op jit(solution)/shard_map/ppermute | solution.py:639
  69.7 2.4 %collective-permute-start.18 = (bf16[2,256,512]{2,1,0:T(8,128)(2,1)S(1)}, bf16[2,256,512]{2,1,0:T(8,128)(2,1)S(1)}, u32[]{:S(2)}, u32[]{:S(2)}) collective-permute-start(bf16[2,256,512]{2,1,0:T(8,128)(2,1)S(1)} %join.3), channel_id=1, source_target_pairs={{0,3},{1,0},{2,1},{3,2},{4,7},{5,4},{6,5},{7,6},{8,11},{9,8},{10,9... | collective-permute-start | bytes 1572872 | tf_op jit(solution)/shard_map/ppermute | solution.py:639
  73.0 1.4 %collective-permute-done.23.refs_4_ = bf16[256,512]{1,0:T(8,128)(2,1)S(1)} collective-permute-done((bf16[256,512]{1,0:T(8,128)(2,1)S(1)}, bf16[256,512]{1,0:T(8,128)(2,1)S(1)}, u32[]{:S(2)}, u32[]{:S(2)}) %collective-permute-start.23) | collective-permute-done | bytes 262176 | tf_op jit(solution)/shard_map/ppermute | solution.py:630
  74.4 3.2 %collective-permute-done.22.refs_3_ = bf16[2,256,512]{2,1,0:T(8,128)(2,1)S(1)} collective-permute-done((bf16[2,256,512]{2,1,0:T(8,128)(2,1)S(1)}, bf16[2,256,512]{2,1,0:T(8,128)(2,1)S(1)}, u32[]{:S(2)}, u32[]{:S(2)}) %collective-permute-start.22) | collective-permute-done | bytes 524320 | tf_op jit(solution)/shard_map/ppermute | solution.py:639
  77.6 5.6 %collective-permute-done.20.refs_2_ = bf16[2,256,512]{2,1,0:T(8,128)(2,1)S(1)} collective-permute-done((bf16[2,256,512]{2,1,0:T(8,128)(2,1)S(1)}, bf16[2,256,512]{2,1,0:T(8,128)(2,1)S(1)}, u32[]{:S(2)}, u32[]{:S(2)}) %collective-permute-start.20) | collective-permute-done | bytes 524320 | tf_op jit(solution)/shard_map/ppermute | solution.py:639
  83.5 2.7 %collective-permute-start.25 = (bf16[2,256,128]{2,1,0:T(8,128)(2,1)S(1)}, bf16[2,256,128]{2,1,0:T(8,128)(2,1)S(1)}, u32[]{:S(2)}, u32[]{:S(2)}) collective-permute-start(bf16[2,256,128]{2,1,0:T(8,128)(2,1)S(1)} %get-tuple-element.83), channel_id=1, source_target_pairs={{0,12},{1,13},{2,14},{3,15},{4,0},{5,1},{6,2},{7,3},{8,4},{9,5},{1... | collective-permute-start | bytes 393224 | tf_op jit(solution)/shard_map/ppermute | solution.py:639
  86.2 2.3 %collective-permute-done.24.refs_1_ = bf16[2,256,128]{2,1,0:T(8,128)(2,1)S(1)} collective-permute-done((bf16[2,256,128]{2,1,0:T(8,128)(2,1)S(1)}, bf16[2,256,128]{2,1,0:T(8,128)(2,1)S(1)}, u32[]{:S(2)}, u32[]{:S(2)}) %collective-permute-start.24) | collective-permute-done | bytes 131104 | tf_op jit(solution)/shard_map/ppermute | solution.py:639
  89.5 2.0 %collective-permute-done.26.refs_3_ = bf16[2,256,128]{2,1,0:T(8,128)(2,1)S(1)} collective-permute-done((bf16[2,256,128]{2,1,0:T(8,128)(2,1)S(1)}, bf16[2,256,128]{2,1,0:T(8,128)(2,1)S(1)}, u32[]{:S(2)}, u32[]{:S(2)}) %collective-permute-start.26) | collective-permute-done | bytes 131104 | tf_op jit(solution)/shard_map/ppermute | solution.py:639
  91.6 2.0 %collective-permute-start.27 = (bf16[128,128]{1,0:T(8,128)(2,1)S(1)}, bf16[128,128]{1,0:T(8,128)(2,1)S(1)}, u32[]{:S(2)}, u32[]{:S(2)}) collective-permute-start(bf16[128,128]{1,0:T(8,128)(2,1)S(1)} %get-tuple-element.86), channel_id=1, source_target_pairs={{0,96},{16,112},{32,0},{48,16},{64,32},{80,48},{96,64},{112,80},{1... | collective-permute-start | bytes 98312 | tf_op jit(solution)/shard_map/ppermute | solution.py:624
  94.6 3.3 %collective-permute-done.28.refs_2_ = bf16[128,128]{1,0:T(8,128)(2,1)S(1)} collective-permute-done((bf16[128,128]{1,0:T(8,128)(2,1)S(1)}, bf16[128,128]{1,0:T(8,128)(2,1)S(1)}, u32[]{:S(2)}, u32[]{:S(2)}) %collective-permute-start.28) | collective-permute-done | bytes 32800 | tf_op jit(solution)/shard_map/ppermute | solution.py:624
  98.4 4.4 %collective-permute-start.30 = (bf16[64,128]{1,0:T(8,128)(2,1)S(1)}, bf16[64,128]{1,0:T(8,128)(2,1)S(1)}, u32[]{:S(2)}, u32[]{:S(2)}) collective-permute-start(bf16[64,128]{1,0:T(8,128)(2,1)S(1)} %get-tuple-element.90), channel_id=1, source_target_pairs={{0,16},{16,0},{32,48},{48,32},{64,80},{80,64},{96,112},{112,96},{1... | collective-permute-start | bytes 49160 | tf_op jit(solution)/shard_map/ppermute | solution.py:630
  (71 shorter events, 21.0 us)
Async XLA Ops:
  0.0 30.2 %copy-start.3 = (bf16[4096]{0:T(1024)(128)(2,1)S(1)}, bf16[4096]{0:T(1024)(128)(2,1)}, u32[]{:S(2)}) copy-start(bf16[4096]{0:T(1024)(128)(2,1)} %param.21) | copy-start | bytes 24580
  4.4 2.4 %collective-permute-start = (bf16[80,768]{1,0:T(8,128)(2,1)S(1)}, bf16[80,768]{1,0:T(8,128)(2,1)S(1)}, u32[]{:S(2)}, u32[]{:S(2)}) collective-permute-start(bf16[80,768]{1,0:T(8,128)(2,1)S(1)} %get-tuple-element.49), channel_id=1, source_target_pairs={{0,16},{16,0},{32,48},{48,32},{64,80},{80,64},{96,112},{112,96},{1... | collective-permute-start | bytes 368648 | tf_op jit(solution)/shard_map/ppermute | solution.py:630
  7.4 5.4 %collective-permute-start.1 = (bf16[128,512]{1,0:T(8,128)(2,1)S(1)}, bf16[128,512]{1,0:T(8,128)(2,1)S(1)}, u32[]{:S(2)}, u32[]{:S(2)}) collective-permute-start(bf16[128,512]{1,0:T(8,128)(2,1)S(1)} %get-tuple-element.52), channel_id=1, source_target_pairs={{0,1},{1,2},{2,3},{3,0},{4,5},{5,6},{6,7},{7,4},{8,9},{9,10},{10,1... | collective-permute-start | bytes 393224 | tf_op jit(solution)/shard_map/ppermute | solution.py:639
  8.8 4.1 %collective-permute-start.2 = (bf16[128,512]{1,0:T(8,128)(2,1)S(1)}, bf16[128,512]{1,0:T(8,128)(2,1)S(1)}, u32[]{:S(2)}, u32[]{:S(2)}) collective-permute-start(bf16[128,512]{1,0:T(8,128)(2,1)S(1)} %get-tuple-element.53), channel_id=1, source_target_pairs={{0,3},{1,0},{2,1},{3,2},{4,7},{5,4},{6,5},{7,6},{8,11},{9,8},{10,9... | collective-permute-start | bytes 393224 | tf_op jit(solution)/shard_map/ppermute | solution.py:639
  10.1 5.6 %collective-permute-start.3 = (bf16[128,512]{1,0:T(8,128)(2,1)S(1)}, bf16[128,512]{1,0:T(8,128)(2,1)S(1)}, u32[]{:S(2)}, u32[]{:S(2)}) collective-permute-start(bf16[128,512]{1,0:T(8,128)(2,1)S(1)} %get-tuple-element.54), channel_id=1, source_target_pairs={{0,2},{1,3},{2,0},{3,1},{4,6},{5,7},{6,4},{7,5},{8,10},{9,11},{10,... | collective-permute-start | bytes 393224 | tf_op jit(solution)/shard_map/ppermute | solution.py:639
  15.8 5.3 %collective-permute-start.4 = (bf16[128,512]{1,0:T(8,128)(2,1)S(1)}, bf16[128,512]{1,0:T(8,128)(2,1)S(1)}, u32[]{:S(2)}, u32[]{:S(2)}) collective-permute-start(bf16[128,512]{1,0:T(8,128)(2,1)S(1)} %plus.1.refs_0_), channel_id=1, source_target_pairs={{0,4},{1,5},{2,6},{3,7},{4,8},{5,9},{6,10},{7,11},{8,12},{9,13},{1... | collective-permute-start | bytes 393224 | tf_op jit(solution)/shard_map/ppermute | solution.py:639
  17.0 4.1 %collective-permute-start.5 = (bf16[128,512]{1,0:T(8,128)(2,1)S(1)}, bf16[128,512]{1,0:T(8,128)(2,1)S(1)}, u32[]{:S(2)}, u32[]{:S(2)}) collective-permute-start(bf16[128,512]{1,0:T(8,128)(2,1)S(1)} %plus.1.refs_0_), channel_id=1, source_target_pairs={{0,12},{1,13},{2,14},{3,15},{4,0},{5,1},{6,2},{7,3},{8,4},{9,5},{1... | collective-permute-start | bytes 393224 | tf_op jit(solution)/shard_map/ppermute | solution.py:639
  18.8 5.3 %collective-permute-start.6 = (bf16[128,512]{1,0:T(8,128)(2,1)S(1)}, bf16[128,512]{1,0:T(8,128)(2,1)S(1)}, u32[]{:S(2)}, u32[]{:S(2)}) collective-permute-start(bf16[128,512]{1,0:T(8,128)(2,1)S(1)} %plus.1.refs_0_), channel_id=1, source_target_pairs={{0,8},{1,9},{2,10},{3,11},{4,12},{5,13},{6,14},{7,15},{8,0},{9,1},... | collective-permute-start | bytes 393224 | tf_op jit(solution)/shard_map/ppermute | solution.py:639
  24.5 6.2 %collective-permute-start.7 = (bf16[128,512]{1,0:T(8,128)(2,1)S(1)}, bf16[128,512]{1,0:T(8,128)(2,1)S(1)}, u32[]{:S(2)}, u32[]{:S(2)}) collective-permute-start(bf16[128,512]{1,0:T(8,128)(2,1)S(1)} %get-tuple-element.61), channel_id=1, source_target_pairs={{0,32},{16,48},{32,64},{48,80},{64,96},{80,112},{96,0},{112,16},{1... | collective-permute-start | bytes 393224 | tf_op jit(solution)/shard_map/ppermute | solution.py:624
  26.2 7.1 %collective-permute-start.8 = (bf16[128,512]{1,0:T(8,128)(2,1)S(1)}, bf16[128,512]{1,0:T(8,128)(2,1)S(1)}, u32[]{:S(2)}, u32[]{:S(2)}) collective-permute-start(bf16[128,512]{1,0:T(8,128)(2,1)S(1)} %get-tuple-element.62), channel_id=1, source_target_pairs={{0,64},{16,80},{32,96},{48,112},{64,0},{80,16},{96,32},{112,48},{1... | collective-permute-start | bytes 393224 | tf_op jit(solution)/shard_map/ppermute | solution.py:624
  29.5 4.1 %collective-permute-start.9 = (bf16[128,512]{1,0:T(8,128)(2,1)S(1)}, bf16[128,512]{1,0:T(8,128)(2,1)S(1)}, u32[]{:S(2)}, u32[]{:S(2)}) collective-permute-start(bf16[128,512]{1,0:T(8,128)(2,1)S(1)} %get-tuple-element.63), channel_id=1, source_target_pairs={{0,96},{16,112},{32,0},{48,16},{64,32},{80,48},{96,64},{112,80},{1... | collective-permute-start | bytes 393224 | tf_op jit(solution)/shard_map/ppermute | solution.py:624
  34.1 19.0 %collective-permute-start.14 = (bf16[2,528,256]{2,1,0:T(8,128)(2,1)S(1)}, bf16[2,528,256]{2,1,0:T(8,128)(2,1)S(1)}, u32[]{:S(2)}, u32[]{:S(2)}) collective-permute-start(bf16[2,528,256]{2,1,0:T(8,128)(2,1)S(1)} %prepare.1.first_ref), channel_id=1, source_target_pairs={{0,1},{1,2},{2,3},{3,0},{4,5},{5,6},{6,7},{7,4},{8,9},{9,10},{10,1... | collective-permute-start | bytes 1622024 | tf_op jit(solution)/shard_map/ppermute | solution.py:639
  34.4 14.8 %collective-permute-start.16 = (bf16[528,256]{1,0:T(8,128)(2,1)S(1)}, bf16[528,256]{1,0:T(8,128)(2,1)S(1)}, u32[]{:S(2)}, u32[]{:S(2)}) collective-permute-start(bf16[528,256]{1,0:T(8,128)(2,1)S(1)} %slice_bitcast_fusion), channel_id=1, source_target_pairs={{0,16},{16,0},{32,48},{48,32},{64,80},{80,64},{96,112},{112,96},{1... | collective-permute-start | bytes 811016 | tf_op jit(solution)/shard_map/ppermute | solution.py:630
  39.5 15.5 %collective-permute-start.12 = (bf16[2,528,256]{2,1,0:T(8,128)(2,1)S(1)}, bf16[2,528,256]{2,1,0:T(8,128)(2,1)S(1)}, u32[]{:S(2)}, u32[]{:S(2)}) collective-permute-start(bf16[2,528,256]{2,1,0:T(8,128)(2,1)S(1)} %prepare.1.first_ref), channel_id=1, source_target_pairs={{0,3},{1,0},{2,1},{3,2},{4,7},{5,4},{6,5},{7,6},{8,11},{9,8},{10,9... | collective-permute-start | bytes 1622024 | tf_op jit(solution)/shard_map/ppermute | solution.py:639
  48.7 10.0 %collective-permute-start.10 = (bf16[2,528,256]{2,1,0:T(8,128)(2,1)S(1)}, bf16[2,528,256]{2,1,0:T(8,128)(2,1)S(1)}, u32[]{:S(2)}, u32[]{:S(2)}) collective-permute-start(bf16[2,528,256]{2,1,0:T(8,128)(2,1)S(1)} %prepare.1.first_ref), channel_id=1, source_target_pairs={{0,2},{1,3},{2,0},{3,1},{4,6},{5,7},{6,4},{7,5},{8,10},{9,11},{10,... | collective-permute-start | bytes 1622024 | tf_op jit(solution)/shard_map/ppermute | solution.py:639
  53.1 8.3 %collective-permute-start.15 = (bf16[528,256]{1,0:T(8,128)(2,1)S(1)}, bf16[528,256]{1,0:T(8,128)(2,1)S(1)}, u32[]{:S(2)}, u32[]{:S(2)}) collective-permute-start(bf16[528,256]{1,0:T(8,128)(2,1)S(1)} %slice_bitcast_fusion.1), channel_id=1, source_target_pairs={{0,16},{16,0},{32,48},{48,32},{64,80},{80,64},{96,112},{112,96},{1... | collective-permute-start | bytes 811016 | tf_op jit(solution)/shard_map/ppermute | solution.py:630
  55.1 7.4 %collective-permute-start.13 = (bf16[528,256]{1,0:T(8,128)(2,1)S(1)}, bf16[528,256]{1,0:T(8,128)(2,1)S(1)}, u32[]{:S(2)}, u32[]{:S(2)}) collective-permute-start(bf16[528,256]{1,0:T(8,128)(2,1)S(1)} %slice_bitcast_fusion.2), channel_id=1, source_target_pairs={{0,16},{16,0},{32,48},{48,32},{64,80},{80,64},{96,112},{112,96},{1... | collective-permute-start | bytes 811016 | tf_op jit(solution)/shard_map/ppermute | solution.py:630
  58.8 4.7 %collective-permute-start.11 = (bf16[528,256]{1,0:T(8,128)(2,1)S(1)}, bf16[528,256]{1,0:T(8,128)(2,1)S(1)}, u32[]{:S(2)}, u32[]{:S(2)}) collective-permute-start(bf16[528,256]{1,0:T(8,128)(2,1)S(1)} %slice_bitcast_fusion.3), channel_id=1, source_target_pairs={{0,16},{16,0},{32,48},{48,32},{64,80},{80,64},{96,112},{112,96},{1... | collective-permute-start | bytes 811016 | tf_op jit(solution)/shard_map/ppermute | solution.py:630
  66.0 1.6 %collective-permute-start.21 = (bf16[256,512]{1,0:T(8,128)(2,1)S(1)}, bf16[256,512]{1,0:T(8,128)(2,1)S(1)}, u32[]{:S(2)}, u32[]{:S(2)}) collective-permute-start(bf16[256,512]{1,0:T(8,128)(2,1)S(1)} %get-tuple-element.79), channel_id=1, source_target_pairs={{0,16},{16,0},{32,48},{48,32},{64,80},{80,64},{96,112},{112,96},{1... | collective-permute-start | bytes 786440 | tf_op jit(solution)/shard_map/ppermute | solution.py:630
  66.1 3.1 %collective-permute-start.19 = (bf16[256,512]{1,0:T(8,128)(2,1)S(1)}, bf16[256,512]{1,0:T(8,128)(2,1)S(1)}, u32[]{:S(2)}, u32[]{:S(2)}) collective-permute-start(bf16[256,512]{1,0:T(8,128)(2,1)S(1)} %get-tuple-element.77), channel_id=1, source_target_pairs={{0,16},{16,0},{32,48},{48,32},{64,80},{80,64},{96,112},{112,96},{1... | collective-permute-start | bytes 786440 | tf_op jit(solution)/shard_map/ppermute | solution.py:630
  67.3 2.4 %collective-permute-start.17 = (bf16[256,512]{1,0:T(8,128)(2,1)S(1)}, bf16[256,512]{1,0:T(8,128)(2,1)S(1)}, u32[]{:S(2)}, u32[]{:S(2)}) collective-permute-start(bf16[256,512]{1,0:T(8,128)(2,1)S(1)} %get-tuple-element.75), channel_id=1, source_target_pairs={{0,16},{16,0},{32,48},{48,32},{64,80},{80,64},{96,112},{112,96},{1... | collective-permute-start | bytes 786440 | tf_op jit(solution)/shard_map/ppermute | solution.py:630
  67.6 10.0 %collective-permute-start.22 = (bf16[2,256,512]{2,1,0:T(8,128)(2,1)S(1)}, bf16[2,256,512]{2,1,0:T(8,128)(2,1)S(1)}, u32[]{:S(2)}, u32[]{:S(2)}) collective-permute-start(bf16[2,256,512]{2,1,0:T(8,128)(2,1)S(1)} %join.5), channel_id=1, source_target_pairs={{0,2},{1,3},{2,0},{3,1},{4,6},{5,7},{6,4},{7,5},{8,10},{9,11},{10,... | collective-permute-start | bytes 1572872 | tf_op jit(solution)/shard_map/ppermute | solution.py:639
  69.3 13.9 %collective-permute-start.20 = (bf16[2,256,512]{2,1,0:T(8,128)(2,1)S(1)}, bf16[2,256,512]{2,1,0:T(8,128)(2,1)S(1)}, u32[]{:S(2)}, u32[]{:S(2)}) collective-permute-start(bf16[2,256,512]{2,1,0:T(8,128)(2,1)S(1)} %join.4), channel_id=1, source_target_pairs={{0,1},{1,2},{2,3},{3,0},{4,5},{5,6},{6,7},{7,4},{8,9},{9,10},{10,1... | collective-permute-start | bytes 1572872 | tf_op jit(solution)/shard_map/ppermute | solution.py:639
  69.7 13.5 %collective-permute-start.18 = (bf16[2,256,512]{2,1,0:T(8,128)(2,1)S(1)}, bf16[2,256,512]{2,1,0:T(8,128)(2,1)S(1)}, u32[]{:S(2)}, u32[]{:S(2)}) collective-permute-start(bf16[2,256,512]{2,1,0:T(8,128)(2,1)S(1)} %join.3), channel_id=1, source_target_pairs={{0,3},{1,0},{2,1},{3,2},{4,7},{5,4},{6,5},{7,6},{8,11},{9,8},{10,9... | collective-permute-start | bytes 1572872 | tf_op jit(solution)/shard_map/ppermute | solution.py:639
  72.8 1.6 %collective-permute-start.23 = (bf16[256,512]{1,0:T(8,128)(2,1)S(1)}, bf16[256,512]{1,0:T(8,128)(2,1)S(1)}, u32[]{:S(2)}, u32[]{:S(2)}) collective-permute-start(bf16[256,512]{1,0:T(8,128)(2,1)S(1)} %get-tuple-element.80), channel_id=1, source_target_pairs={{0,16},{16,0},{32,48},{48,32},{64,80},{80,64},{96,112},{112,96},{1... | collective-permute-start | bytes 786440 | tf_op jit(solution)/shard_map/ppermute | solution.py:630
  83.4 5.1 %collective-permute-start.24 = (bf16[2,256,128]{2,1,0:T(8,128)(2,1)S(1)}, bf16[2,256,128]{2,1,0:T(8,128)(2,1)S(1)}, u32[]{:S(2)}, u32[]{:S(2)}) collective-permute-start(bf16[2,256,128]{2,1,0:T(8,128)(2,1)S(1)} %get-tuple-element.82), channel_id=1, source_target_pairs={{0,4},{1,5},{2,6},{3,7},{4,8},{5,9},{6,10},{7,11},{8,12},{9,13},{1... | collective-permute-start | bytes 393224 | tf_op jit(solution)/shard_map/ppermute | solution.py:639
  83.5 6.0 %collective-permute-start.25 = (bf16[2,256,128]{2,1,0:T(8,128)(2,1)S(1)}, bf16[2,256,128]{2,1,0:T(8,128)(2,1)S(1)}, u32[]{:S(2)}, u32[]{:S(2)}) collective-permute-start(bf16[2,256,128]{2,1,0:T(8,128)(2,1)S(1)} %get-tuple-element.83), channel_id=1, source_target_pairs={{0,12},{1,13},{2,14},{3,15},{4,0},{5,1},{6,2},{7,3},{8,4},{9,5},{1... | collective-permute-start | bytes 393224 | tf_op jit(solution)/shard_map/ppermute | solution.py:639
  86.2 5.3 %collective-permute-start.26 = (bf16[2,256,128]{2,1,0:T(8,128)(2,1)S(1)}, bf16[2,256,128]{2,1,0:T(8,128)(2,1)S(1)}, u32[]{:S(2)}, u32[]{:S(2)}) collective-permute-start(bf16[2,256,128]{2,1,0:T(8,128)(2,1)S(1)} %get-tuple-element.84), channel_id=1, source_target_pairs={{0,8},{1,9},{2,10},{3,11},{4,12},{5,13},{6,14},{7,15},{8,0},{9,1},... | collective-permute-start | bytes 393224 | tf_op jit(solution)/shard_map/ppermute | solution.py:639
  91.6 3.1 %collective-permute-start.27 = (bf16[128,128]{1,0:T(8,128)(2,1)S(1)}, bf16[128,128]{1,0:T(8,128)(2,1)S(1)}, u32[]{:S(2)}, u32[]{:S(2)}) collective-permute-start(bf16[128,128]{1,0:T(8,128)(2,1)S(1)} %get-tuple-element.86), channel_id=1, source_target_pairs={{0,96},{16,112},{32,0},{48,16},{64,32},{80,48},{96,64},{112,80},{1... | collective-permute-start | bytes 98312 | tf_op jit(solution)/shard_map/ppermute | solution.py:624
  93.6 4.3 %collective-permute-start.28 = (bf16[128,128]{1,0:T(8,128)(2,1)S(1)}, bf16[128,128]{1,0:T(8,128)(2,1)S(1)}, u32[]{:S(2)}, u32[]{:S(2)}) collective-permute-start(bf16[128,128]{1,0:T(8,128)(2,1)S(1)} %get-tuple-element.87), channel_id=1, source_target_pairs={{0,64},{16,80},{32,96},{48,112},{64,0},{80,16},{96,32},{112,48},{1... | collective-permute-start | bytes 98312 | tf_op jit(solution)/shard_map/ppermute | solution.py:624
  94.1 4.2 %collective-permute-start.29 = (bf16[128,128]{1,0:T(8,128)(2,1)S(1)}, bf16[128,128]{1,0:T(8,128)(2,1)S(1)}, u32[]{:S(2)}, u32[]{:S(2)}) collective-permute-start(bf16[128,128]{1,0:T(8,128)(2,1)S(1)} %get-tuple-element.88), channel_id=1, source_target_pairs={{0,32},{16,48},{32,64},{48,80},{64,96},{80,112},{96,0},{112,16},{1... | collective-permute-start | bytes 98312 | tf_op jit(solution)/shard_map/ppermute | solution.py:624
  98.4 5.3 %collective-permute-start.30 = (bf16[64,128]{1,0:T(8,128)(2,1)S(1)}, bf16[64,128]{1,0:T(8,128)(2,1)S(1)}, u32[]{:S(2)}, u32[]{:S(2)}) collective-permute-start(bf16[64,128]{1,0:T(8,128)(2,1)S(1)} %get-tuple-element.90), channel_id=1, source_target_pairs={{0,16},{16,0},{32,48},{48,32},{64,80},{80,64},{96,112},{112,96},{1... | collective-permute-start | bytes 49160 | tf_op jit(solution)/shard_map/ppermute | solution.py:630
  (5 other events, 56.0 us)
